TPU v7x, 32 devices: a whole 2x2x4 slice. The times are simulated.
32 devices in a mesh: seq: 8 (over z, x), fsdp: 4 (over y, core).
Axes of the slice: x: 2, y: 2, z: 4, core: 2. Of those that a mesh axis runs over, the one named last changes fastest.
Arguments:
- inputs: bfloat16 [4, 8192, 768], P('fsdp', 'seq'), may hold values from -10 to 10
- cotangent: bfloat16 [4, 8192, 768], P('fsdp', 'seq'), may hold values from -6 to 6
- query_weight: bfloat16 [768, 768], P('fsdp'), may hold values from -0.21875 to 0.21875
- key_weight: bfloat16 [768, 768], P('fsdp'), may hold values from -0.21875 to 0.21875
- value_weight: bfloat16 [768, 768], P('fsdp'), may hold values from -0.21875 to 0.21875
- output_weight: bfloat16 [768, 768], P('fsdp'), may hold values from -0.21875 to 0.21875
- up_weight: bfloat16 [768, 3072], P('fsdp'), may hold values from -0.21875 to 0.21875
- down_weight: bfloat16 [3072, 768], P('fsdp'), may hold values from -0.109375 to 0.109375
- norm_gain: bfloat16 [768], P('fsdp'), may hold values from 0.5 to 1.5
- norm_shift: bfloat16 [768], P('fsdp'), may hold values from -2 to 2
- final_gain: bfloat16 [768], P('fsdp'), may hold values from 0.5 to 1.5
- final_shift: bfloat16 [768], P('fsdp'), may hold values from -2 to 2
- conv_kernel: float32 [65, 12], replicated, may hold values from -1 to 1
Outputs:
- output: bfloat16 [4, 8192, 768], P('fsdp', 'seq')
- grad_inputs: bfloat16 [4, 8192, 768], P('fsdp', 'seq')
- grad_query_weight: float32 [768, 768], P('fsdp')
- grad_key_weight: float32 [768, 768], P('fsdp')
- grad_value_weight: float32 [768, 768], P('fsdp')
- grad_output_weight: float32 [768, 768], P('fsdp')
- grad_up_weight: float32 [768, 3072], P('fsdp')
- grad_down_weight: float32 [3072, 768], P('fsdp')
- grad_norm_gain: float32 [768], P('fsdp')
- grad_norm_shift: float32 [768], P('fsdp')
- grad_final_gain: float32 [768], P('fsdp')
- grad_final_shift: float32 [768], P('fsdp')
- grad_conv_kernel: float32 [65, 12], replicated
All inputs are finite; a program needn't handle non-finite values.
Results may differ from a plain program's by a relative error of at most 0.03.
Values may be sent and summed in bfloat16 or wider, within the bound.
No kernel may reach another device: no remote copies, remote signals or barrier semaphores. Data moves between devices by JAX's collectives and lax.ppermute only.
A program may use at most 256 MiB of HBM per device.

v0:
```python
import jax
import jax.numpy as jnp
from jax import lax
from jax.sharding import PartitionSpec as P

HEADS = 12
HDIM = 64
LANDMARKS = 64
KERNEL = 65
PINV_ITERS = 6


PRECISE = lax.Precision.HIGHEST


def merged(array, axis, combine):
    everything = jax.tree.map(lambda part: lax.all_gather(part, axis), array)
    first = jax.tree.map(lambda part: part[0], everything)

    def step(k, so_far):
        return combine(so_far, jax.tree.map(lambda part: part[k], everything))

    return lax.fori_loop(1, lax.axis_size(axis), step, first)


def padded(array, sides, width):
    for axis, dim in sides:
        size, length = (lax.axis_size(axis), array.shape[dim])
        up = [(i, (i + 1) % size) for i in range(size - 1)]
        down = [(j, i) for i, j in up]
        last = lax.slice_in_dim(array, length - width, length, axis=dim)
        first = lax.slice_in_dim(array, 0, width, axis=dim)
        before = lax.ppermute(last, axis, up)
        after = lax.ppermute(first, axis, down)
        array = jnp.concatenate([before, array, after], axis=dim)
    return array


def matrix_product(formula, former, latter):
    return jnp.einsum(formula, former, latter, precision=PRECISE)


def approximate_inverse(matrix):
    order_size = matrix.shape[-1]
    column_sums = jnp.sum(matrix, axis=1)
    row_sums = jnp.sum(matrix, axis=2)
    factor = 1.0 / (jnp.max(column_sums, axis=1) * jnp.max(row_sums, axis=1))
    approx = jnp.swapaxes(matrix, 1, 2) * factor[:, None, None]
    identity = jnp.eye(order_size, dtype=jnp.float32)
    for repeat in range(PINV_ITERS):
        applied = matrix_product("hij,hjk->hik", matrix, approx)
        nested = 7.0 * identity - applied
        nested = 15.0 * identity - matrix_product("hij,hjk->hik", applied, nested)
        nested = 13.0 * identity - matrix_product("hij,hjk->hik", applied, nested)
        approx = 0.25 * matrix_product("hij,hjk->hik", approx, nested)
    return approx


def landmark_core(landmark_queries, landmark_keys, blended_values):
    score_matrix = matrix_product("ytk,wtk->tyw", landmark_queries, landmark_keys)
    return matrix_product(
        "ptr,prb->ptb", approximate_inverse(jax.nn.softmax(score_matrix, axis=2)), blended_values
    )


def normalize(residual, gain, shift):
    center = residual - jnp.mean(residual, axis=-1, keepdims=True)
    variance = jnp.mean(center * center, axis=-1, keepdims=True)
    return center * lax.rsqrt(variance + 1e-05) * gain + shift


def exact_gelu(values):
    return jax.nn.gelu(values, approximate=False)


def combine_partial(former, latter):
    max_former, sum_former, mix_former = former
    max_latter, sum_latter, mix_latter = latter
    largest = jnp.maximum(max_former, max_latter)
    scale_former = jnp.exp(max_former - largest)
    scale_latter = jnp.exp(max_latter - largest)
    return (
        largest,
        sum_former * scale_former + sum_latter * scale_latter,
        mix_former * scale_former[:, :, None] + mix_latter * scale_latter[:, :, None],
    )


def grouped_conv(signal, taps):
    width = signal.shape[1]
    return lax.conv_general_dilated(
        signal[None],
        taps[:, None, :],
        (1,),
        "VALID",
        dimension_numbers=("NWC", "WIO", "NWC"),
        feature_group_count=width,
        precision=PRECISE,
    )[0]


def shards(
    inputs,
    cotangent,
    query_weight,
    key_weight,
    value_weight,
    output_weight,
    up_weight,
    down_weight,
    norm_gain,
    norm_shift,
    final_gain,
    final_shift,
    conv_kernel,
):
    single_float = jnp.float32
    bf16 = jnp.bfloat16
    (
        query_full,
        key_full,
        value_full,
        output_full,
        up_full,
        down_full,
        gain_full,
        shift_full,
        last_gain,
        last_shift,
    ) = (
        lax.all_gather(query_weight, "fsdp", axis=0, tiled=True),
        lax.all_gather(key_weight, "fsdp", axis=0, tiled=True),
        lax.all_gather(value_weight, "fsdp", axis=0, tiled=True),
        lax.all_gather(output_weight, "fsdp", axis=0, tiled=True),
        lax.all_gather(up_weight, "fsdp", axis=0, tiled=True),
        lax.all_gather(down_weight, "fsdp", axis=0, tiled=True),
        lax.all_gather(norm_gain, "fsdp", axis=0, tiled=True),
        lax.all_gather(norm_shift, "fsdp", axis=0, tiled=True),
        lax.all_gather(final_gain, "fsdp", axis=0, tiled=True),
        lax.all_gather(final_shift, "fsdp", axis=0, tiled=True),
    )
    token_rows = inputs[0]
    token_sequence, embedding_width = token_rows.shape
    marks_local = LANDMARKS // lax.axis_size("seq")
    segment = token_sequence // marks_local
    reach = KERNEL // 2
    factor = HDIM ** (-0.25)
    queries = (
        factor * jnp.dot(token_rows, query_full, preferred_element_type=single_float)
    ).astype(bf16)
    keys = (factor * jnp.dot(token_rows, key_full, preferred_element_type=single_float)).astype(
        bf16
    )
    values = jnp.dot(token_rows, value_full, preferred_element_type=single_float).astype(bf16)
    query_local = jnp.mean(
        queries.reshape(marks_local, segment, embedding_width), axis=1, dtype=single_float
    ).astype(bf16)
    key_local = jnp.mean(
        keys.reshape(marks_local, segment, embedding_width), axis=1, dtype=single_float
    ).astype(bf16)
    query_landmark_rows, key_landmark_rows = (
        lax.all_gather(query_local, "seq", axis=0, tiled=True),
        lax.all_gather(key_local, "seq", axis=0, tiled=True),
    )
    query_landmark_rows = query_landmark_rows.reshape(LANDMARKS, HEADS, HDIM)
    key_landmark_rows = key_landmark_rows.reshape(LANDMARKS, HEADS, HDIM)
    query_per_head = queries.reshape(token_sequence, HEADS, HDIM)
    key_per_head = keys.reshape(token_sequence, HEADS, HDIM)
    value_per_head = values.reshape(token_sequence, HEADS, HDIM)
    score_lead = jnp.einsum(
        "xfk,rfk->fxr", key_landmark_rows, query_per_head, preferred_element_type=single_float
    )
    probability_lead = jax.nn.softmax(score_lead, axis=1)
    front_lowrank = probability_lead.astype(bf16)
    score_rear = jnp.einsum(
        "xfk,rfk->fxr", query_landmark_rows, key_per_head, preferred_element_type=single_float
    )
    local_max = jnp.max(score_rear, axis=2)
    exponent_term = jnp.exp(score_rear - local_max[:, :, None])
    local_sum = jnp.sum(exponent_term, axis=2)
    value_single = value_per_head.astype(single_float)
    nearby_mixture = matrix_product("pal,lpx->pax", exponent_term, value_single)
    largest, totals, mix_sum = merged(
        (local_max, local_sum, nearby_mixture), "seq", combine_partial
    )
    blended_values = mix_sum / totals[:, :, None]
    log_total = largest + jnp.log(totals)
    combined_float, core_pull = jax.vjp(
        landmark_core,
        query_landmark_rows.astype(single_float),
        key_landmark_rows.astype(single_float),
        blended_values,
    )
    combined_output = combined_float.astype(bf16)
    attended_rows = jnp.einsum(
        "qas,qau->squ", front_lowrank, combined_output, preferred_element_type=single_float
    )
    padded_values = padded(values, (("seq", 0),), reach)
    padded_float = padded_values.astype(single_float)
    taps = jnp.repeat(conv_kernel, HDIM, axis=1)
    conv_sum = grouped_conv(padded_float, taps)
    context = (attended_rows.reshape(token_sequence, embedding_width) + conv_sum).astype(bf16)
    branch = jnp.dot(context, output_full, preferred_element_type=single_float)
    hidden, first_pull = jax.vjp(
        normalize,
        token_rows.astype(single_float) + branch,
        gain_full.astype(single_float),
        shift_full.astype(single_float),
    )
    hidden_low = hidden.astype(bf16)
    expanded = jnp.dot(hidden_low, up_full, preferred_element_type=single_float)
    activated, gelu_pull = jax.vjp(exact_gelu, expanded)
    activated_low = activated.astype(bf16)
    reduced = jnp.dot(activated_low, down_full, preferred_element_type=single_float)
    result, second_pull = jax.vjp(
        normalize, hidden + reduced, last_gain.astype(single_float), last_shift.astype(single_float)
    )
    grad_second, grad_last_gain, grad_last_shift = second_pull(cotangent[0].astype(single_float))
    grad_reduced = grad_second.astype(bf16)
    grad_down = jnp.dot(activated_low.T, grad_reduced, preferred_element_type=single_float)
    (grad_expanded,) = gelu_pull(
        jnp.dot(grad_reduced, down_full.T, preferred_element_type=single_float)
    )
    grad_expanded = grad_expanded.astype(bf16)
    grad_up = jnp.dot(hidden_low.T, grad_expanded, preferred_element_type=single_float)
    grad_hidden = grad_second + jnp.dot(
        grad_expanded, up_full.T, preferred_element_type=single_float
    )
    grad_first, grad_gain, grad_shift = first_pull(grad_hidden)
    grad_branch = grad_first.astype(bf16)
    grad_output = jnp.dot(context.T, grad_branch, preferred_element_type=single_float)
    grad_context = jnp.dot(grad_branch, output_full.T, preferred_element_type=single_float).astype(
        bf16
    )
    context_per_head = grad_context.reshape(token_sequence, HEADS, HDIM)
    mixture_portion = jnp.einsum(
        "pal,lpx->pax", front_lowrank, context_per_head, preferred_element_type=single_float
    )
    grad_combined = lax.psum(mixture_portion.astype(jnp.bfloat16), "seq").astype(jnp.float32)
    grad_probs_front = jnp.einsum(
        "yvz,vuz->vuy", context_per_head, combined_output, preferred_element_type=single_float
    )
    gradient_scores_lead = (
        probability_lead
        * (grad_probs_front - jnp.sum(probability_lead * grad_probs_front, axis=1, keepdims=True))
    ).astype(bf16)
    grad_queries = jnp.einsum(
        "xeg,exb->gxb", gradient_scores_lead, key_landmark_rows, preferred_element_type=single_float
    )
    key_marks_part = jnp.einsum(
        "elr,rej->lej", gradient_scores_lead, query_per_head, preferred_element_type=single_float
    )
    grad_query_core, grad_key_core, gradient_mixed = core_pull(grad_combined)
    probability_rear = jnp.exp(score_rear - log_total[:, :, None])
    gradient_probs_rear = matrix_product("ofa,uoa->ofu", gradient_mixed, value_single)
    row_dot = jnp.sum(gradient_mixed * blended_values, axis=2)
    gradient_scores_rear = (probability_rear * (gradient_probs_rear - row_dot[:, :, None])).astype(
        bf16
    )
    query_marks_part = jnp.einsum(
        "elr,rej->lej", gradient_scores_rear, key_per_head, preferred_element_type=single_float
    )
    grad_keys = jnp.einsum(
        "xeg,exb->gxb",
        gradient_scores_rear,
        query_landmark_rows,
        preferred_element_type=single_float,
    )
    gradient_value_rows = matrix_product("qas,qau->squ", probability_rear, gradient_mixed).reshape(
        token_sequence, embedding_width
    )
    query_own, key_own = (
        lax.psum_scatter(
            query_marks_part.astype(jnp.bfloat16), "seq", scatter_dimension=0, tiled=True
        ).astype(jnp.float32),
        lax.psum_scatter(
            key_marks_part.astype(jnp.bfloat16), "seq", scatter_dimension=0, tiled=True
        ).astype(jnp.float32),
    )
    first_mark = lax.axis_index("seq") * marks_local
    query_own = query_own + lax.dynamic_slice_in_dim(grad_query_core, first_mark, marks_local, 0)
    key_own = key_own + lax.dynamic_slice_in_dim(grad_key_core, first_mark, marks_local, 0)
    grad_queries = (
        grad_queries.reshape(marks_local, segment, HEADS, HDIM) + query_own[:, None] / segment
    )
    grad_keys = grad_keys.reshape(marks_local, segment, HEADS, HDIM) + key_own[:, None] / segment
    padded_grads = padded(grad_context, (("seq", 0),), reach)
    gradient_value_rows = gradient_value_rows + grouped_conv(
        padded_grads.astype(single_float), taps[::-1]
    )
    context_float = grad_context.astype(single_float)
    kernel_full = lax.conv_general_dilated(
        padded_float[None],
        context_float[:, None, :],
        (1,),
        "VALID",
        dimension_numbers=("NWC", "WIO", "NWC"),
        feature_group_count=embedding_width,
        precision=PRECISE,
    )[0]
    kernel_part = jnp.sum(kernel_full.reshape(KERNEL, HEADS, HDIM), axis=2)
    grad_kernel = lax.psum(kernel_part, ("seq", "fsdp"))
    query_low = grad_queries.reshape(token_sequence, embedding_width).astype(bf16)
    key_low = grad_keys.reshape(token_sequence, embedding_width).astype(bf16)
    value_low = gradient_value_rows.astype(bf16)
    grad_tokens = (
        grad_first
        + factor * jnp.dot(query_low, query_full.T, preferred_element_type=single_float)
        + factor * jnp.dot(key_low, key_full.T, preferred_element_type=single_float)
        + jnp.dot(value_low, value_full.T, preferred_element_type=single_float)
    )
    grad_query = factor * jnp.dot(token_rows.T, query_low, preferred_element_type=single_float)
    grad_key = factor * jnp.dot(token_rows.T, key_low, preferred_element_type=single_float)
    grad_value = jnp.dot(token_rows.T, value_low, preferred_element_type=single_float)
    (
        sum_query,
        sum_key,
        sum_value,
        sum_output,
        sum_up,
        sum_down,
        sum_gain,
        sum_shift,
        sum_last_gain,
        sum_last_shift,
    ) = (
        lax.psum(grad_query.astype(jnp.bfloat16), "seq").astype(jnp.float32),
        lax.psum(grad_key.astype(jnp.bfloat16), "seq").astype(jnp.float32),
        lax.psum(grad_value.astype(jnp.bfloat16), "seq").astype(jnp.float32),
        lax.psum(grad_output.astype(jnp.bfloat16), "seq").astype(jnp.float32),
        lax.psum(grad_up.astype(jnp.bfloat16), "seq").astype(jnp.float32),
        lax.psum(grad_down.astype(jnp.bfloat16), "seq").astype(jnp.float32),
        lax.psum(grad_gain.astype(jnp.bfloat16), "seq").astype(jnp.float32),
        lax.psum(grad_shift.astype(jnp.bfloat16), "seq").astype(jnp.float32),
        lax.psum(grad_last_gain.astype(jnp.bfloat16), "seq").astype(jnp.float32),
        lax.psum(grad_last_shift.astype(jnp.bfloat16), "seq").astype(jnp.float32),
    )
    (
        share_query,
        share_key,
        share_value,
        share_output,
        share_up,
        share_down,
        share_gain,
        share_shift,
        share_last_gain,
        share_last_shift,
    ) = (
        lax.psum_scatter(
            sum_query.astype(jnp.bfloat16), "fsdp", scatter_dimension=0, tiled=True
        ).astype(jnp.float32),
        lax.psum_scatter(
            sum_key.astype(jnp.bfloat16), "fsdp", scatter_dimension=0, tiled=True
        ).astype(jnp.float32),
        lax.psum_scatter(
            sum_value.astype(jnp.bfloat16), "fsdp", scatter_dimension=0, tiled=True
        ).astype(jnp.float32),
        lax.psum_scatter(
            sum_output.astype(jnp.bfloat16), "fsdp", scatter_dimension=0, tiled=True
        ).astype(jnp.float32),
        lax.psum_scatter(
            sum_up.astype(jnp.bfloat16), "fsdp", scatter_dimension=0, tiled=True
        ).astype(jnp.float32),
        lax.psum_scatter(
            sum_down.astype(jnp.bfloat16), "fsdp", scatter_dimension=0, tiled=True
        ).astype(jnp.float32),
        lax.psum_scatter(
            sum_gain.astype(jnp.bfloat16), "fsdp", scatter_dimension=0, tiled=True
        ).astype(jnp.float32),
        lax.psum_scatter(
            sum_shift.astype(jnp.bfloat16), "fsdp", scatter_dimension=0, tiled=True
        ).astype(jnp.float32),
        lax.psum_scatter(
            sum_last_gain.astype(jnp.bfloat16), "fsdp", scatter_dimension=0, tiled=True
        ).astype(jnp.float32),
        lax.psum_scatter(
            sum_last_shift.astype(jnp.bfloat16), "fsdp", scatter_dimension=0, tiled=True
        ).astype(jnp.float32),
    )
    return (
        result.astype(bf16)[None],
        grad_tokens.astype(bf16)[None],
        share_query,
        share_key,
        share_value,
        share_output,
        share_up,
        share_down,
        share_gain,
        share_shift,
        share_last_gain,
        share_last_shift,
        grad_kernel,
    )


def solution(mesh):
    in_specs = (
        P("fsdp", "seq", None),
        P("fsdp", "seq", None),
        P("fsdp", None),
        P("fsdp", None),
        P("fsdp", None),
        P("fsdp", None),
        P("fsdp", None),
        P("fsdp", None),
        P("fsdp"),
        P("fsdp"),
        P("fsdp"),
        P("fsdp"),
        P(),
    )
    out_specs = (
        P("fsdp", "seq", None),
        P("fsdp", "seq", None),
        P("fsdp", None),
        P("fsdp", None),
        P("fsdp", None),
        P("fsdp", None),
        P("fsdp", None),
        P("fsdp", None),
        P("fsdp"),
        P("fsdp"),
        P("fsdp"),
        P("fsdp"),
        P(),
    )
    return jax.shard_map(shards, mesh=mesh, in_specs=in_specs, out_specs=out_specs, check_vma=False)
```

profile of v0, /device:TPU:0, one launch (start us, length us, event | category | flops | bytes accessed | tf_op | source)
XLA Modules:
  0.0 1017.8 jit_solution(5025849167384846941)
XLA Ops:
  9.4 20.3 %all-gather.17.cloned.1.call-done = bf16[768,768]{1,0:T(8,128)(2,1)} async-done(((bf16[192,768]{1,0:T(8,128)(2,1)}), bf16[768,768]{1,0:T(8,128)(2,1)}) %all-gather.17.cloned.1.call-update) | async-done | bytes 1179664 | tf_op jit(solution)/shard_map/all_gather | solution.py:133
  34.6 14.3 %all-gather.15.cloned.1.call-done = bf16[768,768]{1,0:T(8,128)(2,1)} async-done(((bf16[192,768]{1,0:T(8,128)(2,1)}), bf16[768,768]{1,0:T(8,128)(2,1)}) %all-gather.15.cloned.1.call-update) | async-done | bytes 1179664 | tf_op jit(solution)/shard_map/all_gather | solution.py:132
  53.6 14.3 %all-gather.13.cloned.1.call-done = bf16[768,768]{1,0:T(8,128)(2,1)} async-done(((bf16[192,768]{1,0:T(8,128)(2,1)}), bf16[768,768]{1,0:T(8,128)(2,1)}) %all-gather.13.cloned.1.call-update) | async-done | bytes 1179664 | tf_op jit(solution)/shard_map/all_gather | solution.py:131
  72.2 30.6 %all_gather.55 = bf16[64,768]{1,0:T(8,128)(2,1)S(1)} all-gather(bf16[8,768]{1,0:T(8,128)(2,1)S(1)} %multiply_convert_fusion.8), channel_id=1, replica_groups=mesh['seq'=8,'fsdp'=4] {'seq'}, dimensions={0}, use_global_device_ids=true | all-gather | bytes 110592 | tf_op jit(solution)/shard_map/all_gather | solution.py:162
  105.1 5.2 fusion.28
  120.5 6.2 all-reduce.11
  133.5 31.5 %all_gather.57 = bf16[64,768]{1,0:T(8,128)(2,1)S(1)} all-gather(bf16[8,768]{1,0:T(8,128)(2,1)S(1)} %multiply_convert_fusion.7), channel_id=1, replica_groups=mesh['seq'=8,'fsdp'=4] {'seq'}, dimensions={0}, use_global_device_ids=true | all-gather | bytes 110592 | tf_op jit(solution)/shard_map/all_gather | solution.py:163
  194.7 11.3 %convolution_multiply_fusion.2 = f32[12,64,64]{2,1,0:T(8,128)S(1)} fusion(f32[12,64,64]{2,1,0:T(8,128)S(1)} %convolution_multiply_fusion.3, f32[12,64,64]{2,1,0:T(8,128)S(1)} %convolution_subtract_fusion.2), kind=kOutput, calls=%fused_computation.179 | convolution fusion | flops 37797888 | bytes 589824 | tf_op jit(solution)/shard_map/jvp(hij,hjk->hik)/dot_general | solution.py:40
  210.1 31.3 %all-gather.4 = f32[8,12,64]{2,1,0:T(8,128)S(1)} all-gather(f32[1,12,64]{2,1,0:T(8,128)S(1)} %bitcast.383), channel_id=3, replica_groups=mesh['seq'=8,'fsdp'=4] {'seq'}, dimensions={0}, use_global_device_ids=true | all-gather | bytes 27648 | tf_op jit(solution)/shard_map/all_gather | solution.py:17
  241.4 30.5 %all-gather.3 = f32[8,12,64]{2,1,0:T(8,128)S(1)} all-gather(f32[1,12,64]{2,1,0:T(8,128)S(1)} %bitcast.382), channel_id=2, replica_groups=mesh['seq'=8,'fsdp'=4] {'seq'}, dimensions={0}, use_global_device_ids=true | all-gather | bytes 27648 | tf_op jit(solution)/shard_map/all_gather | solution.py:17
  278.5 16.7 %broadcast_select_fusion.1 = f32[8,136,768]{2,0,1:T(8,128)S(1)} fusion(pred[8,136]{0,1:T(8,128)(4,1)S(1)} %copy-done.157, f32[65,1,768]{2,1,0:T(1,128)S(1)} %copy-done.113, bf16[1,7,64,768]{3,1,2,0:T(8,128)(2,1)S(1)} %slice.42, bf16[1,8,136,768]{3,1,2,0:T(8,128)(2,1)S(1)} %copy.162), kind=kOutput, calls=%fused_computation.103 | convolution fusion | flops 659963904 | bytes 5902400 | tf_op jit(solution)/shard_map/conv_general_dilated | solution.py:91
  299.0 15.6 %while.19 = (s32[]{:T(128)}, f32[12,64]{1,0:T(8,128)S(1)}, f32[12,64]{1,0:T(8,128)S(1)}, f32[12,64,64]{2,1,0:T(8,128)S(1)}, f32[8,12,64]{2,1,0:T(8,128)}, /*inde...) while((s32[]{:T(128)}, f32[12,64]{1,0:T(8,128)S(1)}, ...), condition=%wide.region_11.0_spmd, body=%wide.region_10.0_spmd.sunk | while | flops 152069 | bytes 620687 | solution.py:23
  332.8 35.7 %multiply_convert_fusion = (bf16[1024,3072]{1,0:T(8,128)(2,1)}, f32[1024,3072]{1,0:T(8,128)}, f32[1024,3072]{1,0:T(8,128)}) fusion(bf16[768,3072]{1,0:T(8,128)(2,1)} %all-gather.21.cloned.1.call-done, f32[1024,768]{1,0:T(8,128)S(1)} %get-tuple-element.307, f32[768]{0:T(1024)S(1)} %copy-done.138, f32[768]{0:T(1024)S(1)} %copy-done.127, ...), kind=kOutput, calls=%fused_computation.13 | convolution fusion | flops 5040242688 | bytes 39335936 | tf_op jit(solution)/shard_map/dot_general | solution.py:211
  368.5 8.8 fusion.193
  384.4 18.0 %add_convert_fusion = bf16[1024,3072]{1,0:T(8,128)(2,1)} fusion(f32[1024,3072]{1,0:T(8,128)} %get-tuple-element.287, f32[1024,3072]{1,0:T(8,128)} %get-tuple-element.308, bf16[3072,768]{1,0:T(8,128)(2,1)} %all-gather.23.cloned.1.call-done, f32[1024,768]{1,0:T(8,128)} %get-tuple-element.285, f32[1024]{0:T(1024)S(1)} %negate_multiply_fusion.2), kind=kOutput, calls=%fused_computation.12 | convolution fusion | flops 4877451264 | bytes 39325696 | tf_op jit(solution)/shard_map/dot_general | solution.py:222
  402.3 10.5 %multiply_reduce_fusion = (bf16[768]{0:T(1024)(128)(2,1)}, f32[1024]{0:T(1024)S(1)}, bf16[768]{0:T(1024)(128)(2,1)}, f32[1024,768]{1,0:T(8,128)S(1)}) fusion(f32[1024,768]{1,0:T(8,128)S(1)} %get-tuple-element.307, f32[1024]{0:T(1024)S(1)} %fusion.158, f32[1024]{0:T(1024)S(1)} %broadcast_multiply_fusion.1, f32[768]{0:T(1024)S(1)} %copy-done.127, ...), kind=kOutput, calls=%fused_computation.60 | convolution fusion | flops 4839699456 | bytes 20469760 | tf_op jit(solution)/shard_map/dot_general | solution.py:226
  438.8 17.0 %broadcast_select_fusion = f32[8,136,768]{2,0,1:T(8,128)S(1)} fusion(pred[8,136]{0,1:T(8,128)(4,1)S(1)} %copy-done.158, bf16[1,7,64,768]{3,1,2,0:T(8,128)(2,1)S(1)} %slice.46, bf16[1,8,136,768]{3,1,2,0:T(8,128)(2,1)S(1)} %copy.203, f32[65,1,768]{2,0,1:T(8,128)S(1)} %bitcast.381), kind=kOutput, calls=%fused_computation.102 | convolution fusion | flops 659963904 | bytes 5902400 | tf_op jit(solution)/shard_map/conv_general_dilated | solution.py:91
  461.5 41.6 %all-reduce.15.cloned.1.call-done = bf16[12,64,64]{2,1,0:T(8,128)(2,1)} async-done(((bf16[12,64,64]{2,1,0:T(8,128)(2,1)}), bf16[12,64,64]{2,1,0:T(8,128)(2,1)}) %all-reduce.15.cloned.1.call-update) | async-done | bytes 98320 | tf_op jit(solution)/shard_map/psum | solution.py:239
  548.3 6.2 fusion.24
  581.6 49.3 %reduce-scatter.15.cloned.1.call-done = bf16[8,12,64]{2,1,0:T(8,128)(2,1)} async-done(((bf16[64,12,64]{2,1,0:T(8,128)(2,1)}), bf16[8,12,64]{2,1,0:T(8,128)(2,1)}) %reduce-scatter.15.cloned.1.call-update) | async-done | bytes 12304 | tf_op jit(solution)/shard_map/reduce_scatter | solution.py:273
  650.5 9.9 convolution_convert_fusion.1
  662.2 10.3 %convolution_convert_fusion = bf16[3072,768]{1,0:T(8,128)(2,1)} fusion(bf16[1024,3072]{1,0:T(8,128)(2,1)} %get-tuple-element.286, f32[1024,768]{1,0:T(8,128)S(1)} %copy-done.85, f32[1024]{0:T(1024)S(1)} %copy-done.141), kind=kOutput, calls=%fused_computation.27 | convolution fusion | flops 4835770368 | bytes 14159872 | tf_op jit(solution)/shard_map/dot_general | solution.py:220
  677.0 10.1 reduce-scatter.27.cloned.1.call-done
  689.0 27.2 %reduce-scatter.25.cloned.1.call-done = bf16[192,768]{1,0:T(8,128)(2,1)} async-done(((bf16[768,768]{1,0:T(8,128)(2,1)}), bf16[192,768]{1,0:T(8,128)(2,1)}) %reduce-scatter.25.cloned.1.call-update) | async-done | bytes 294928
  718.1 26.3 %reduce-scatter.19.cloned.1.call-done = bf16[192,768]{1,0:T(8,128)(2,1)} async-done(((bf16[768,768]{1,0:T(8,128)(2,1)}), bf16[192,768]{1,0:T(8,128)(2,1)}) %reduce-scatter.19.cloned.1.call-update) | async-done | bytes 294928 | tf_op jit(solution)/shard_map/reduce_scatter | solution.py:359
  744.3 50.4 %reduce-scatter.21.cloned.1.call-done = bf16[192,3072]{1,0:T(8,128)(2,1)} async-done(((bf16[768,3072]{1,0:T(8,128)(2,1)}), bf16[192,3072]{1,0:T(8,128)(2,1)}) %reduce-scatter.21.cloned.1.call-update) | async-done | bytes 1179664 | tf_op jit(solution)/shard_map/reduce_scatter | solution.py:362
  794.7 50.3 %reduce-scatter.23.cloned.1.call-done = bf16[768,768]{1,0:T(8,128)(2,1)} async-done(((bf16[3072,768]{1,0:T(8,128)(2,1)}), bf16[768,768]{1,0:T(8,128)(2,1)}) %reduce-scatter.23.cloned.1.call-update) | async-done | bytes 1179664 | tf_op jit(solution)/shard_map/reduce_scatter | solution.py:365
  845.1 24.4 %fusion.96 = f32[65,768]{1,0:T(8,128)S(1)} fusion(bf16[1024,1,768]{2,0,1:T(8,128)(2,1)} %bitcast.371, bf16[1,1088,768]{2,1,0:T(8,128)(2,1)} %get-tuple-element.288), kind=kOutput, calls=%fused_computation.200 | convolution fusion | flops 102236160 | bytes 3443712 | tf_op jit(solution)/shard_map/conv_general_dilated | solution.py:292
  869.6 10.9 %all-reduce.10 = (bf16[768]{0:T(1024)(128)(2,1)S(1)}, bf16[768]{0:T(1024)(128)(2,1)S(1)}, bf16[768]{0:T(1024)(128)(2,1)S(1)}, bf16[768]{0:T(1024)(128)(2,1)S(1)}, bf16[768]{0:T(1024)(128)(2,1)S(1)}) all-reduce(bf16[768]{0:T(1024)(128)(2,1)S(1)} %dynamic-update-slice.3, ...), channel_id=1, replica_groups=mesh['seq'=8,'fsdp'=4] {'fsdp'}, use_global_device_ids=true, to_apply=%add.3 | all-reduce | flops 3840 | bytes 15360
  880.8 22.3 %all-reduce.8 = (bf16[192]{0:T(256)(128)(2,1)S(1)}, bf16[192]{0:T(256)(128)(2,1)S(1)}, bf16[192]{0:T(256)(128)(2,1)S(1)}, bf16[192]{0:T(256)(128)(2,1)S(1)}) all-reduce(bf16[192]{0:T(256)(128)(2,1)S(1)} %dynamic-slice.13, bf16[192]{0:T(256)(128)(2,1)S(1)} %dynamic-slice.15, ...), channel_id=1, replica_groups=mesh['seq'=8,'fsdp'=4] {'seq'}, use_global_device_ids=true, to_apply=%region_44.0 | all-reduce | flops 768 | bytes 3072 | tf_op jit(solution)/shard_map/psum | solution.py:333
  907.8 37.8 %psum.95 = f32[65,12]{1,0:T(8,128)S(1)} all-reduce(f32[65,12]{1,0:T(8,128)S(1)} %reduce_sum.302), channel_id=1, replica_groups=mesh['seq'=8,'fsdp'=4] {'seq','fsdp'}, use_global_device_ids=true, to_apply=%region_56.0 | all-reduce | flops 780 | bytes 6240 | tf_op jit(solution)/shard_map/psum | solution.py:302
  966.6 34.0 %all-reduce.17.cloned.1.call-done = (bf16[192,768]{0,1:T(8,128)(2,1)}, bf16[192,768]{0,1:T(8,128)(2,1)}, bf16[192,768]{0,1:T(8,128)(2,1)}, bf16[192,768]{1,0:T(8...) async-done(((bf16[192,768]{0,1:T(8,128)(2,1)}, bf16[192,768]{0,1:T(8,128)(2,1)}, bf16[192,768]{0,1:T(8,128)(2,1)}, bf16[192,768]{1,0:T(8,128)(2,1)}, ...) | async-done | bytes 3538960 | tf_op jit(solution)/shard_map/psum | solution.py:327
  (605 shorter events, 285.7 us)
Async XLA Ops:
  7.2 22.6 %all-gather.17.cloned.1.call-start = ((), (), s32[]{:S(2)}) async-start(), calls=%async_computation.10 | async-start | bytes 1474560 | tf_op jit(solution)/shard_map/all_gather | solution.py:133
  7.9 40.9 %all-gather.15.cloned.1.call-start = ((), (), s32[]{:S(2)}) async-start(), calls=%async_computation.9 | async-start | bytes 1474560 | tf_op jit(solution)/shard_map/all_gather | solution.py:132
  8.7 59.2 %all-gather.13.cloned.1.call-start = ((), (), s32[]{:S(2)}) async-start(), calls=%async_computation.8 | async-start | bytes 1474560 | tf_op jit(solution)/shard_map/all_gather | solution.py:131
  9.4 288.6 %all-gather.25.cloned.1.call-start = ((), (), s32[]{:S(2)}) async-start(), calls=%async_computation.17 | async-start | bytes 3538944 | tf_op jit(solution)/shard_map/all_gather | solution.py:17
  105.1 69.4 %copy-start = (f32[12,64,1024]{2,1,0:T(8,128)}, f32[12,64,1024]{2,1,0:T(8,128)S(1)}, u32[]{:S(2)}) copy-start(f32[12,64,1024]{2,1,0:T(8,128)S(1)} %get-tuple-element.303) | copy-start | bytes 9437188
  110.4 218.0 %all-gather.19.cloned.1.call-start = ((), (), s32[]{:S(2)}) async-start(), calls=%async_computation.11 | async-start | bytes 1474560 | tf_op jit(solution)/shard_map/all_gather | solution.py:134
  111.0 221.7 %all-gather.21.cloned.1.call-start = ((), (), s32[]{:S(2)}) async-start(), calls=%async_computation.12 | async-start | bytes 5898240 | tf_op jit(solution)/shard_map/all_gather | solution.py:135
  111.5 257.0 %all-gather.23.cloned.1.call-start = ((), (), s32[]{:S(2)}) async-start(), calls=%async_computation.13 | async-start | bytes 5898240 | tf_op jit(solution)/shard_map/all_gather | solution.py:136
  112.3 390.8 %all-reduce.15.cloned.1.call-start = ((), (), s32[]{:S(2)}) async-start(), calls=%async_computation.14 | async-start | bytes 393216 | tf_op jit(solution)/shard_map/psum | solution.py:239
  175.7 99.6 %collective-permute-start = (bf16[32,768]{1,0:T(8,128)(2,1)}, bf16[32,768]{1,0:T(8,128)(2,1)}, u32[]{:S(2)}, u32[]{:S(2)}) collective-permute-start(bf16[32,768]{1,0:T(8,128)(2,1)} %get-tuple-element.292), channel_id=1, source_target_pairs={{0,4},{4,8},{8,12},{12,16},{16,20},{20,24},{24,28},{1,5},{5,9},{9,... | collective-permute-start | bytes 147464 | tf_op jit(solution)/shard_map/ppermute | solution.py:33
  179.4 96.0 %collective-permute-start.1 = (bf16[32,768]{1,0:T(8,128)(2,1)}, bf16[32,768]{1,0:T(8,128)(2,1)}, u32[]{:S(2)}, u32[]{:S(2)}) collective-permute-start(bf16[32,768]{1,0:T(8,128)(2,1)} %get-tuple-element.293), channel_id=1, source_target_pairs={{4,0},{8,4},{12,8},{16,12},{20,16},{24,20},{28,24},{5,1},{9,5},{13... | collective-permute-start | bytes 147464 | tf_op jit(solution)/shard_map/ppermute | solution.py:34
  207.4 64.5 %copy-start.88 = (bf16[64,12,64]{2,1,0:T(8,128)(2,1)S(1)}, bf16[64,12,64]{2,1,0:T(8,128)(2,1)}, u32[]{:S(2)}) copy-start(bf16[64,12,64]{2,1,0:T(8,128)(2,1)} %reshape.200) | copy-start | bytes 294916
  210.1 67.5 %copy-start.12 = (bf16[1024,768]{0,1:T(8,128)(2,1)}, bf16[1024,768]{0,1:T(8,128)(2,1)S(1)}, u32[]{:S(2)}) copy-start(bf16[1024,768]{0,1:T(8,128)(2,1)S(1)} %copy.158) | copy-start | bytes 4718596
  210.1 65.2 %copy-start.42 = (bf16[1024,768]{1,0:T(8,128)(2,1)S(1)}, bf16[1024,768]{1,0:T(8,128)(2,1)}, u32[]{:S(2)}) copy-start(bf16[1024,768]{1,0:T(8,128)(2,1)} %copy-done.41) | copy-start | bytes 4718596
  332.1 80.8 %copy-start.33 = (f32[1024,768]{1,0:T(8,128)}, f32[1024,768]{1,0:T(8,128)S(1)}, u32[]{:S(2)}) copy-start(f32[1024,768]{1,0:T(8,128)S(1)} %get-tuple-element.307) | copy-start | bytes 9437188
  332.1 80.8 %copy-start.122 = (f32[1024]{0:T(1024)}, f32[1024]{0:T(1024)S(1)}, u32[]{:S(2)}) copy-start(f32[1024]{0:T(1024)S(1)} %broadcast_multiply_fusion.1) | copy-start | bytes 12292
  332.6 80.3 %copy-start.129 = (f32[1024]{0:T(1024)}, f32[1024]{0:T(1024)S(1)}, u32[]{:S(2)}) copy-start(f32[1024]{0:T(1024)S(1)} %fusion.158) | copy-start | bytes 12292
  426.6 11.2 %collective-permute-start.2 = (bf16[32,768]{1,0:T(8,128)(2,1)S(1)}, bf16[32,768]{1,0:T(8,128)(2,1)S(1)}, u32[]{:S(2)}, u32[]{:S(2)}) collective-permute-start(bf16[32,768]{1,0:T(8,128)(2,1)S(1)} %get-tuple-element.290), channel_id=1, source_target_pairs={{0,4},{4,8},{8,12},{12,16},{16,20},{20,24},{24,28},{1,5},{5,9},{9,... | collective-permute-start | bytes 147464 | tf_op jit(solution)/shard_map/ppermute | solution.py:33
  430.5 7.2 collective-permute-start.3
  431.8 135.3 %reduce-scatter.17.cloned.1.call-start = ((), (), s32[]{:S(2)}) async-start(), calls=%async_computation.16 | async-start | bytes 294912 | tf_op jit(solution)/shard_map/reduce_scatter | solution.py:276
  437.4 193.5 %reduce-scatter.15.cloned.1.call-start = ((), (), s32[]{:S(2)}) async-start(), calls=%async_computation.15 | async-start | bytes 294912 | tf_op jit(solution)/shard_map/reduce_scatter | solution.py:273
  561.0 114.1 %reduce-scatter.29.cloned.1.call-start = ((), (), s32[]{:S(2)}) async-start(), calls=%async_computation.23 | async-start | bytes 1474560
  561.8 125.4 %reduce-scatter.27.cloned.1.call-start = ((), (), s32[]{:S(2)}) async-start(), calls=%async_computation.22 | async-start | bytes 1474560
  581.0 135.2 %reduce-scatter.25.cloned.1.call-start = ((), (), s32[]{:S(2)}) async-start(), calls=%async_computation.21 | async-start | bytes 1474560
  645.1 99.2 %reduce-scatter.19.cloned.1.call-start = ((), (), s32[]{:S(2)}) async-start(), calls=%async_computation.18 | async-start | bytes 1474560 | tf_op jit(solution)/shard_map/reduce_scatter | solution.py:359
  650.4 144.4 %reduce-scatter.21.cloned.1.call-start = ((), (), s32[]{:S(2)}) async-start(), calls=%async_computation.19 | async-start | bytes 5898240 | tf_op jit(solution)/shard_map/reduce_scatter | solution.py:362
  660.4 184.6 %reduce-scatter.23.cloned.1.call-start = ((), (), s32[]{:S(2)}) async-start(), calls=%async_computation.20 | async-start | bytes 5898240 | tf_op jit(solution)/shard_map/reduce_scatter | solution.py:365
  672.6 328.0 %all-reduce.17.cloned.1.call-start = ((), (), s32[]{:S(2)}) async-start(), calls=%async_computation.24 | async-start | bytes 7667712 | tf_op jit(solution)/shard_map/psum | solution.py:327
  845.1 101.2 %copy-start.3 = (f32[1024,768]{1,0:T(8,128)S(1)}, f32[1024,768]{1,0:T(8,128)}, u32[]{:S(2)}) copy-start(f32[1024,768]{1,0:T(8,128)} %copy-done.2) | copy-start | bytes 9437188
  845.1 101.2 %copy-start.115 = (f32[1024]{0:T(1024)S(1)}, f32[1024]{0:T(1024)}, u32[]{:S(2)}) copy-start(f32[1024]{0:T(1024)} %copy-done.114) | copy-start | bytes 12292
  845.1 101.2 %copy-start.119 = (f32[768]{0:T(1024)S(1)}, f32[768]{0:T(1024)}, u32[]{:S(2)}) copy-start(f32[768]{0:T(1024)} %convert_element_type.250) | copy-start | bytes 9220
  845.1 101.2 %copy-start.121 = (f32[1024]{0:T(1024)S(1)}, f32[1024]{0:T(1024)}, u32[]{:S(2)}) copy-start(f32[1024]{0:T(1024)} %copy-done.120) | copy-start | bytes 12292
  (155 other events, 1137.8 us)
Sparse Core Ops, SparseCore 0:
  9.6 20.1 all-gather.16
  31.3 17.4 all-gather.14
  50.4 17.4 all-gather.12
  110.5 61.5 all-gather.24
  173.5 16.2 all-gather.18
  191.2 37.4 all-gather.20
  230.2 37.4 all-gather.22
  431.9 71.1 all-reduce.14
  506.8 60.2 reduce-scatter.16
  570.6 60.2 reduce-scatter.14
  633.6 24.7 reduce-scatter.28
  661.4 25.6 reduce-scatter.26
  690.4 25.6 reduce-scatter.24
  718.6 25.6 reduce-scatter.18
  746.9 47.8 reduce-scatter.20
  797.1 47.8 reduce-scatter.22
  850.5 150.0 all-reduce.16
where the time goes:
time: 1030 us; the launch traced here: 1020 us
  waiting for transfers between devices  345 us (33%)
  matrix products  299 us (29%)
  blocking collectives  201 us (20%)
  local copies, waits for them, and re-layouts  86.4 us (8%)
  other arithmetic  55.9 us (5%)
  between operations  18.4 us (2%)
  starting transfers between devices  11.3 us (1%)
    dot_general x81, matrix products, matrix_product(): return jnp.einsum(formula, former, latter, precision=PRECISE)  86.1 us
    all_gather x2, blocking collectives, merged(): everything = jax.tree.map(lambda part: lax.all_gather(part, axis), array)  61.8 us
    reduce_scatter x1, waiting for transfers between devices, shards(): lax.psum_scatter(sum_up.astype(jnp.bfloat16), 'fsdp', scatter_dimension=0...  50.4 us
    reduce_scatter x1, waiting for transfers between devices, shards(): lax.psum_scatter(sum_down.astype(jnp.bfloat16), 'fsdp', scatter_dimension...  50.3 us
    reduce_scatter x1, waiting for transfers between devices, shards(): lax.psum_scatter(query_marks_part.astype(jnp.bfloat16), 'seq', scatter_di...  49.3 us
    unnamed x20, waiting for transfers between devices  41.9 us
    psum x1, waiting for transfers between devices, shards(): lax.psum(mixture_portion.astype(jnp.bfloat16), 'seq').astype(jnp.float32)  41.6 us
    psum x1, blocking collectives, shards(): grad_kernel = lax.psum(kernel_part, ('seq', 'fsdp'))  37.8 us
  transfers between devices with their start and end apart: 21, of which 12 were waited for; matrix products, arithmetic and copies ran while one was open for 34% of the time, Pallas kernels for 0%

commit v1 on v0

v1 whole, which is shorter than its diff:
```python
import functools

import jax
import jax.numpy as jnp
from jax import lax
from jax.experimental import pallas as pl
from jax.experimental.pallas import tpu as pltpu
from jax.sharding import PartitionSpec as P

HEADS = 12
HDIM = 64
LANDMARKS = 64
KERNEL = 65
PINV_ITERS = 6
REACH = KERNEL // 2
EDGE = 128
SCALE = HDIM ** (-0.25)
F32 = jnp.float32
BF16 = jnp.bfloat16
VM = 56 * 1024 * 1024


def nn(a, b):
    return jnp.dot(a, b, preferred_element_type=F32)


def nt(a, b):
    return lax.dot_general(a, b, (((1,), (1,)), ((), ())), preferred_element_type=F32)


def tn(a, b):
    return lax.dot_general(a, b, (((0,), (0,)), ((), ())), preferred_element_type=F32)


def split(a):
    high = a.astype(BF16)
    return high, (a - high.astype(F32)).astype(BF16)


def nn3(a, b):
    ah, al = split(a)
    bh, bl = split(b)
    return nn(jnp.concatenate([ah, ah, al], 1), jnp.concatenate([bh, bl, bh], 0))


def nt3(a, b):
    ah, al = split(a)
    bh, bl = split(b)
    return nt(jnp.concatenate([ah, ah, al], 1), jnp.concatenate([bh, bl, bh], 1))


def tn3(a, b):
    ah, al = split(a)
    bh, bl = split(b)
    return tn(jnp.concatenate([ah, ah, al], 0), jnp.concatenate([bh, bl, bh], 0))


def lanes(shape):
    return lax.broadcasted_iota(jnp.int32, shape, len(shape) - 1)


def hs(h):
    return slice(h * HDIM, (h + 1) * HDIM)


def vspec():
    return pl.BlockSpec(memory_space=pltpu.VMEM)


def sspec():
    return pl.BlockSpec(memory_space=pltpu.SMEM)


def aspec():
    return pl.BlockSpec(memory_space=pl.ANY)


def shape(dims, kind):
    return jax.ShapeDtypeStruct(tuple(dims), kind)


def params():
    return pltpu.CompilerParams(vmem_limit_bytes=VM)


def cost(flops, traffic, trans=0):
    return pl.CostEstimate(flops=int(flops), bytes_accessed=int(traffic), transcendentals=int(trans))


def placed(pieces, whole, sems, me, start):
    rows = pieces[0].shape[0]
    for k, piece in enumerate(pieces):
        at = pl.multiple_of((me ^ k) * rows, 16)
        copy = pltpu.make_async_copy(piece, whole.at[pl.ds(at, rows)], sems.at[k])
        if start:
            copy.start()
        else:
            copy.wait()


def front_kernel(count, me_ref, x_ref, xm_ref, *refs):
    pieces = refs[:count]
    (xt_ref, qt_ref, kt_ref, vt_ref, fw_ref, eb_ref, mix_ref, st_ref, msg_ref, qm_ref, km_ref,
     top_ref, end_ref, w_ref, sems) = refs[count:]
    me = me_ref[0]
    placed(pieces, w_ref, sems, me, True)
    tokens, width = x_ref.shape
    step = 256
    for b in range(tokens // step):
        rows = slice(b * step, (b + 1) * step)
        xt_ref[:, rows] = x_ref[rows, :].T
    placed(pieces, w_ref, sems, me, False)
    high, low = split(xm_ref[...])
    both = w_ref[:, : 2 * width]
    marks = SCALE * (nn(high, both) + nn(low, both))
    qm = marks[:, :width].astype(BF16)
    km = marks[:, width:].astype(BF16)
    qm_ref[...] = qm
    km_ref[...] = km
    for b in range(tokens // step):
        rows = slice(b * step, (b + 1) * step)
        part = x_ref[rows, :]
        for i, (out, scale) in enumerate(((qt_ref, SCALE), (kt_ref, SCALE), (vt_ref, None))):
            y = nn(part, w_ref[:, i * width : (i + 1) * width])
            if scale is not None:
                y = y * scale
            y = y.astype(BF16)
            if i == 2 and b == 0:
                top_ref[...] = y[:REACH]
            if i == 2 and b == tokens // step - 1:
                end_ref[...] = y[step - REACH :]
            out[:, rows] = y.T
    lane = lanes((LANDMARKS, 128))
    stats = jnp.zeros((LANDMARKS, 128), F32)
    pair = []
    for h in range(HEADS):
        s = nn(km[:, hs(h)], qt_ref[hs(h), :])
        s = jnp.exp(s - jnp.max(s, axis=0, keepdims=True))
        fw_ref[hs(h), :] = (s * (1.0 / jnp.sum(s, axis=0, keepdims=True))).astype(BF16)
        s = nn(qm[:, hs(h)], kt_ref[hs(h), :])
        top = jnp.max(s, axis=1, keepdims=True).astype(BF16).astype(F32)
        e = jnp.exp(s - top).astype(BF16)
        eb_ref[hs(h), :] = e
        total = jnp.sum(e.astype(F32), axis=1, keepdims=True)
        stats = jnp.where(lane == h, top, stats)
        stats = jnp.where(lane == 16 + h, total, stats)
        pair.append(nt(e, vt_ref[hs(h), :]))
        if h % 2:
            both = jnp.concatenate(pair, 1)
            mix_ref[h // 2] = both
            msg_ref[h // 2] = both.astype(BF16)
            pair = []
    st_ref[...] = stats
    msg_ref[HEADS // 2] = stat_message(stats)


def stat_message(stats):
    lane = lanes(stats.shape)
    high = stats.astype(BF16).astype(F32)
    low = pltpu.roll(stats - high, 16, 1)
    return jnp.where((lane >= 32) & (lane < 48), low, high).astype(BF16)


def front(me, x, xm, pieces):
    tokens, width = x.shape
    pairs = HEADS // 2
    flat = shape((width, tokens), BF16)
    return pl.pallas_call(
        functools.partial(front_kernel, len(pieces)),
        out_shape=[flat] * 6
        + [
            shape((pairs, LANDMARKS, 128), F32),
            shape((LANDMARKS, 128), F32),
            shape((pairs + 1, LANDMARKS, 128), BF16),
            shape((LANDMARKS, width), BF16),
            shape((LANDMARKS, width), BF16),
            shape((REACH, width), BF16),
            shape((REACH, width), BF16),
        ],
        in_specs=[sspec(), vspec(), vspec()] + [aspec()] * len(pieces),
        out_specs=[vspec()] * 13,
        scratch_shapes=[
            pltpu.VMEM((width, 3 * width), BF16),
            pltpu.SemaphoreType.DMA((len(pieces),)),
        ],
        compiler_params=params(),
        cost_estimate=cost(4.5e9, 16e6, 2e6),
        name="front",
    )(me, x, xm, *pieces)


def merge_kernel(mix_ref, st_ref, got_ref, mix_out, st_out, msg_ref):
    lane = lanes((LANDMARKS, 128))
    got = got_ref[HEADS // 2].astype(F32)
    stats = st_ref[...]
    got = got + jnp.where((lane >= 16) & (lane < 32), pltpu.roll(got, 112, 1), 0.0)
    largest = jnp.maximum(stats, got)
    mine = jnp.exp(jnp.minimum(stats - largest, 0.0))
    theirs = jnp.exp(jnp.minimum(got - largest, 0.0))
    totals = stats * pltpu.roll(mine, 16, 1) + got * pltpu.roll(theirs, 16, 1)
    new = jnp.where(lane < 16, largest, jnp.where(lane < 32, totals, 0.0))
    st_out[...] = new
    for i in range(HEADS // 2):
        a = jnp.where(lane < 64, mine[:, 2 * i : 2 * i + 1], mine[:, 2 * i + 1 : 2 * i + 2])
        b = jnp.where(lane < 64, theirs[:, 2 * i : 2 * i + 1], theirs[:, 2 * i + 1 : 2 * i + 2])
        y = mix_ref[i] * a + got_ref[i].astype(F32) * b
        mix_out[i] = y
        msg_ref[i] = y.astype(BF16)
    msg_ref[HEADS // 2] = stat_message(new)


def merge(mix, stats, got):
    return pl.pallas_call(
        merge_kernel,
        out_shape=[shape(mix.shape, F32), shape(stats.shape, F32), shape(got.shape, BF16)],
        in_specs=[vspec()] * 3,
        out_specs=[vspec()] * 3,
        compiler_params=params(),
        cost_estimate=cost(1e6, 1e6),
        name="merge",
    )(mix, stats, got)


def eye(scale):
    n = LANDMARKS
    return jnp.where(
        lax.broadcasted_iota(jnp.int32, (n, n), 0) == lax.broadcasted_iota(jnp.int32, (n, n), 1),
        jnp.float32(scale),
        0.0,
    )


def landmark_softmax(qm, km, h):
    s = nt(qm[:, hs(h)], km[:, hs(h)])
    s = jnp.exp(s - jnp.max(s, axis=1, keepdims=True))
    return s / jnp.sum(s, axis=1, keepdims=True)


def first_inverse(a):
    columns = jnp.max(jnp.sum(a, axis=0, keepdims=True), axis=1, keepdims=True)
    rows = jnp.max(jnp.sum(a, axis=1, keepdims=True), axis=0, keepdims=True)
    return a.T * (1.0 / (columns * rows))


def inverse_kernel(qm_ref, km_ref, a_ref, z_ref):
    qm, km = qm_ref[...], km_ref[...]
    for h in range(HEADS):
        a = landmark_softmax(qm, km, h)
        a_ref[h] = a
        z_ref[h] = first_inverse(a)

    def step(_, carry):
        ps = [nn3(a_ref[h], z_ref[h]) for h in range(HEADS)]
        ns = [eye(7.0) - p for p in ps]
        ns = [eye(15.0) - nn3(p, n) for p, n in zip(ps, ns)]
        ns = [eye(13.0) - nn3(p, n) for p, n in zip(ps, ns)]
        for h in range(HEADS):
            z_ref[h] = 0.25 * nn3(z_ref[h], ns[h])
        return carry

    lax.fori_loop(0, PINV_ITERS, step, 0)


def inverse(qm, km):
    square = shape((HEADS, LANDMARKS, LANDMARKS), F32)
    return pl.pallas_call(
        inverse_kernel,
        out_shape=[square] * 2,
        in_specs=[vspec()] * 2,
        out_specs=[vspec()] * 2,
        compiler_params=params(),
        cost_estimate=cost(1e9, 1e6),
        name="inverse",
    )(qm, km)


def inverse_back_kernel(qm_ref, km_ref, a_ref, mix_ref, gc_ref, gq_ref, gk_ref, zs, ps, ms, ns, gz, ga):
    qm, km = qm_ref[...], km_ref[...]
    every = range(HEADS)
    for h in every:
        zs[0, h] = first_inverse(a_ref[h])

    def ahead(i, carry):
        p = [nn3(a_ref[h], zs[i, h]) for h in every]
        m = [eye(15.0) - nn3(x, eye(7.0) - x) for x in p]
        n = [eye(13.0) - nn3(x, y) for x, y in zip(p, m)]
        for h in every:
            ps[i, h] = p[h]
            ms[i, h] = m[h]
            ns[i, h] = n[h]
            zs[i + 1, h] = 0.25 * nn3(zs[i, h], n[h])
        return carry

    lax.fori_loop(0, PINV_ITERS - 1, ahead, 0)
    last = PINV_ITERS - 1
    for h in every:
        p = nn3(a_ref[h], zs[last, h])
        m = eye(15.0) - nn3(p, eye(7.0) - p)
        ps[last, h] = p
        ms[last, h] = m
        ns[last, h] = eye(13.0) - nn3(p, m)
        half = slice((h % 2) * HDIM, (h % 2) * HDIM + HDIM)
        gz[h] = nt3(gc_ref[h // 2][:, half], mix_ref[h // 2][:, half])
        ga[h] = jnp.zeros((LANDMARKS, LANDMARKS), F32)

    def back(i, carry):
        i = last - i
        g = [0.25 * gz[h] for h in every]
        g3 = [-tn3(zs[i, h], g[h]) for h in every]
        gz1 = [nt3(g[h], ns[i, h]) for h in every]
        gp = [nt3(g3[h], ms[i, h]) for h in every]
        g2 = [-tn3(ps[i, h], g3[h]) for h in every]
        gp = [gp[h] + nt3(g2[h], eye(7.0) - ps[i, h]) for h in every]
        gp = [gp[h] - tn3(ps[i, h], g2[h]) for h in every]
        for h in every:
            ga[h] = ga[h] + nt3(gp[h], zs[i, h])
            gz[h] = gz1[h] + tn3(a_ref[h], gp[h])
        return carry

    lax.fori_loop(0, PINV_ITERS, back, 0)
    n = LANDMARKS
    for pair in range(HEADS // 2):
        gqs, gks = [], []
        for h in (2 * pair, 2 * pair + 1):
            a = a_ref[h]
            csum = jnp.sum(a, axis=0, keepdims=True)
            rsum = jnp.sum(a, axis=1, keepdims=True)
            cmax = jnp.max(csum, axis=1, keepdims=True)
            rmax = jnp.max(rsum, axis=0, keepdims=True)
            scale = 1.0 / (cmax * rmax)
            gfirst = gz[h]
            gs = jnp.sum(jnp.sum(gfirst * a.T, axis=1, keepdims=True), axis=0, keepdims=True)
            ctop = (csum == cmax).astype(F32)
            rtop = (rsum == rmax).astype(F32)
            gcol = -gs * scale / cmax * ctop / jnp.sum(ctop, axis=1, keepdims=True)
            grow = -gs * scale / rmax * rtop / jnp.sum(rtop, axis=0, keepdims=True)
            g = ga[h] + gfirst.T * scale + gcol + grow
            g = a * (g - jnp.sum(g * a, axis=1, keepdims=True))
            high, low = split(g)
            gqs.append(nn(jnp.concatenate([high, low], 1), jnp.concatenate([km[:, hs(h)]] * 2, 0)))
            gks.append(tn(jnp.concatenate([high, low], 0), jnp.concatenate([qm[:, hs(h)]] * 2, 0)))
        both = slice(pair * 128, pair * 128 + 128)
        gq_ref[:, both] = jnp.concatenate(gqs, 1)
        gk_ref[:, both] = jnp.concatenate(gks, 1)


def inverse_back(qm, km, a, mix, gc):
    square = (HEADS, LANDMARKS, LANDMARKS)
    out = shape(qm.shape, F32)
    return pl.pallas_call(
        inverse_back_kernel,
        out_shape=[out] * 2,
        in_specs=[vspec()] * 5,
        out_specs=[vspec()] * 2,
        scratch_shapes=[pltpu.VMEM((PINV_ITERS,) + square, F32) for _ in range(4)]
        + [pltpu.VMEM(square, F32)] * 2,
        compiler_params=params(),
        cost_estimate=cost(3e9, 2e6),
        name="inverse_back",
    )(qm, km, a, mix, gc)


def widen(out_ref, flat_ref, before_ref, after_ref):
    width, tokens = flat_ref.shape
    zero = jnp.zeros((EDGE - REACH, width), BF16)
    out_ref[:, :EDGE] = jnp.concatenate([zero, before_ref[...]], 0).T
    out_ref[:, EDGE : EDGE + tokens] = flat_ref[...]
    out_ref[:, EDGE + tokens :] = jnp.concatenate([after_ref[...], zero], 0).T


def band(row, step):
    wide = jnp.broadcast_to(row, (step, step + 2 * EDGE))
    return pltpu.roll(wide, 0, 1, stride=1, stride_axis=0).astype(BF16)


def stacked(ref, h, step, margin):
    blocks = (ref.shape[1] - 2 * margin) // step if margin else ref.shape[1] // step
    return jnp.concatenate(
        [ref[hs(h), b * step : (b + 1) * step + 2 * margin] for b in range(blocks)], 0
    )


def conv_kernel_body(vt_ref, before_ref, after_ref, taps_ref, out_ref, wide_ref):
    widen(wide_ref, vt_ref, before_ref, after_ref)
    step = 256
    for h in range(HEADS):
        y = nt(stacked(wide_ref, h, step, EDGE), band(taps_ref[h : h + 1, :], step))
        for b in range(vt_ref.shape[1] // step):
            out_ref[hs(h), b * step : (b + 1) * step] = y[b * HDIM : (b + 1) * HDIM, :]


def conv(vt, before, after, taps):
    width, tokens = vt.shape
    return pl.pallas_call(
        conv_kernel_body,
        out_shape=shape(vt.shape, F32),
        in_specs=[vspec()] * 4,
        out_specs=vspec(),
        scratch_shapes=[pltpu.VMEM((width, tokens + 2 * EDGE), BF16)],
        compiler_params=params(),
        cost_estimate=cost(2e9, 6e6),
        name="conv",
    )(vt, before, after, taps)


def conv_back_kernel(vt_ref, vb_ref, va_ref, gt_ref, gb_ref, ga_ref, taps_ref, out_ref, tap_ref, vwide, gwide):
    widen(vwide, vt_ref, vb_ref, va_ref)
    widen(gwide, gt_ref, gb_ref, ga_ref)
    step = 256
    tokens = vt_ref.shape[1]
    flip = (
        lax.broadcasted_iota(jnp.int32, (step, step), 0)
        + lax.broadcasted_iota(jnp.int32, (step, step), 1)
        == step - 1
    ).astype(BF16)
    rows = []
    for h in range(HEADS):
        y = nt(stacked(gwide, h, step, EDGE), band(taps_ref[h : h + 1, :], step))
        for b in range(tokens // step):
            out_ref[hs(h), b * step : (b + 1) * step] = y[b * HDIM : (b + 1) * HDIM, :]
        turned = nn(stacked(gt_ref, h, step, 0), flip).astype(BF16)
        d = tn(turned, stacked(vwide, h, step, EDGE))
        d = pltpu.roll(d, 0, 1, stride=1, stride_axis=0)
        rows.append(jnp.sum(d, axis=0, keepdims=True))
    rows = jnp.concatenate(rows + [jnp.zeros((4, step + 2 * EDGE), F32)], 0)
    first = step - 1 + EDGE - REACH
    tap_ref[...] = pltpu.roll(rows, step + 2 * EDGE - first, 1)[:, :128]


def conv_back(vt, vb, va, gt, gb, ga, taps):
    width, tokens = vt.shape
    wide = pltpu.VMEM((width, tokens + 2 * EDGE), BF16)
    return pl.pallas_call(
        conv_back_kernel,
        out_shape=[shape(vt.shape, F32), shape((16, 128), F32)],
        in_specs=[vspec()] * 7,
        out_specs=[vspec()] * 2,
        scratch_shapes=[wide, wide],
        compiler_params=params(),
        cost_estimate=cost(4e9, 10e6),
        name="conv_back",
    )(vt, vb, va, gt, gb, ga, taps)


def gelu_pair(x):
    phi = 0.5 * (1.0 + lax.erf(x * (0.5**0.5)))
    return x * phi, phi + x * ((0.5 / jnp.pi) ** 0.5 * jnp.exp(-0.5 * x * x))


def norm_stats(r):
    center = r - jnp.mean(r, axis=-1, keepdims=True)
    rstd = lax.rsqrt(jnp.mean(center * center, axis=-1, keepdims=True) + 1e-05)
    return center * rstd, rstd


def norm_back(gy, xhat, rstd):
    return rstd * (
        gy - jnp.mean(gy, axis=-1, keepdims=True) - xhat * jnp.mean(gy * xhat, axis=-1, keepdims=True)
    )


def mid1_kernel(count, me_ref, z_ref, mix_ref, st_ref, fw_ref, conv_ref, x_ref, gains_ref, *refs):
    wo, up = refs[:count], refs[count : 2 * count]
    (ctx_ref, hidt_ref, xhat_ref, rstd_ref, act_ref, slope_ref, comb_ref, mixn_ref,
     wo_ref, up_ref, sems) = refs[2 * count :]
    me = me_ref[0]

    @pl.when(pl.program_id(0) == 0)
    def _():
        placed(wo, wo_ref, sems.at[0], me, True)
        placed(up, up_ref, sems.at[1], me, True)
        lane = lanes((LANDMARKS, 128))
        stats = st_ref[...]
        for i in range(HEADS // 2):
            low, high = 16 + 2 * i, 17 + 2 * i
            total = jnp.where(lane < 64, stats[:, low : low + 1], stats[:, high : high + 1])
            mixed = mix_ref[i] / total
            mixn_ref[i] = mixed
            comb_ref[i] = jnp.concatenate(
                [nn3(z_ref[2 * i], mixed[:, :HDIM]), nn3(z_ref[2 * i + 1], mixed[:, HDIM:])], 1
            ).astype(BF16)
        placed(wo, wo_ref, sems.at[0], me, False)
        placed(up, up_ref, sems.at[1], me, False)

    for h in range(HEADS):
        half = slice((h % 2) * HDIM, (h % 2) * HDIM + HDIM)
        att = tn(comb_ref[h // 2][:, half], fw_ref[hs(h), :])
        ctx_ref[hs(h), :] = (att + conv_ref[hs(h), :]).astype(BF16)
    context = ctx_ref[...].T
    branch = nn(context, wo_ref[...])
    xhat, rstd = norm_stats(x_ref[...].astype(F32) + branch)
    xhat_ref[...] = xhat
    rstd_ref[...] = jnp.broadcast_to(rstd, rstd_ref.shape)
    hidden = (xhat * gains_ref[0:1, :] + gains_ref[1:2, :]).astype(BF16)
    hidt_ref[...] = hidden.T
    step = 512
    for c in range(up_ref.shape[1] // step):
        cols = slice(c * step, (c + 1) * step)
        act, slope = gelu_pair(nn(hidden, up_ref[:, cols]))
        act_ref[:, cols] = act.astype(BF16)
        slope_ref[:, cols] = slope.astype(BF16)


def mid1(me, z, mix, stats, fw, convt, x, gains, wo, up):
    tokens, width = x.shape
    ff = up[0].shape[1]
    step = 256
    pairs = HEADS // 2

    def whole(a):
        return pl.BlockSpec(a.shape, lambda i, n=a.ndim: (0,) * n)

    tall = pl.BlockSpec((width, step), lambda i: (0, i))
    row = pl.BlockSpec((step, width), lambda i: (i, 0))
    big = pl.BlockSpec((step, ff), lambda i: (i, 0))
    small = pl.BlockSpec((pairs, LANDMARKS, 128), lambda i: (0, 0, 0))
    return pl.pallas_call(
        functools.partial(mid1_kernel, len(wo)),
        grid=(tokens // step,),
        out_shape=[
            shape((width, tokens), BF16),
            shape((width, tokens), BF16),
            shape((tokens, width), F32),
            shape((tokens, 128), F32),
            shape((tokens, ff), BF16),
            shape((tokens, ff), BF16),
            shape((pairs, LANDMARKS, 128), BF16),
            shape((pairs, LANDMARKS, 128), F32),
        ],
        in_specs=[sspec(), whole(z), whole(mix), whole(stats), tall, tall, row, whole(gains)]
        + [aspec()] * (len(wo) + len(up)),
        out_specs=[tall, tall, row, pl.BlockSpec((step, 128), lambda i: (i, 0)), big, big, small, small],
        scratch_shapes=[
            pltpu.VMEM((width, width), BF16),
            pltpu.VMEM((width, ff), BF16),
            pltpu.SemaphoreType.DMA((2, len(wo))),
        ],
        compiler_params=params(),
        cost_estimate=cost(20e9, 30e6, 6e6),
        name="mid_one",
    )(me, z, mix, stats, fw, convt, x, gains, *wo, *up)


def mid2_kernel(count, me_ref, act_ref, xhat_ref, ct_ref, gains_ref, *refs):
    down = refs[:count]
    out_ref, second_ref, redt_ref, sums_ref, down_ref, sems = refs[count:]
    me = me_ref[0]

    @pl.when(pl.program_id(0) == 0)
    def _():
        placed(down, down_ref, sems, me, True)
        sums_ref[...] = jnp.zeros_like(sums_ref)
        placed(down, down_ref, sems, me, False)

    reduced = nn(act_ref[...], down_ref[...])
    hidden = xhat_ref[...] * gains_ref[0:1, :] + gains_ref[1:2, :]
    xhat, rstd = norm_stats(hidden + reduced)
    out_ref[...] = (xhat * gains_ref[2:3, :] + gains_ref[3:4, :]).astype(BF16)
    ct = ct_ref[...].astype(F32)
    sums_ref[0:1, :] = sums_ref[0:1, :] + jnp.sum(ct * xhat, axis=0, keepdims=True)
    sums_ref[1:2, :] = sums_ref[1:2, :] + jnp.sum(ct, axis=0, keepdims=True)
    second = norm_back(ct * gains_ref[2:3, :], xhat, rstd)
    second_ref[...] = second
    redt_ref[...] = second.astype(BF16).T


def mid2(me, act, xhat, ct, gains, down):
    tokens, width = ct.shape
    ff = act.shape[1]
    step = 256
    row = pl.BlockSpec((step, width), lambda i: (i, 0))
    return pl.pallas_call(
        functools.partial(mid2_kernel, len(down)),
        grid=(tokens // step,),
        out_shape=[
            shape((tokens, width), BF16),
            shape((tokens, width), F32),
            shape((width, tokens), BF16),
            shape((8, width), F32),
        ],
        in_specs=[
            sspec(),
            pl.BlockSpec((step, ff), lambda i: (i, 0)),
            row,
            row,
            pl.BlockSpec(gains.shape, lambda i: (0, 0)),
        ]
        + [aspec()] * len(down),
        out_specs=[
            row,
            row,
            pl.BlockSpec((width, step), lambda i: (0, i)),
            pl.BlockSpec((8, width), lambda i: (0, 0)),
        ],
        scratch_shapes=[pltpu.VMEM((ff, width), BF16), pltpu.SemaphoreType.DMA((len(down),))],
        compiler_params=params(),
        cost_estimate=cost(7e9, 20e6),
        name="mid_two",
    )(me, act, xhat, ct, gains, *down)


def mid3_kernel(count, me_ref, second_ref, slope_ref, xhat_ref, rstd_ref, fw_ref, gains_ref, *refs):
    wo, up, down = refs[:count], refs[count : 2 * count], refs[2 * count : 3 * count]
    (ge_ref, first_ref, branch_ref, gct_ref, top_ref, end_ref, sums_ref, gc_ref,
     wo_ref, up_ref, down_ref, sems) = refs[3 * count :]
    me = me_ref[0]
    at = pl.program_id(0)

    @pl.when(at == 0)
    def _():
        placed(down, down_ref, sems.at[0], me, True)
        placed(up, up_ref, sems.at[1], me, True)
        placed(wo, wo_ref, sems.at[2], me, True)
        sums_ref[...] = jnp.zeros_like(sums_ref)
        gc_ref[...] = jnp.zeros_like(gc_ref)
        placed(down, down_ref, sems.at[0], me, False)
        placed(up, up_ref, sems.at[1], me, False)
        placed(wo, wo_ref, sems.at[2], me, False)

    second = second_ref[...]
    red = second.astype(BF16)
    step = 512
    g = second
    for c in range(up_ref.shape[1] // step):
        cols = slice(c * step, (c + 1) * step)
        ge = (nt(red, down_ref[cols, :]) * slope_ref[:, cols].astype(F32)).astype(BF16)
        ge_ref[:, cols] = ge
        g = g + nt(ge, up_ref[:, cols])
    xhat = xhat_ref[...]
    sums_ref[0:1, :] = sums_ref[0:1, :] + jnp.sum(g * xhat, axis=0, keepdims=True)
    sums_ref[1:2, :] = sums_ref[1:2, :] + jnp.sum(g, axis=0, keepdims=True)
    first = norm_back(g * gains_ref[0:1, :], xhat, rstd_ref[:, 0:1])
    first_ref[...] = first
    branch = first.astype(BF16)
    branch_ref[...] = branch
    gctx = nt(branch, wo_ref[...]).astype(BF16)

    @pl.when(at == 0)
    def _():
        top_ref[...] = gctx[:REACH]

    @pl.when(at == pl.num_programs(0) - 1)
    def _():
        end_ref[...] = gctx[gctx.shape[0] - REACH :]

    gct_ref[...] = gctx.T
    for i in range(HEADS // 2):
        gc_ref[i] = gc_ref[i] + jnp.concatenate(
            [nt(fw_ref[hs(h), :], gct_ref[hs(h), :]) for h in (2 * i, 2 * i + 1)], 1
        )


def mid3(me, second, slope, xhat, rstd, fw, gains, wo, up, down):
    tokens, width = second.shape
    ff = slope.shape[1]
    step = 256
    pairs = HEADS // 2
    row = pl.BlockSpec((step, width), lambda i: (i, 0))
    tall = pl.BlockSpec((width, step), lambda i: (0, i))
    big = pl.BlockSpec((step, ff), lambda i: (i, 0))
    edge = pl.BlockSpec((REACH, width), lambda i: (0, 0))
    return pl.pallas_call(
        functools.partial(mid3_kernel, len(wo)),
        grid=(tokens // step,),
        out_shape=[
            shape((tokens, ff), BF16),
            shape((tokens, width), F32),
            shape((tokens, width), BF16),
            shape((width, tokens), BF16),
            shape((REACH, width), BF16),
            shape((REACH, width), BF16),
            shape((8, width), F32),
            shape((pairs, LANDMARKS, 128), F32),
        ],
        in_specs=[
            sspec(),
            row,
            big,
            row,
            pl.BlockSpec((step, 128), lambda i: (i, 0)),
            tall,
            pl.BlockSpec(gains.shape, lambda i: (0, 0)),
        ]
        + [aspec()] * (3 * len(wo)),
        out_specs=[
            big,
            row,
            row,
            tall,
            edge,
            edge,
            pl.BlockSpec((8, width), lambda i: (0, 0)),
            pl.BlockSpec((pairs, LANDMARKS, 128), lambda i: (0, 0, 0)),
        ],
        scratch_shapes=[
            pltpu.VMEM((width, width), BF16),
            pltpu.VMEM((width, ff), BF16),
            pltpu.VMEM((ff, width), BF16),
            pltpu.SemaphoreType.DMA((3, len(wo))),
        ],
        compiler_params=params(),
        cost_estimate=cost(20e9, 40e6),
        name="mid_three",
    )(me, second, slope, xhat, rstd, fw, gains, *wo, *up, *down)


def lead_back_kernel(gct_ref, fw_ref, qt_ref, comb_ref, km_ref, gq_ref, gkm_ref):
    km = km_ref[...]
    pair = []
    for h in range(HEADS):
        half = slice((h % 2) * HDIM, (h % 2) * HDIM + HDIM)
        pf = fw_ref[hs(h), :].astype(F32)
        g = nn(comb_ref[h // 2][:, half], gct_ref[hs(h), :])
        gs = (pf * (g - jnp.sum(pf * g, axis=0, keepdims=True))).astype(BF16)
        gq_ref[hs(h), :] = tn(km[:, hs(h)], gs).astype(BF16)
        pair.append(nt(gs, qt_ref[hs(h), :]))
        if h % 2:
            gkm_ref[:, (h - 1) * HDIM : (h + 1) * HDIM] = jnp.concatenate(pair, 1)
            pair = []


def lead_back(gct, fw, qt, comb, km):
    return pl.pallas_call(
        lead_back_kernel,
        out_shape=[shape(gct.shape, BF16), shape(km.shape, F32)],
        in_specs=[vspec()] * 5,
        out_specs=[vspec()] * 2,
        compiler_params=params(),
        cost_estimate=cost(3e9, 6e6),
        name="lead_back",
    )(gct, fw, qt, comb, km)


def rear_back_kernel(z_ref, gc_ref, mixn_ref, st_ref, own_ref, eb_ref, vt_ref, kt_ref, qm_ref, gvc_ref,
                     gk_ref, gv_ref, gqm_ref):
    qm = qm_ref[...]
    scale = jnp.exp(own_ref[...] - st_ref[...])
    pair = []
    for h in range(HEADS):
        half = slice((h % 2) * HDIM, (h % 2) * HDIM + HDIM)
        gmix = tn3(z_ref[h], gc_ref[h // 2][:, half]).astype(BF16)
        dot = jnp.sum(gmix.astype(F32) * mixn_ref[h // 2][:, half], axis=1, keepdims=True)
        factor = scale[:, h : h + 1] / st_ref[:, 16 + h : 17 + h]
        pb = eb_ref[hs(h), :].astype(F32) * factor
        gs = (pb * (nn(gmix, vt_ref[hs(h), :]) - dot)).astype(BF16)
        gk_ref[hs(h), :] = tn(qm[:, hs(h)], gs).astype(BF16)
        gv_ref[hs(h), :] = (tn(gmix, pb.astype(BF16)) + gvc_ref[hs(h), :]).astype(BF16)
        pair.append(nt(gs, kt_ref[hs(h), :]))
        if h % 2:
            gqm_ref[:, (h - 1) * HDIM : (h + 1) * HDIM] = jnp.concatenate(pair, 1)
            pair = []


def rear_back(z, gc, mixn, stats, own, eb, vt, kt, qm, gvc):
    return pl.pallas_call(
        rear_back_kernel,
        out_shape=[shape(vt.shape, BF16), shape(vt.shape, BF16), shape(qm.shape, F32)],
        in_specs=[vspec()] * 10,
        out_specs=[vspec()] * 3,
        compiler_params=params(),
        cost_estimate=cost(3e9, 10e6),
        name="rear_back",
    )(z, gc, mixn, stats, own, eb, vt, kt, qm, gvc)


def last_kernel(count, segment, me_ref, gq_ref, gk_ref, gv_ref, first_ref, own_ref, *refs):
    pieces = refs[:count]
    out_ref, w_ref, sems = refs[count:]
    me = me_ref[0]
    width = gq_ref.shape[0]

    @pl.when(pl.program_id(0) == 0)
    def _():
        placed(pieces, w_ref, sems, me, True)
        placed(pieces, w_ref, sems, me, False)

    wq, wk, wv = (w_ref[:, i * width : (i + 1) * width] for i in range(3))
    g = SCALE * (nn(wq, gq_ref[...]) + nn(wk, gk_ref[...])) + nn(wv, gv_ref[...])
    own = own_ref[...]
    marks = (SCALE / segment) * (
        nt(own[:, :width].astype(BF16), wq) + nt(own[:, width:].astype(BF16), wk)
    )
    step = out_ref.shape[0]
    token = pl.program_id(0) * step + lax.broadcasted_iota(jnp.int32, (step, own.shape[0]), 0)
    mark = lax.broadcasted_iota(jnp.int32, (step, own.shape[0]), 1) * segment
    pick = ((token >= mark) & (token < mark + segment)).astype(BF16)
    high, low = split(marks)
    spread = nn(pick, high) + nn(pick, low)
    out_ref[...] = (first_ref[...] + g.T + spread).astype(BF16)


def last(me, gq, gk, gv, first, own, pieces, segment):
    width, tokens = gq.shape
    step = 256
    tall = pl.BlockSpec((width, step), lambda i: (0, i))
    row = pl.BlockSpec((step, width), lambda i: (i, 0))
    return pl.pallas_call(
        functools.partial(last_kernel, len(pieces), segment),
        grid=(tokens // step,),
        out_shape=shape((tokens, width), BF16),
        in_specs=[sspec(), tall, tall, tall, row, pl.BlockSpec(own.shape, lambda i: (0, 0))]
        + [aspec()] * len(pieces),
        out_specs=row,
        scratch_shapes=[
            pltpu.VMEM((width, 3 * width), BF16),
            pltpu.SemaphoreType.DMA((len(pieces),)),
        ],
        compiler_params=params(),
        cost_estimate=cost(4e9, 12e6),
        name="last",
    )(me, gq, gk, gv, first, own, *pieces)


def bits(axis):
    size = lax.axis_size(axis)
    assert size & (size - 1) == 0
    return [1 << i for i in range(size.bit_length() - 1)]


def swap(array, axis, bit):
    return lax.ppermute(array, axis, [(i, i ^ bit) for i in range(lax.axis_size(axis))])


def shift(array, axis, by):
    size = lax.axis_size(axis)
    return lax.ppermute(array, axis, [(i, i + by) for i in range(size) if 0 <= i + by < size])


def gathered(array, axis):
    pieces = {0: array}
    order = bits(axis)
    for bit in order[1:] + order[:1]:
        pieces.update({k | bit: swap(piece, axis, bit) for k, piece in list(pieces.items())})
    return [pieces[k] for k in range(lax.axis_size(axis))]


def scattered(pieces, axis):
    pieces = dict(enumerate(pieces))
    for bit in bits(axis):
        pieces = {
            k: (piece.astype(F32) + swap(pieces[k | bit], axis, bit).astype(F32)).astype(BF16)
            for k, piece in pieces.items()
            if not k & bit
        }
    return pieces[0]


def joined(array, axis, dim):
    index = lax.axis_index(axis)
    for bit in bits(axis):
        other = swap(array, axis, bit)
        upper = (index & bit) != 0
        array = jnp.where(
            upper,
            jnp.concatenate([other, array], dim),
            jnp.concatenate([array, other], dim),
        )
    return array


def halved(array, axis, dim):
    index = lax.axis_index(axis)
    for bit in reversed(bits(axis)):
        half = array.shape[dim] // 2
        upper = ((index & bit) != 0).astype(jnp.int32)
        keep = lax.dynamic_slice_in_dim(array, upper * half, half, dim)
        send = lax.dynamic_slice_in_dim(array, (1 - upper) * half, half, dim)
        array = (keep.astype(F32) + swap(send, axis, bit).astype(F32)).astype(BF16)
    return array


def halved_near(array, axis, dim):
    index = lax.axis_index(axis)
    for bit in bits(axis):
        half = array.shape[dim] // 2
        upper = ((index & bit) != 0).astype(jnp.int32)
        keep = lax.dynamic_slice_in_dim(array, upper * half, half, dim)
        send = lax.dynamic_slice_in_dim(array, (1 - upper) * half, half, dim)
        array = (keep.astype(F32) + swap(send, axis, bit).astype(F32)).astype(BF16)
    return array


def joined_near(array, axis, dim):
    index = lax.axis_index(axis)
    for bit in reversed(bits(axis)):
        other = swap(array, axis, bit)
        array = jnp.where(
            (index & bit) != 0,
            jnp.concatenate([other, array], dim),
            jnp.concatenate([array, other], dim),
        )
    return array


def summed(pieces, dim=0):
    mine = scattered(pieces, "fsdp")
    return joined_near(halved_near(mine, "seq", dim), "seq", dim)


def shards(
    inputs,
    cotangent,
    query_weight,
    key_weight,
    value_weight,
    output_weight,
    up_weight,
    down_weight,
    norm_gain,
    norm_shift,
    final_gain,
    final_shift,
    conv_kernel,
):
    x = inputs[0]
    ct = cotangent[0]
    tokens, width = x.shape
    marks = LANDMARKS // lax.axis_size("seq")
    segment = tokens // marks
    count = lax.axis_size("fsdp")
    rows = width // count
    ff = up_weight.shape[1]
    here = lax.axis_index("fsdp")
    me = here.astype(jnp.int32).reshape(1)
    place = lax.axis_index("seq")

    wqkv = gathered(jnp.concatenate([query_weight, key_weight, value_weight], 1), "fsdp")
    xm = jnp.mean(x.reshape(marks, segment, width), axis=1, dtype=F32)
    xm = joined(xm, "seq", 0)
    gains = jnp.stack([norm_gain, norm_shift, final_gain, final_shift])
    gains = lax.all_gather(gains, "fsdp", axis=1, tiled=True).astype(F32)
    gains = jnp.pad(gains, ((0, 4), (0, 0)))
    wo = gathered(output_weight, "fsdp")
    up = gathered(up_weight, "fsdp")
    down = gathered(down_weight, "fsdp")
    space = 256 + 2 * EDGE
    taps = jnp.pad(conv_kernel.T, ((0, 4), (EDGE - REACH, space - KERNEL - EDGE + REACH)))
    spat = jnp.pad(conv_kernel[::-1].T, ((0, 4), (EDGE - REACH, space - KERNEL - EDGE + REACH)))

    (xt, qt, kt, vt, fw, eb, mix, stats, msg, qm, km, v_top, v_end) = front(me, x, xm, wqkv)
    own = stats
    v_before = shift(v_end, "seq", 1)
    v_after = shift(v_top, "seq", -1)
    a, z = inverse(qm, km)
    for bit in bits("seq"):
        mix, stats, msg = merge(mix, stats, swap(msg, "seq", bit))
    convt = conv(vt, v_before, v_after, taps)

    ctxt, hidt, xhat, rstd, act, slope, comb, mixn = mid1(
        me, z, mix, stats, fw, convt, x, gains, wo, up
    )
    out, second, redt, sums2 = mid2(me, act, xhat, ct, gains, down)

    def cut(array, k, size, dim):
        return lax.dynamic_slice_in_dim(array, (here ^ k) * size, size, dim)

    part = ff // count
    g_down = summed([nn(redt, cut(act, k, part, 1)).astype(BF16) for k in range(count)])
    ge, first, branch, gct, g_top, g_end, sums1, gc = mid3(
        me, second, slope, xhat, rstd, fw, gains, wo, up, down
    )
    g_before = shift(g_end, "seq", 1)
    g_after = shift(g_top, "seq", -1)
    for bit in bits("seq"):
        gc = gc + swap(gc.astype(BF16), "seq", bit).astype(F32)
    g_up = summed([nn(cut(hidt, k, rows, 0), ge).astype(BF16) for k in range(count)])
    g_wo = summed([nn(cut(ctxt, k, rows, 0), branch).astype(BF16) for k in range(count)])
    gq, gkm = lead_back(gct, fw, qt, comb, km)
    gvc, g_taps = conv_back(vt, v_before, v_after, gct, g_before, g_after, spat)
    little = jnp.concatenate([sums1[:2], sums2[:2], g_taps[:HEADS].reshape(-1, width)], 0)
    little = jnp.pad(little, ((0, -little.shape[0] % 8), (0, 0)))
    for axis in ("fsdp", "seq"):
        for bit in bits(axis):
            little = little + swap(little, axis, bit)

    gqm_core, gkm_core = inverse_back(qm, km, a, mixn, gc)
    gk, gv, gqm = rear_back(z, gc, mixn, stats, own, eb, vt, kt, qm, gvc)
    mark = lax.broadcasted_iota(jnp.int32, (LANDMARKS, 1), 0)
    owned = (mark >= place * marks) & (mark < (place + 1) * marks)
    gqm = gqm + jnp.where(owned, gqm_core, 0.0)
    gkm = gkm + jnp.where(owned, gkm_core, 0.0)
    landed = halved(jnp.concatenate([gqm, gkm], 1).astype(BF16), "seq", 0).astype(F32)
    xmt = xm.T.astype(BF16)
    xe = jnp.concatenate([xt, xmt], 1)
    gqe = jnp.concatenate([gq, gqm.T.astype(BF16)], 1)
    gke = jnp.concatenate([gk, gkm.T.astype(BF16)], 1)

    def qkv(k):
        lhs = cut(xe, k, rows, 0)
        return jnp.concatenate(
            [
                (SCALE * nt(lhs, gqe)).astype(BF16),
                (SCALE * nt(lhs, gke)).astype(BF16),
                nt(lhs[:, :tokens], gv).astype(BF16),
            ],
            1,
        )

    g_qkv = summed([qkv(k) for k in range(count)])
    grad_x = last(me, gq, gk, gv, first, landed, wqkv, segment)

    def mine(row):
        return lax.dynamic_slice_in_dim(row, here * rows, rows, 0)

    g_kernel = little[4:].reshape(-1)[: HEADS * 128].reshape(HEADS, 128)[:, :KERNEL].T
    return (
        out[None],
        grad_x[None],
        g_qkv[:, :width].astype(F32),
        g_qkv[:, width : 2 * width].astype(F32),
        g_qkv[:, 2 * width :].astype(F32),
        g_wo.astype(F32),
        g_up.astype(F32),
        g_down.T.astype(F32),
        mine(little[0]),
        mine(little[1]),
        mine(little[2]),
        mine(little[3]),
        g_kernel,
    )


def solution(mesh):
    tokens = P("fsdp", "seq", None)
    matrix = P("fsdp", None)
    row = P("fsdp")
    in_specs = (tokens,) * 2 + (matrix,) * 6 + (row,) * 4 + (P(),)
    out_specs = (tokens,) * 2 + (matrix,) * 6 + (row,) * 4 + (P(),)
    return jax.shard_map(shards, mesh=mesh, in_specs=in_specs, out_specs=out_specs, check_vma=False)
```

time: 1030 us -> 542 us (0.53)
  matrix products: 299 us -> 42.1 us
  blocking collectives: 201 us -> 5.46 us
  Pallas kernels: 0 us -> 158 us
  waiting for transfers between devices: 345 us -> 219 us
  local copies, waits for them, and re-layouts: 86.4 us -> 19.9 us
  starting transfers between devices: 11.3 us -> 68 us
  other arithmetic: 55.9 us -> 18.4 us
  between operations: 18.4 us -> 2.04 us
    ppermute x4 -> x69, waiting for transfers between devices: 0.01 us -> 219 us  [the longest x65 219 us: swap(): lax.ppermute(array, axis, [(i, i ^ bit) for i in range(lax.axis_size(axis...]
    dot_general x107 -> x24, matrix products: 238 us -> 42.1 us  [the longest x12 32.2 us: nn(): return jnp.dot(a, b, preferred_element_type=F32)]
    reduce_scatter x5 -> x0, waiting for transfers between devices: 179 us -> none  [the longest x1 50.4 us: shards(): lax.psum_scatter(sum_up.astype(jnp.bfloat16), 'fsdp', scatter_dimension=0...]
    pallas_call x0 -> x14, Pallas kernels: none -> 158 us  [the longest x1 26.3 us: mid3(): pl.pallas_call(functools.partial(mid3_kernel, len(wo)), grid=(tokens // s...]
    all_gather x4 -> x1, blocking collectives: 124 us -> 5.46 us  [shards(): gains = lax.all_gather(gains, 'fsdp', axis=1, tiled=True).astype(F32)]
    psum x2 -> x0, waiting for transfers between devices: 75.6 us -> none  [the longest x1 41.6 us: shards(): lax.psum(mixture_portion.astype(jnp.bfloat16), 'seq').astype(jnp.float32)]
    psum x2 -> x0, blocking collectives: 60.2 us -> none  [the longest x1 37.8 us: shards(): grad_kernel = lax.psum(kernel_part, ('seq', 'fsdp'))]
    conv_general_dilated x3 -> x0, matrix products: 58.2 us -> none  [the longest x2 33.8 us: grouped_conv(): lax.conv_general_dilated(signal[None], taps[:, None, :], (1,), 'VALID', d...]
  transfers between devices with their start and end apart: 21 -> 69, of which waited for: 12 -> 35; matrix products, arithmetic and copies ran while one was open for 34% -> 12% of each run, Pallas kernels for 0% -> 22%
where the time goes in v1:
time: 542 us; the launch traced here: 533 us
  waiting for transfers between devices  219 us (40%)
  Pallas kernels  158 us (29%)
  starting transfers between devices  68 us (13%)
  matrix products  42.1 us (8%)
  local copies, waits for them, and re-layouts  19.9 us (4%)
  other arithmetic  18.4 us (3%)
  blocking collectives  5.46 us (1%)
    ppermute x65, waiting for transfers between devices, swap(): lax.ppermute(array, axis, [(i, i ^ bit) for i in range(lax.axis_size(axis...  219 us
    ppermute x65, starting transfers between devices, swap(): lax.ppermute(array, axis, [(i, i ^ bit) for i in range(lax.axis_size(axis...  56.6 us
    dot_general x12, matrix products, nn(): return jnp.dot(a, b, preferred_element_type=F32)  32.2 us
    pallas_call x1, Pallas kernels, mid3(): pl.pallas_call(functools.partial(mid3_kernel, len(wo)), grid=(tokens // s...  26.3 us
    pallas_call x1, Pallas kernels, inverse_back(): pl.pallas_call(inverse_back_kernel, out_shape=[out] * 2, in_specs=[vspec(...  23.2 us
    pallas_call x1, Pallas kernels, mid1(): pl.pallas_call(functools.partial(mid1_kernel, len(wo)), grid=(tokens // s...  20.8 us
    pallas_call x1, Pallas kernels, front(): pl.pallas_call(functools.partial(front_kernel, len(pieces)), out_shape=[f...  15.3 us
    pallas_call x1, Pallas kernels, mid2(): pl.pallas_call(functools.partial(mid2_kernel, len(down)), grid=(tokens //...  13.9 us
  transfers between devices with their start and end apart: 69, of which 35 were waited for; matrix products, arithmetic and copies ran while one was open for 12% of the time, Pallas kernels for 22%

profile of v1, /device:TPU:0, one launch (start us, length us, event | category | flops | bytes accessed | tf_op | source)
XLA Modules:
  0.0 532.5 jit_solution(10244689591788237284)
XLA Ops:
  7.0 20.4 %collective-permute-done.4.refs_2_ = bf16[192,2304]{1,0:T(8,128)(2,1)S(1)} collective-permute-done((bf16[192,2304]{1,0:T(8,128)(2,1)S(1)}, bf16[192,2304]{1,0:T(8,128)(2,1)S(1)}, u32[]{:S(2)}, u32[]{:S(2)}) %collective-permute-start.4) | collective-permute-done | bytes 884768 | tf_op jit(solution)/shard_map/ppermute | solution.py:821
  45.2 7.6 %collective-permute-done.15.refs_6_ = bf16[192,3072]{1,0:T(8,128)(2,1)} collective-permute-done((bf16[192,3072]{1,0:T(8,128)(2,1)}, bf16[192,3072]{1,0:T(8,128)(2,1)}, u32[]{:S(2)}, u32[]{:S(2)}) %collective-permute-start.15) | collective-permute-done | bytes 1179680 | tf_op jit(solution)/shard_map/ppermute | solution.py:821
  52.9 15.3 %front.1 = (bf16[768,1024]{1,0:T(8,128)(2,1)}, bf16[768,1024]{1,0:T(8,128)(2,1)}, bf16[768,1024]{1,0:T(8,128)(2,1)}, bf16[768,1024]{1,0:T(8,128)(2,1)}, bf16[768...) custom-call(s32[1]{0:T(128)} %bitcast.me_ref, ...), custom_call_target="tpu_custom_call" | custom-call | flops 4499999744 | bytes 16000000 | tf_op jit(solution)/shard_map/front/pallas_call | solution.py:168
  78.9 5.5 %all-gather = bf16[4,192,4]{1,2,0:T(4,128)(2,1)S(1)} all-gather(bf16[1,192,4]{1,2,0:T(4,128)(2,1)S(1)} %maximum_bitcast_fusion), channel_id=1, replica_groups=mesh['seq'=8,'fsdp'=4] {'fsdp'}, dimensions={0}, use_global_device_ids=true | all-gather | bytes 7680 | tf_op jit(solution)/shard_map/all_gather | solution.py:931
  88.5 4.5 collective-permute-start.9
  103.3 9.9 %inverse.1 = (f32[12,64,64]{2,1,0:T(8,128)}, f32[12,64,64]{2,1,0:T(8,128)}) custom-call(bf16[64,768]{1,0:T(8,128)(2,1)} %get-tuple-element.65.qm_ref, bf16[64,768]{1,0:T(8,128)(2,1)} %get-tuple-element.66.km_ref), custom_call_target="tpu_custom_call" | custom-call | flops 1000000000 | bytes 1000000 | tf_op jit(solution)/shard_map/inverse/pallas_call | solution.py:266
  121.0 20.8 %mid_one.1 = (bf16[768,1024]{1,0:T(8,128)(2,1)}, bf16[768,1024]{1,0:T(8,128)(2,1)}, f32[1024,768]{1,0:T(8,128)}, f32[1024,128]{1,0:T(8,128)}, bf16[1024,3072]{1,...) custom-call(s32[1]{0:T(128)} %bitcast.me_ref, ...), custom_call_target="tpu_custom_call" | custom-call | flops 20000000000 | bytes 30000000 | tf_op jit(solution)/shard_map/mid_one/pallas_call | solution.py:517
  143.2 13.9 %mid_two.1 = (bf16[1024,768]{1,0:T(8,128)(2,1)}, f32[1024,768]{1,0:T(8,128)}, bf16[768,1024]{1,0:T(8,128)(2,1)}, f32[8,768]{1,0:T(8,128)}) custom-call(s32[1]{0:T(128)} %bitcast.me_ref, bf16[1024,3072]{1,0:T(8,128)(2,1)} %get-tuple-element.83.act_ref, f32[1024,768]{1,0:T(8,128)} %get-tuple-element.84.xhat_ref, bf16[1024,768]{1,0:T(8,128)(2,1)} %bitcast.66, ...), custom_call_target="tpu_custom_call" | custom-call | flops 7000000000 | bytes 20000000 | tf_op jit(solution)/shard_map/mid_two/pallas_call | solution.py:572
  157.2 26.3 %mid_three.1 = (bf16[1024,3072]{1,0:T(8,128)(2,1)}, f32[1024,768]{1,0:T(8,128)}, bf16[1024,768]{1,0:T(8,128)(2,1)}, bf16[768,1024]{1,0:T(8,128)(2,1)}, bf16[32,7...) custom-call(s32[1]{0:T(128)} %bitcast.me_ref, ...), custom_call_target="tpu_custom_call" | custom-call | flops 20000000000 | bytes 40000000 | tf_op jit(solution)/shard_map/mid_three/pallas_call | solution.py:662
  183.6 5.5 %convolution_convert_fusion.2 = bf16[192,3072]{1,0:T(8,128)(2,1)} fusion(bf16[1024,3072]{1,0:T(8,128)(2,1)} %get-tuple-element.112, bf16[768,1024]{1,0:T(8,128)(2,1)S(1)} %copy-done.41, s32[]{:T(128)S(6)} %select_n.224), kind=kOutput, calls=%fused_computation.4 | convolution fusion | flops 1208549376 | bytes 7864324 | tf_op jit(solution)/shard_map/dot_general | solution.py:24
  207.3 7.5 %conv_back.1 = (f32[768,1024]{1,0:T(8,128)}, f32[16,128]{1,0:T(8,128)}) custom-call(bf16[768,1024]{1,0:T(8,128)(2,1)} %get-tuple-element.80.vt_ref, bf16[32,768]{1,0:T(8,128)(2,1)} %copy-done.31, bf16[32,768]{1,0:T(8,128)(2,1)} %copy-done.30, bf16[768,1024]{1,0:T(8,128)(2,1)} %get-tuple-element.89.gct_ref.gt_ref, bf16[32,768]{1,0:T(8,128)(2,1)} %copy-done.34, ...), custom_call_target="tpu_custom_call" | custom-call | flops 4000000000 | bytes 10000000 | tf_op jit(solution)/shard_map/conv_back/pallas_call | solution.py:433
  224.7 6.6 %lead_back.1 = (bf16[768,1024]{1,0:T(8,128)(2,1)}, f32[64,768]{1,0:T(8,128)}) custom-call(bf16[768,1024]{1,0:T(8,128)(2,1)} %get-tuple-element.89.gct_ref.gt_ref, bf16[768,1024]{1,0:T(8,128)(2,1)} %get-tuple-element.79.fw_ref, bf16[768,1024]{1,0:T(8,128)(2,1)} %get-tuple-element.90.qt_ref, bf16[6,64,128]{2,1,0:T(8,128)(2,1)} %get-tuple-element.91.comb_ref, ...), custom_call_target="tpu_custom_call" | custom-call | flops 3000000000 | bytes 6000000 | tf_op jit(solution)/shard_map/lead_back/pallas_call | solution.py:723
  260.1 23.2 %inverse_back.1 = (f32[64,768]{1,0:T(8,128)}, f32[64,768]{1,0:T(8,128)}) custom-call(bf16[64,768]{1,0:T(8,128)(2,1)} %get-tuple-element.65.qm_ref, bf16[64,768]{1,0:T(8,128)(2,1)} %get-tuple-element.66.km_ref, f32[12,64,64]{2,1,0:T(8,128)} %get-tuple-element.104.a_ref, f32[6,64,128]{2,1,0:T(8,128)} %get-tuple-element.94.mixn_ref.mix_ref, ...), custom_call_target="tpu_custom_call" | custom-call | flops 3000000000 | bytes 2000000 | tf_op jit(solution)/shard_map/inverse_back/pallas_call | solution.py:350
  283.3 10.0 %rear_back.1 = (bf16[768,1024]{1,0:T(8,128)(2,1)}, bf16[768,1024]{1,0:T(8,128)(2,1)}, f32[64,768]{1,0:T(8,128)}) custom-call(f32[12,64,64]{2,1,0:T(8,128)} %get-tuple-element.67.z_ref, f32[6,64,128]{2,1,0:T(8,128)} %convert_add_fusion.gc_ref, f32[6,64,128]{2,1,0:T(8,128)} %get-tuple-element.94.mixn_ref.mix_ref, f32[64,128]{1,0:T(8,128)} %get-tuple-element.78.st_ref, ...), custom_call_target="tpu_custom_call" | custom-call | flops 3000000000 | bytes 10000000 | tf_op jit(solution)/shard_map/rear_back/pallas_call | solution.py:755
  307.9 6.3 %collective-permute-done.25 = bf16[32,1536]{1,0:T(8,128)(2,1)S(1)} collective-permute-done((bf16[32,1536]{1,0:T(8,128)(2,1)S(1)}, bf16[32,1536]{1,0:T(8,128)(2,1)S(1)}, u32[]{:S(2)}, u32[]{:S(2)}) %collective-permute-start.25) | collective-permute-done | bytes 98336 | tf_op jit(solution)/shard_map/ppermute | solution.py:821
  314.8 8.3 %collective-permute-done.39 = bf16[192,768]{1,0:T(8,128)(2,1)S(1)} collective-permute-done((bf16[192,768]{1,0:T(8,128)(2,1)S(1)}, bf16[192,768]{1,0:T(8,128)(2,1)S(1)}, u32[]{:S(2)}, u32[]{:S(2)}) %collective-permute-start.39) | collective-permute-done | bytes 294944 | tf_op jit(solution)/shard_map/ppermute | solution.py:821
  330.1 4.5 collective-permute-done.26
  334.7 4.7 collective-permute-done.41
  339.5 4.8 collective-permute-done.42
  353.1 13.7 %last.1 = bf16[1024,768]{1,0:T(8,128)(2,1)} custom-call(s32[1]{0:T(128)} %bitcast.me_ref, bf16[768,1024]{1,0:T(8,128)(2,1)} %get-tuple-element.92.gq_ref, bf16[768,1024]{1,0:T(8,128)(2,1)} %get-tuple-element.100.gk_ref, bf16[768,1024]{1,0:T(8,128)(2,1)} %get-tuple-element.101.gv_ref, f32[1024,768]{1,0:T(8,128)} %get-tuple-element.102.first_ref, ...), custom_call_target="tpu_custom_call" | custom-call | flops 4000000000 | bytes 12000000 | tf_op jit(solution)/shard_map/last/pallas_call | solution.py:797
  368.1 5.2 collective-permute-done.45
  378.2 4.5 fusion.8
  383.5 12.4 %collective-permute-done.30 = bf16[192,2304]{1,0:T(8,128)(2,1)S(1)} collective-permute-done((bf16[192,2304]{1,0:T(8,128)(2,1)S(1)}, bf16[192,2304]{1,0:T(8,128)(2,1)S(1)}, u32[]{:S(2)}, u32[]{:S(2)}) %collective-permute-start.30) | collective-permute-done | bytes 884768 | tf_op jit(solution)/shard_map/ppermute | solution.py:821
  397.1 24.0 %collective-permute-done.57 = bf16[768,768]{1,0:T(8,128)(2,1)S(1)} collective-permute-done((bf16[768,768]{1,0:T(8,128)(2,1)S(1)}, bf16[768,768]{1,0:T(8,128)(2,1)S(1)}, u32[]{:S(2)}, u32[]{:S(2)}) %collective-permute-start.57) | collective-permute-done | bytes 1179680 | tf_op jit(solution)/shard_map/ppermute | solution.py:821
  426.1 19.0 %collective-permute-done.48 = bf16[192,3072]{1,0:T(8,128)(2,1)S(1)} collective-permute-done((bf16[192,3072]{1,0:T(8,128)(2,1)S(1)}, bf16[192,3072]{1,0:T(8,128)(2,1)S(1)}, u32[]{:S(2)}, u32[]{:S(2)}) %collective-permute-start.48) | collective-permute-done | bytes 1179680 | tf_op jit(solution)/shard_map/ppermute | solution.py:821
  449.9 4.4 collective-permute-done.33
  456.7 6.0 %collective-permute-done.49 = bf16[96,3072]{1,0:T(8,128)(2,1)S(1)} collective-permute-done((bf16[96,3072]{1,0:T(8,128)(2,1)S(1)}, bf16[96,3072]{1,0:T(8,128)(2,1)S(1)}, u32[]{:S(2)}, u32[]{:S(2)}) %collective-permute-start.49) | collective-permute-done | bytes 589856 | tf_op jit(solution)/shard_map/ppermute | solution.py:821
  466.2 6.4 %collective-permute-done.50 = bf16[48,3072]{1,0:T(8,128)(2,1)S(1)} collective-permute-done((bf16[48,3072]{1,0:T(8,128)(2,1)S(1)}, bf16[48,3072]{1,0:T(8,128)(2,1)S(1)}, u32[]{:S(2)}, u32[]{:S(2)}) %collective-permute-start.50) | collective-permute-done | bytes 294944 | tf_op jit(solution)/shard_map/ppermute | solution.py:821
  475.9 9.4 %collective-permute-done.51 = bf16[24,3072]{1,0:T(8,128)(2,1)S(1)} collective-permute-done((bf16[24,3072]{1,0:T(8,128)(2,1)S(1)}, bf16[24,3072]{1,0:T(8,128)(2,1)S(1)}, u32[]{:S(2)}, u32[]{:S(2)}) %collective-permute-start.51) | collective-permute-done | bytes 147488 | tf_op jit(solution)/shard_map/ppermute | solution.py:821
  498.1 5.1 collective-permute-done.62
  510.4 10.5 %collective-permute-done.63 = bf16[384,768]{1,0:T(8,128)(2,1)S(1)} collective-permute-done((bf16[384,768]{1,0:T(8,128)(2,1)S(1)}, bf16[384,768]{1,0:T(8,128)(2,1)S(1)}, u32[]{:S(2)}, u32[]{:S(2)}) %collective-permute-start.63) | collective-permute-done | bytes 589856 | tf_op jit(solution)/shard_map/ppermute | solution.py:821
  523.1 7.6 %collective-permute-done.54 = bf16[96,3072]{1,0:T(8,128)(2,1)S(1)} collective-permute-done((bf16[96,3072]{1,0:T(8,128)(2,1)S(1)}, bf16[96,3072]{1,0:T(8,128)(2,1)S(1)}, u32[]{:S(2)}, u32[]{:S(2)}) %collective-permute-start.54) | collective-permute-done | bytes 589856 | tf_op jit(solution)/shard_map/ppermute | solution.py:821
  (341 shorter events, 196.4 us)
Async XLA Ops:
  3.9 23.5 %collective-permute-start.4 = (bf16[192,2304]{1,0:T(8,128)(2,1)S(1)}, bf16[192,2304]{1,0:T(8,128)(2,1)S(1)}, u32[]{:S(2)}, u32[]{:S(2)}) collective-permute-start(bf16[192,2304]{1,0:T(8,128)(2,1)S(1)} %constant_dynamic-update-slice_fusion.refs_0_), channel_id=1, source_target_pairs={{0,2},{1,3},{2,0},{3,1},{4,6},{5,7},{6,4},{7,5},{8,10},{9,11},{10,... | collective-permute-start | bytes 2654216 | tf_op jit(solution)/shard_map/ppermute | solution.py:821
  6.9 45.9 %collective-permute-start.15 = (bf16[192,3072]{1,0:T(8,128)(2,1)}, bf16[192,3072]{1,0:T(8,128)(2,1)}, u32[]{:S(2)}, u32[]{:S(2)}) collective-permute-start(bf16[192,3072]{1,0:T(8,128)(2,1)} %refs_4_.3), channel_id=1, source_target_pairs={{0,2},{1,3},{2,0},{3,1},{4,6},{5,7},{6,4},{7,5},{8,10},{9,11},{10,... | collective-permute-start | bytes 3538952 | tf_op jit(solution)/shard_map/ppermute | solution.py:821
  7.0 45.8 %collective-permute-start.3 = (bf16[192,2304]{1,0:T(8,128)(2,1)S(1)}, bf16[192,2304]{1,0:T(8,128)(2,1)}, u32[]{:S(2)}, u32[]{:S(2)}) collective-permute-start(bf16[192,2304]{1,0:T(8,128)(2,1)S(1)} %constant_dynamic-update-slice_fusion.refs_0_), channel_id=1, source_target_pairs={{0,1},{1,0},{2,3},{3,2},{4,5},{5,4},{6,7},{7,6},{8,9},{9,8},{10,11... | collective-permute-start | bytes 2654216 | tf_op jit(solution)/shard_map/ppermute | solution.py:821
  27.4 25.4 %collective-permute-start.5 = (bf16[192,2304]{1,0:T(8,128)(2,1)S(1)}, bf16[192,2304]{1,0:T(8,128)(2,1)}, u32[]{:S(2)}, u32[]{:S(2)}) collective-permute-start(bf16[192,2304]{1,0:T(8,128)(2,1)S(1)} %collective-permute-done.4.refs_2_), channel_id=1, source_target_pairs={{0,1},{1,0},{2,3},{3,2},{4,5},{5,4},{6,7},{7,6},{8,9},{9,8},{10,11... | collective-permute-start | bytes 2654216 | tf_op jit(solution)/shard_map/ppermute | solution.py:821
  38.8 81.4 %collective-permute-start.14 = (bf16[192,3072]{1,0:T(8,128)(2,1)S(1)}, bf16[192,3072]{1,0:T(8,128)(2,1)}, u32[]{:S(2)}, u32[]{:S(2)}) collective-permute-start(bf16[192,3072]{1,0:T(8,128)(2,1)S(1)} %copy-done.21), channel_id=1, source_target_pairs={{0,1},{1,0},{2,3},{3,2},{4,5},{5,4},{6,7},{7,6},{8,9},{9,8},{10,11... | collective-permute-start | bytes 3538952 | tf_op jit(solution)/shard_map/ppermute | solution.py:821
  42.9 77.3 %collective-permute-start.18 = (bf16[768,768]{1,0:T(8,128)(2,1)}, bf16[768,768]{1,0:T(8,128)(2,1)}, u32[]{:S(2)}, u32[]{:S(2)}) collective-permute-start(bf16[768,768]{1,0:T(8,128)(2,1)} %refs_8_.1), channel_id=1, source_target_pairs={{0,2},{1,3},{2,0},{3,1},{4,6},{5,7},{6,4},{7,5},{8,10},{9,11},{10,... | collective-permute-start | bytes 3538952 | tf_op jit(solution)/shard_map/ppermute | solution.py:821
  52.7 67.5 %collective-permute-start.16 = (bf16[192,3072]{1,0:T(8,128)(2,1)}, bf16[192,3072]{1,0:T(8,128)(2,1)}, u32[]{:S(2)}, u32[]{:S(2)}) collective-permute-start(bf16[192,3072]{1,0:T(8,128)(2,1)} %collective-permute-done.15.refs_6_), channel_id=1, source_target_pairs={{0,1},{1,0},{2,3},{3,2},{4,5},{5,4},{6,7},{7,6},{8,9},{9,8},{10,11... | collective-permute-start | bytes 3538952 | tf_op jit(solution)/shard_map/ppermute | solution.py:821
  70.3 18.3 %collective-permute-start.12 = (bf16[192,768]{1,0:T(8,128)(2,1)S(1)}, bf16[192,768]{1,0:T(8,128)(2,1)}, u32[]{:S(2)}, u32[]{:S(2)}) collective-permute-start(bf16[192,768]{1,0:T(8,128)(2,1)S(1)} %copy-done.27), channel_id=1, source_target_pairs={{0,2},{1,3},{2,0},{3,1},{4,6},{5,7},{6,4},{7,5},{8,10},{9,11},{10,... | collective-permute-start | bytes 884744 | tf_op jit(solution)/shard_map/ppermute | solution.py:821
  98.1 21.5 %collective-permute-start.11 = (bf16[192,768]{1,0:T(8,128)(2,1)S(1)}, bf16[192,768]{1,0:T(8,128)(2,1)S(1)}, u32[]{:S(2)}, u32[]{:S(2)}) collective-permute-start(bf16[192,768]{1,0:T(8,128)(2,1)S(1)} %copy-done.27), channel_id=1, source_target_pairs={{0,1},{1,0},{2,3},{3,2},{4,5},{5,4},{6,7},{7,6},{8,9},{9,8},{10,11... | collective-permute-start | bytes 884744 | tf_op jit(solution)/shard_map/ppermute | solution.py:821
  101.7 18.6 %collective-permute-start.13 = (bf16[192,768]{1,0:T(8,128)(2,1)}, bf16[192,768]{1,0:T(8,128)(2,1)S(1)}, u32[]{:S(2)}, u32[]{:S(2)}) collective-permute-start(bf16[192,768]{1,0:T(8,128)(2,1)} %collective-permute-done.12.refs_2_), channel_id=1, source_target_pairs={{0,1},{1,0},{2,3},{3,2},{4,5},{5,4},{6,7},{7,6},{8,9},{9,8},{10,11... | collective-permute-start | bytes 884744 | tf_op jit(solution)/shard_map/ppermute | solution.py:821
  119.6 22.2 %collective-permute-start.17 = (bf16[768,768]{1,0:T(8,128)(2,1)S(1)}, bf16[768,768]{1,0:T(8,128)(2,1)S(1)}, u32[]{:S(2)}, u32[]{:S(2)}) collective-permute-start(bf16[768,768]{1,0:T(8,128)(2,1)S(1)} %copy-done.22), channel_id=1, source_target_pairs={{0,1},{1,0},{2,3},{3,2},{4,5},{5,4},{6,7},{7,6},{8,9},{9,8},{10,11... | collective-permute-start | bytes 3538952 | tf_op jit(solution)/shard_map/ppermute | solution.py:821
  120.2 21.6 %collective-permute-start.19 = (bf16[768,768]{1,0:T(8,128)(2,1)}, bf16[768,768]{1,0:T(8,128)(2,1)S(1)}, u32[]{:S(2)}, u32[]{:S(2)}) collective-permute-start(bf16[768,768]{1,0:T(8,128)(2,1)} %collective-permute-done.18.refs_2_.refs_10_), channel_id=1, source_target_pairs={{0,1},{1,0},{2,3},{3,2},{4,5},{5,4},{6,7},{7,6},{8,9},{9,8},{10,11... | collective-permute-start | bytes 3538952 | tf_op jit(solution)/shard_map/ppermute | solution.py:821
  191.6 15.1 %collective-permute-start.23 = (bf16[32,768]{1,0:T(8,128)(2,1)S(1)}, bf16[32,768]{1,0:T(8,128)(2,1)S(1)}, u32[]{:S(2)}, u32[]{:S(2)}) collective-permute-start(bf16[32,768]{1,0:T(8,128)(2,1)S(1)} %copy-done.33), channel_id=1, source_target_pairs={{0,4},{4,8},{8,12},{12,16},{16,20},{20,24},{24,28},{1,5},{5,9},{9,... | collective-permute-start | bytes 147464 | tf_op jit(solution)/shard_map/ppermute | solution.py:826
  199.7 175.0 %collective-permute-start.56 = (bf16[768,768]{1,0:T(8,128)(2,1)}, bf16[768,768]{1,0:T(8,128)(2,1)}, u32[]{:S(2)}, u32[]{:S(2)}) collective-permute-start(bf16[768,768]{1,0:T(8,128)(2,1)} %fusion.26), channel_id=1, source_target_pairs={{0,1},{1,0},{2,3},{3,2},{4,5},{5,4},{6,7},{7,6},{8,9},{9,8},{10,11... | collective-permute-start | bytes 3538952 | tf_op jit(solution)/shard_map/ppermute | solution.py:821
  206.3 190.9 %collective-permute-start.55 = (bf16[768,768]{1,0:T(8,128)(2,1)}, bf16[768,768]{1,0:T(8,128)(2,1)}, u32[]{:S(2)}, u32[]{:S(2)}) collective-permute-start(bf16[768,768]{1,0:T(8,128)(2,1)} %fusion.20), channel_id=1, source_target_pairs={{0,1},{1,0},{2,3},{3,2},{4,5},{5,4},{6,7},{7,6},{8,9},{9,8},{10,11... | collective-permute-start | bytes 3538952 | tf_op jit(solution)/shard_map/ppermute | solution.py:821
  220.0 156.6 %collective-permute-start.47 = (bf16[192,3072]{1,0:T(8,128)(2,1)}, bf16[192,3072]{1,0:T(8,128)(2,1)}, u32[]{:S(2)}, u32[]{:S(2)}) collective-permute-start(bf16[192,3072]{1,0:T(8,128)(2,1)} %convolution_convert_fusion), channel_id=1, source_target_pairs={{0,1},{1,0},{2,3},{3,2},{4,5},{5,4},{6,7},{7,6},{8,9},{9,8},{10,11... | collective-permute-start | bytes 3538952 | tf_op jit(solution)/shard_map/ppermute | solution.py:821
  220.4 18.7 %collective-permute-start.20 = (bf16[6,64,128]{2,1,0:T(8,128)(2,1)S(1)}, bf16[6,64,128]{2,1,0:T(8,128)(2,1)S(1)}, u32[]{:S(2)}, u32[]{:S(2)}) collective-permute-start(bf16[6,64,128]{2,1,0:T(8,128)(2,1)S(1)} %convert_element_type.413), channel_id=1, source_target_pairs={{0,4},{4,0},{8,12},{12,8},{16,20},{20,16},{24,28},{28,24},{1,5},{5... | collective-permute-start | bytes 294920 | tf_op jit(solution)/shard_map/ppermute | solution.py:821
  249.2 65.5 %collective-permute-start.37 = (bf16[192,768]{1,0:T(8,128)(2,1)}, bf16[192,768]{1,0:T(8,128)(2,1)}, u32[]{:S(2)}, u32[]{:S(2)}) collective-permute-start(bf16[192,768]{1,0:T(8,128)(2,1)} %convolution_convert_fusion.6), channel_id=1, source_target_pairs={{0,1},{1,0},{2,3},{3,2},{4,5},{5,4},{6,7},{7,6},{8,9},{9,8},{10,11... | collective-permute-start | bytes 884744 | tf_op jit(solution)/shard_map/ppermute | solution.py:821
  314.7 52.3 %collective-permute-start.29 = (bf16[192,2304]{1,0:T(8,128)(2,1)S(1)}, bf16[192,2304]{1,0:T(8,128)(2,1)S(1)}, u32[]{:S(2)}, u32[]{:S(2)}) collective-permute-start(bf16[192,2304]{1,0:T(8,128)(2,1)S(1)} %pad_maximum_fusion.3), channel_id=1, source_target_pairs={{0,1},{1,0},{2,3},{3,2},{4,5},{5,4},{6,7},{7,6},{8,9},{9,8},{10,11... | collective-permute-start | bytes 2654216 | tf_op jit(solution)/shard_map/ppermute | solution.py:821
  366.9 15.8 %collective-permute-start.28 = (bf16[192,2304]{1,0:T(8,128)(2,1)S(1)}, bf16[192,2304]{1,0:T(8,128)(2,1)S(1)}, u32[]{:S(2)}, u32[]{:S(2)}) collective-permute-start(bf16[192,2304]{1,0:T(8,128)(2,1)S(1)} %pad_maximum_fusion.2), channel_id=1, source_target_pairs={{0,1},{1,0},{2,3},{3,2},{4,5},{5,4},{6,7},{7,6},{8,9},{9,8},{10,11... | collective-permute-start | bytes 2654216 | tf_op jit(solution)/shard_map/ppermute | solution.py:821
  373.3 22.6 %collective-permute-start.30 = (bf16[192,2304]{1,0:T(8,128)(2,1)S(1)}, bf16[192,2304]{1,0:T(8,128)(2,1)S(1)}, u32[]{:S(2)}, u32[]{:S(2)}) collective-permute-start(bf16[192,2304]{1,0:T(8,128)(2,1)S(1)} %add_convert_fusion.4), channel_id=1, source_target_pairs={{0,2},{1,3},{2,0},{3,1},{4,6},{5,7},{6,4},{7,5},{8,10},{9,11},{10,... | collective-permute-start | bytes 2654216 | tf_op jit(solution)/shard_map/ppermute | solution.py:821
  374.7 51.4 %collective-permute-start.46 = (bf16[192,3072]{1,0:T(8,128)(2,1)S(1)}, bf16[192,3072]{1,0:T(8,128)(2,1)S(1)}, u32[]{:S(2)}, u32[]{:S(2)}) collective-permute-start(bf16[192,3072]{1,0:T(8,128)(2,1)S(1)} %copy-done.23), channel_id=1, source_target_pairs={{0,1},{1,0},{2,3},{3,2},{4,5},{5,4},{6,7},{7,6},{8,9},{9,8},{10,11... | collective-permute-start | bytes 3538952 | tf_op jit(solution)/shard_map/ppermute | solution.py:821
  376.6 44.6 %collective-permute-start.57 = (bf16[768,768]{1,0:T(8,128)(2,1)S(1)}, bf16[768,768]{1,0:T(8,128)(2,1)S(1)}, u32[]{:S(2)}, u32[]{:S(2)}) collective-permute-start(bf16[768,768]{1,0:T(8,128)(2,1)S(1)} %add_convert_fusion.1), channel_id=1, source_target_pairs={{0,2},{1,3},{2,0},{3,1},{4,6},{5,7},{6,4},{7,5},{8,10},{9,11},{10,... | collective-permute-start | bytes 3538952 | tf_op jit(solution)/shard_map/ppermute | solution.py:821
  382.7 62.5 %collective-permute-start.48 = (bf16[192,3072]{1,0:T(8,128)(2,1)S(1)}, bf16[192,3072]{1,0:T(8,128)(2,1)S(1)}, u32[]{:S(2)}, u32[]{:S(2)}) collective-permute-start(bf16[192,3072]{1,0:T(8,128)(2,1)S(1)} %fusion.8), channel_id=1, source_target_pairs={{0,2},{1,3},{2,0},{3,1},{4,6},{5,7},{6,4},{7,5},{8,10},{9,11},{10,... | collective-permute-start | bytes 3538952 | tf_op jit(solution)/shard_map/ppermute | solution.py:821
  396.3 27.7 %collective-permute-start.31 = (bf16[96,2304]{1,0:T(8,128)(2,1)S(1)}, bf16[96,2304]{1,0:T(8,128)(2,1)S(1)}, u32[]{:S(2)}, u32[]{:S(2)}) collective-permute-start(bf16[96,2304]{1,0:T(8,128)(2,1)S(1)} %constant_dynamic-slice_fusion.15), channel_id=1, source_target_pairs={{0,4},{4,0},{8,12},{12,8},{16,20},{20,16},{24,28},{28,24},{1,5},{5... | collective-permute-start | bytes 1327112 | tf_op jit(solution)/shard_map/ppermute | solution.py:821
  423.0 31.7 %collective-permute-start.58 = (bf16[384,768]{1,0:T(8,128)(2,1)S(1)}, bf16[384,768]{1,0:T(8,128)(2,1)S(1)}, u32[]{:S(2)}, u32[]{:S(2)}) collective-permute-start(bf16[384,768]{1,0:T(8,128)(2,1)S(1)} %constant_dynamic-slice_fusion.6), channel_id=1, source_target_pairs={{0,4},{4,0},{8,12},{12,8},{16,20},{20,16},{24,28},{28,24},{1,5},{5... | collective-permute-start | bytes 1769480 | tf_op jit(solution)/shard_map/ppermute | solution.py:821
  424.1 22.8 %collective-permute-start.32 = (bf16[48,2304]{1,0:T(8,128)(2,1)S(1)}, bf16[48,2304]{1,0:T(8,128)(2,1)S(1)}, u32[]{:S(2)}, u32[]{:S(2)}) collective-permute-start(bf16[48,2304]{1,0:T(8,128)(2,1)S(1)} %constant_dynamic-slice_fusion.14), channel_id=1, source_target_pairs={{0,8},{4,12},{8,0},{12,4},{16,24},{20,28},{24,16},{28,20},{1,9},{5... | collective-permute-start | bytes 663560 | tf_op jit(solution)/shard_map/ppermute | solution.py:821
  454.4 31.0 %collective-permute-start.34 = (bf16[24,2304]{1,0:T(8,128)(2,1)S(1)}, bf16[24,2304]{1,0:T(8,128)(2,1)S(1)}, u32[]{:S(2)}, u32[]{:S(2)}) collective-permute-start(bf16[24,2304]{1,0:T(8,128)(2,1)S(1)} %add_convert_fusion.15), channel_id=1, source_target_pairs={{0,16},{4,20},{8,24},{12,28},{16,0},{20,4},{24,8},{28,12},{1,17},{... | collective-permute-start | bytes 331784 | tf_op jit(solution)/shard_map/ppermute | solution.py:821
  473.8 17.2 %collective-permute-start.61 = (bf16[96,768]{1,0:T(8,128)(2,1)S(1)}, bf16[96,768]{1,0:T(8,128)(2,1)S(1)}, u32[]{:S(2)}, u32[]{:S(2)}) collective-permute-start(bf16[96,768]{1,0:T(8,128)(2,1)S(1)} %add_convert_fusion.12), channel_id=1, source_target_pairs={{0,16},{4,20},{8,24},{12,28},{16,0},{20,4},{24,8},{28,12},{1,17},{... | collective-permute-start | bytes 442376 | tf_op jit(solution)/shard_map/ppermute | solution.py:821
  493.3 14.4 %collective-permute-start.53 = (bf16[48,3072]{1,0:T(8,128)(2,1)S(1)}, bf16[48,3072]{1,0:T(8,128)(2,1)S(1)}, u32[]{:S(2)}, u32[]{:S(2)}) collective-permute-start(bf16[48,3072]{1,0:T(8,128)(2,1)S(1)} %maximum_select_fusion.7), channel_id=1, source_target_pairs={{0,8},{4,12},{8,0},{12,4},{16,24},{20,28},{24,16},{28,20},{1,9},{5... | collective-permute-start | bytes 884744 | tf_op jit(solution)/shard_map/ppermute | solution.py:821
  503.4 17.5 %collective-permute-start.63 = (bf16[384,768]{1,0:T(8,128)(2,1)S(1)}, bf16[384,768]{1,0:T(8,128)(2,1)S(1)}, u32[]{:S(2)}, u32[]{:S(2)}) collective-permute-start(bf16[384,768]{1,0:T(8,128)(2,1)S(1)} %maximum_select_fusion.4), channel_id=1, source_target_pairs={{0,4},{4,0},{8,12},{12,8},{16,20},{20,16},{24,28},{28,24},{1,5},{5... | collective-permute-start | bytes 1769480 | tf_op jit(solution)/shard_map/ppermute | solution.py:821
  507.8 22.9 %collective-permute-start.54 = (bf16[96,3072]{1,0:T(8,128)(2,1)S(1)}, bf16[96,3072]{1,0:T(8,128)(2,1)S(1)}, u32[]{:S(2)}, u32[]{:S(2)}) collective-permute-start(bf16[96,3072]{1,0:T(8,128)(2,1)S(1)} %maximum_select_fusion.3), channel_id=1, source_target_pairs={{0,4},{4,0},{8,12},{12,8},{16,20},{20,16},{24,28},{28,24},{1,5},{5... | collective-permute-start | bytes 1769480 | tf_op jit(solution)/shard_map/ppermute | solution.py:821
  (87 other events, 964.0 us)

commit v2 on v1

v2 whole, which is shorter than its diff:
```python
import functools

import jax
import jax.numpy as jnp
from jax import lax
from jax.experimental import pallas as pl
from jax.experimental.pallas import tpu as pltpu
from jax.sharding import PartitionSpec as P

HEADS = 12
HDIM = 64
LANDMARKS = 64
KERNEL = 65
PINV_ITERS = 6
REACH = KERNEL // 2
EDGE = 128
SCALE = HDIM ** (-0.25)
F32 = jnp.float32
BF16 = jnp.bfloat16
VM = 56 * 1024 * 1024


def nn(a, b):
    return jnp.dot(a, b, preferred_element_type=F32)


def nt(a, b):
    return lax.dot_general(a, b, (((1,), (1,)), ((), ())), preferred_element_type=F32)


def tn(a, b):
    return lax.dot_general(a, b, (((0,), (0,)), ((), ())), preferred_element_type=F32)


def split(a):
    high = a.astype(BF16)
    return high, (a - high.astype(F32)).astype(BF16)


def nn3(a, b):
    ah, al = split(a)
    bh, bl = split(b)
    return nn(jnp.concatenate([ah, ah, al], 1), jnp.concatenate([bh, bl, bh], 0))


def nt3(a, b):
    ah, al = split(a)
    bh, bl = split(b)
    return nt(jnp.concatenate([ah, ah, al], 1), jnp.concatenate([bh, bl, bh], 1))


def tn3(a, b):
    ah, al = split(a)
    bh, bl = split(b)
    return tn(jnp.concatenate([ah, ah, al], 0), jnp.concatenate([bh, bl, bh], 0))


def lanes(shape):
    return lax.broadcasted_iota(jnp.int32, shape, len(shape) - 1)


def hs(h):
    return slice(h * HDIM, (h + 1) * HDIM)


def vspec():
    return pl.BlockSpec(memory_space=pltpu.VMEM)


def sspec():
    return pl.BlockSpec(memory_space=pltpu.SMEM)


def aspec():
    return pl.BlockSpec(memory_space=pl.ANY)


def shape(dims, kind):
    return jax.ShapeDtypeStruct(tuple(dims), kind)


def params():
    return pltpu.CompilerParams(vmem_limit_bytes=VM)


def cost(flops, traffic, trans=0):
    return pl.CostEstimate(flops=int(flops), bytes_accessed=int(traffic), transcendentals=int(trans))


def call(kernel, args, in_specs, out_shape, out_specs, name, work, grid=(), scratch=(), after=()):
    count, extra = len(args), len(after)

    def body(*refs):
        kernel(*refs[:count], *refs[count + extra :])

    return pl.pallas_call(
        body,
        grid=grid,
        out_shape=out_shape,
        in_specs=list(in_specs) + [aspec()] * extra,
        out_specs=out_specs,
        scratch_shapes=list(scratch),
        compiler_params=params(),
        cost_estimate=work,
        name=name,
    )(*args, *after)


def placed(pieces, whole, sems, me, start):
    rows = pieces[0].shape[0]
    for k, piece in enumerate(pieces):
        at = pl.multiple_of((me ^ k) * rows, 16)
        copy = pltpu.make_async_copy(piece, whole.at[pl.ds(at, rows)], sems.at[k])
        if start:
            copy.start()
        else:
            copy.wait()


def xor_rows(out_ref, value, me, count):
    rows = value.shape[0] // count
    for r in range(count):
        at = pl.multiple_of((me ^ r) * rows, 16)
        out_ref[pl.ds(at, rows), :] = value[r * rows : (r + 1) * rows]


def pack_kernel(x_ref, *refs):
    weights, (all_ref, xm_ref, sems) = refs[:-3], refs[-3:]
    copies = []
    for i, w in enumerate(weights):
        to = all_ref.at[:, pl.ds(i * w.shape[1], w.shape[1])]
        copies.append(pltpu.make_async_copy(w, to, sems.at[i]))
        copies[-1].start()
    size, marks, width = xm_ref.shape
    tokens = x_ref.shape[0]
    segment = tokens // marks
    means = [
        jnp.mean(x_ref[m * segment : (m + 1) * segment, :].astype(F32), axis=0, keepdims=True)
        for m in range(marks)
    ]
    means = jnp.concatenate(means, 0)
    for i in range(size):
        xm_ref[i] = means
    for copy in copies:
        copy.wait()


def pack(x, weights, size, marks):
    rows, width = weights[0].shape
    return call(
        pack_kernel,
        (x, *weights),
        [vspec()] * 4,
        [shape((rows, 3 * width), BF16), shape((size, marks, width), F32)],
        [vspec()] * 2,
        "pack",
        cost(1e6, 1e5),
        scratch=[pltpu.SemaphoreType.DMA((3,))],
    )


def front_kernel(count, me_ref, x_ref, xm_ref, *refs):
    pieces = refs[:count]
    (xt_ref, xmt_ref, qt_ref, kt_ref, vt_ref, fw_ref, eb_ref, st_ref, msg_ref, qm_ref, km_ref,
     top_ref, end_ref, w_ref, sems) = refs[count:]
    me = me_ref[0]
    placed(pieces, w_ref, sems, me, True)
    tokens, width = x_ref.shape
    step = 256
    for b in range(tokens // step):
        rows = slice(b * step, (b + 1) * step)
        xor_rows(xt_ref.at[:, rows], x_ref[rows, :].T, me, count)
    placed(pieces, w_ref, sems, me, False)
    high, low = split(xm_ref[...])
    wide = jnp.concatenate([xm_ref[...], jnp.zeros_like(xm_ref)], 0)
    xor_rows(xmt_ref, wide.T.astype(BF16)[:, :LANDMARKS], me, count)
    both = w_ref[:, : 2 * width]
    marks = SCALE * (nn(high, both) + nn(low, both))
    qm = marks[:, :width].astype(BF16)
    km = marks[:, width:].astype(BF16)
    qm_ref[...] = qm
    km_ref[...] = km
    for b in range(tokens // step):
        rows = slice(b * step, (b + 1) * step)
        part = x_ref[rows, :]
        for i, (out, scale) in enumerate(((qt_ref, SCALE), (kt_ref, SCALE), (vt_ref, None))):
            y = nn(part, w_ref[:, i * width : (i + 1) * width])
            if scale is not None:
                y = y * scale
            y = y.astype(BF16)
            if i == 2 and b == 0:
                top_ref[...] = y[:REACH]
            if i == 2 and b == tokens // step - 1:
                end_ref[...] = y[step - REACH :]
            out[:, rows] = y.T
    lane = lanes((LANDMARKS, 128))
    stats = jnp.zeros((LANDMARKS, 128), F32)
    pair = []
    for h in range(HEADS):
        s = nn(km[:, hs(h)], qt_ref[hs(h), :])
        s = jnp.exp(s - jnp.max(s, axis=0, keepdims=True))
        fw_ref[hs(h), :] = (s * (1.0 / jnp.sum(s, axis=0, keepdims=True))).astype(BF16)
        s = nn(qm[:, hs(h)], kt_ref[hs(h), :])
        top = jnp.max(s, axis=1, keepdims=True).astype(BF16).astype(F32)
        e = jnp.exp(s - top).astype(BF16)
        eb_ref[hs(h), :] = e
        total = jnp.sum(e.astype(F32), axis=1, keepdims=True)
        stats = jnp.where(lane == h, top, stats)
        stats = jnp.where(lane == 16 + h, total, stats)
        pair.append(nt(e, vt_ref[hs(h), :]))
        if h % 2:
            both = jnp.concatenate(pair, 1).astype(BF16)
            for d in range(msg_ref.shape[0]):
                msg_ref[d, h // 2] = both
            pair = []
    st_ref[...] = stats
    for d in range(msg_ref.shape[0]):
        msg_ref[d, HEADS // 2] = stat_message(stats)


def stat_message(stats):
    lane = lanes(stats.shape)
    high = stats.astype(BF16).astype(F32)
    low = pltpu.roll(stats - high, 16, 1)
    return jnp.where((lane >= 32) & (lane < 48), low, high).astype(BF16)


def front(me, x, xm, pieces, size):
    tokens, width = x.shape
    pairs = HEADS // 2
    flat = shape((width, tokens), BF16)
    return pl.pallas_call(
        functools.partial(front_kernel, len(pieces)),
        out_shape=[flat, shape((width, LANDMARKS), BF16)]
        + [flat] * 5
        + [
            shape((LANDMARKS, 128), F32),
            shape((size, pairs + 1, LANDMARKS, 128), BF16),
            shape((LANDMARKS, width), BF16),
            shape((LANDMARKS, width), BF16),
            shape((REACH, width), BF16),
            shape((REACH, width), BF16),
        ],
        in_specs=[sspec(), vspec(), vspec()] + [aspec()] * len(pieces),
        out_specs=[vspec()] * 13,
        scratch_shapes=[
            pltpu.VMEM((width, 3 * width), BF16),
            pltpu.SemaphoreType.DMA((len(pieces),)),
        ],
        compiler_params=params(),
        cost_estimate=cost(4.5e+08, 1.6e+06),
        name="front",
    )(me, x, xm, *pieces)


def merged(msg_ref, mixn_ref, st_ref):
    lane = lanes((LANDMARKS, 128))
    size = msg_ref.shape[0]
    stats = []
    for d in range(size):
        got = msg_ref[d, HEADS // 2].astype(F32)
        stats.append(got + jnp.where((lane >= 16) & (lane < 32), pltpu.roll(got, 112, 1), 0.0))
    largest = functools.reduce(jnp.maximum, stats)
    weights = [jnp.exp(jnp.minimum(st - largest, 0.0)) for st in stats]
    total = sum(st * pltpu.roll(w, 16, 1) for st, w in zip(stats, weights))
    st_ref[...] = jnp.where(lane < 16, largest, total)
    for i in range(HEADS // 2):

        def both(a, at):
            return jnp.where(lane < HDIM, a[:, at : at + 1], a[:, at + 1 : at + 2])

        y = sum(msg_ref[d, i].astype(F32) * both(weights[d], 2 * i) for d in range(size))
        mixn_ref[i] = y / both(total, 16 + 2 * i)


def eye(scale):
    n = LANDMARKS
    return jnp.where(
        lax.broadcasted_iota(jnp.int32, (n, n), 0) == lax.broadcasted_iota(jnp.int32, (n, n), 1),
        jnp.float32(scale),
        0.0,
    )


def landmark_softmax(qm, km, h):
    s = nt(qm[:, hs(h)], km[:, hs(h)])
    s = jnp.exp(s - jnp.max(s, axis=1, keepdims=True))
    return s / jnp.sum(s, axis=1, keepdims=True)


def first_inverse(a):
    columns = jnp.max(jnp.sum(a, axis=0, keepdims=True), axis=1, keepdims=True)
    rows = jnp.max(jnp.sum(a, axis=1, keepdims=True), axis=0, keepdims=True)
    return a.T * (1.0 / (columns * rows))


def inverse_kernel(qm_ref, km_ref, a_ref, z_ref, zs, ps, ms, ns):
    qm, km = qm_ref[...], km_ref[...]
    every = range(HEADS)
    for h in every:
        a = landmark_softmax(qm, km, h)
        a_ref[h] = a
        z_ref[h] = first_inverse(a)

    def step(i, carry):
        p = [nn3(a_ref[h], z_ref[h]) for h in every]
        m = [eye(15.0) - nn3(x, eye(7.0) - x) for x in p]
        n = [eye(13.0) - nn3(x, y) for x, y in zip(p, m)]
        for h in every:
            ps[i, h] = p[h]
            ms[i, h] = m[h]
            ns[i, h] = n[h]
            zs[i, h] = z_ref[h]
            z_ref[h] = 0.25 * nn3(z_ref[h], n[h])
        return carry

    lax.fori_loop(0, PINV_ITERS, step, 0)


def inverse(qm, km):
    square = shape((HEADS, LANDMARKS, LANDMARKS), F32)
    steps = shape((PINV_ITERS, HEADS, LANDMARKS, LANDMARKS), F32)
    return call(
        inverse_kernel,
        (qm, km),
        [vspec()] * 2,
        [square] * 2 + [steps] * 4,
        [vspec()] * 6,
        "inverse",
        cost(1e8, 1e6),
    )


def inverse_back_kernel(size, me_ref, qm_ref, km_ref, a_ref, mix_ref, gc_ref, zs, ps, ms, ns, gqp_ref, gkp_ref,
                        gq_ref, gk_ref, gz, ga):
    place = me_ref[1]
    slots = range(-(-HEADS // size))
    heads = [place + size * j for j in slots]
    safe = [jnp.minimum(h, HEADS - 1) for h in heads]
    lane = lanes((LANDMARKS, 128))
    last = PINV_ITERS - 1
    gq_ref[...] = gqp_ref[...]
    gk_ref[...] = gkp_ref[...]

    def half(pair, h):
        return jnp.where(h % 2 == 0, pair[:, :HDIM], pair[:, HDIM:])

    for j in slots:
        h = safe[j]
        gz[j] = nt3(half(gc_ref[h // 2], h), half(mix_ref[h // 2], h))
        ga[j] = jnp.zeros((LANDMARKS, LANDMARKS), F32)

    def back(i, carry):
        i = last - i
        for j in slots:
            h = safe[j]
            z, p, m, n, a = zs[i, h], ps[i, h], ms[i, h], ns[i, h], a_ref[h]
            g = 0.25 * gz[j]
            g3 = -tn3(z, g)
            g2 = -tn3(p, g3)
            gp = nt3(g3, m) + nt3(g2, eye(7.0) - p) - tn3(p, g2)
            ga[j] = ga[j] + nt3(gp, z)
            gz[j] = nt3(g, n) + tn3(a, gp)
        return carry

    lax.fori_loop(0, PINV_ITERS, back, 0)
    for j in slots:
        h = safe[j]
        a = a_ref[h]
        csum = jnp.sum(a, axis=0, keepdims=True)
        rsum = jnp.sum(a, axis=1, keepdims=True)
        cmax = jnp.max(csum, axis=1, keepdims=True)
        rmax = jnp.max(rsum, axis=0, keepdims=True)
        scale = 1.0 / (cmax * rmax)
        gfirst = gz[j]
        gs = jnp.sum(jnp.sum(gfirst * a.T, axis=1, keepdims=True), axis=0, keepdims=True)
        ctop = (csum == cmax).astype(F32)
        rtop = (rsum == rmax).astype(F32)
        gcol = -gs * scale / cmax * ctop / jnp.sum(ctop, axis=1, keepdims=True)
        grow = -gs * scale / rmax * rtop / jnp.sum(rtop, axis=0, keepdims=True)
        g = ga[j] + gfirst.T * scale + gcol + grow
        g = a * (g - jnp.sum(g * a, axis=1, keepdims=True))
        high, low = split(g)
        at = pl.ds(pl.multiple_of(h // 2 * 128, 128), 128)
        qm, km = half(qm_ref[:, at].astype(F32), h), half(km_ref[:, at].astype(F32), h)
        qm, km = qm.astype(BF16), km.astype(BF16)
        gq = nn(jnp.concatenate([high, low], 1), jnp.concatenate([km] * 2, 0))
        gk = tn(jnp.concatenate([high, low], 0), jnp.concatenate([qm] * 2, 0))
        mine = ((lane >= HDIM) == (h % 2 == 1)) & (heads[j] < HEADS)
        gq_ref[:, at] = gq_ref[:, at] + jnp.where(mine, jnp.concatenate([gq, gq], 1), 0.0)
        gk_ref[:, at] = gk_ref[:, at] + jnp.where(mine, jnp.concatenate([gk, gk], 1), 0.0)


def inverse_back(me, qm, km, a, mix, gc, saved, gqm, gkm, size, after=()):
    square = (-(-HEADS // size), LANDMARKS, LANDMARKS)
    out = shape(qm.shape, F32)
    return call(
        functools.partial(inverse_back_kernel, size),
        (me, qm, km, a, mix, gc, *saved, gqm, gkm),
        [sspec()] + [vspec()] * 11,
        [out] * 2,
        [vspec()] * 2,
        "inverse_back",
        cost(2e8, 2e6),
        scratch=[pltpu.VMEM(square, F32)] * 2,
        after=after,
    )


def widen(out_ref, flat_ref, before_ref, after_ref):
    width, tokens = flat_ref.shape
    zero = jnp.zeros((EDGE - REACH, width), BF16)
    out_ref[:, :EDGE] = jnp.concatenate([zero, before_ref[...]], 0).T
    out_ref[:, EDGE : EDGE + tokens] = flat_ref[...]
    out_ref[:, EDGE + tokens :] = jnp.concatenate([after_ref[...], zero], 0).T


def band(row, step):
    wide = jnp.broadcast_to(row, (step, step + 2 * EDGE))
    return pltpu.roll(wide, 0, 1, stride=1, stride_axis=0).astype(BF16)


def stacked(ref, h, step, margin):
    blocks = (ref.shape[1] - 2 * margin) // step if margin else ref.shape[1] // step
    return jnp.concatenate(
        [ref[hs(h), b * step : (b + 1) * step + 2 * margin] for b in range(blocks)], 0
    )


def conv_kernel_body(vt_ref, before_ref, after_ref, taps_ref, out_ref, wide_ref):
    widen(wide_ref, vt_ref, before_ref, after_ref)
    step = 256
    for h in range(HEADS):
        y = nt(stacked(wide_ref, h, step, EDGE), band(taps_ref[h : h + 1, :], step))
        for b in range(vt_ref.shape[1] // step):
            out_ref[hs(h), b * step : (b + 1) * step] = y[b * HDIM : (b + 1) * HDIM, :]


def conv(vt, before, after, taps):
    width, tokens = vt.shape
    return pl.pallas_call(
        conv_kernel_body,
        out_shape=shape(vt.shape, F32),
        in_specs=[vspec()] * 4,
        out_specs=vspec(),
        scratch_shapes=[pltpu.VMEM((width, tokens + 2 * EDGE), BF16)],
        compiler_params=params(),
        cost_estimate=cost(2e+08, 600000),
        name="conv",
    )(vt, before, after, taps)


def conv_back_kernel(vt_ref, vb_ref, va_ref, gt_ref, gb_ref, ga_ref, taps_ref, out_ref, tap_ref, vwide, gwide):
    widen(vwide, vt_ref, vb_ref, va_ref)
    widen(gwide, gt_ref, gb_ref, ga_ref)
    step = 256
    tokens = vt_ref.shape[1]
    flip = (
        lax.broadcasted_iota(jnp.int32, (step, step), 0)
        + lax.broadcasted_iota(jnp.int32, (step, step), 1)
        == step - 1
    ).astype(BF16)
    rows = []
    for h in range(HEADS):
        y = nt(stacked(gwide, h, step, EDGE), band(taps_ref[h : h + 1, :], step))
        for b in range(tokens // step):
            out_ref[hs(h), b * step : (b + 1) * step] = y[b * HDIM : (b + 1) * HDIM, :]
        turned = nn(stacked(gt_ref, h, step, 0), flip).astype(BF16)
        d = tn(turned, stacked(vwide, h, step, EDGE))
        d = pltpu.roll(d, 0, 1, stride=1, stride_axis=0)
        rows.append(jnp.sum(d, axis=0, keepdims=True))
    rows = jnp.concatenate(rows + [jnp.zeros((4, step + 2 * EDGE), F32)], 0)
    first = step - 1 + EDGE - REACH
    tap_ref[...] = pltpu.roll(rows, step + 2 * EDGE - first, 1)[:, :128]


def conv_back(vt, vb, va, gt, gb, ga, taps, after=()):
    width, tokens = vt.shape
    wide = pltpu.VMEM((width, tokens + 2 * EDGE), BF16)
    return call(
        conv_back_kernel,
        (vt, vb, va, gt, gb, ga, taps),
        [vspec()] * 7,
        [shape(vt.shape, F32), shape((16, 128), F32)],
        [vspec()] * 2,
        "conv_back",
        cost(4e8, 1e6),
        scratch=[wide, wide],
        after=after,
    )


def gelu_pair(x):
    phi = 0.5 * (1.0 + lax.erf(x * (0.5**0.5)))
    return x * phi, phi + x * ((0.5 / jnp.pi) ** 0.5 * jnp.exp(-0.5 * x * x))


def norm_stats(r):
    center = r - jnp.mean(r, axis=-1, keepdims=True)
    rstd = lax.rsqrt(jnp.mean(center * center, axis=-1, keepdims=True) + 1e-05)
    return center * rstd, rstd


def norm_back(gy, xhat, rstd):
    return rstd * (
        gy - jnp.mean(gy, axis=-1, keepdims=True) - xhat * jnp.mean(gy * xhat, axis=-1, keepdims=True)
    )


STEP = 256


def whole(a):
    return pl.BlockSpec(a.shape, lambda i, n=a.ndim: (0,) * n)


def fixed(*dims):
    return pl.BlockSpec(dims, lambda i, n=len(dims): (0,) * n)


def tall(rows):
    return pl.BlockSpec((rows, STEP), lambda i: (0, i))


def row(width):
    return pl.BlockSpec((STEP, width), lambda i: (i, 0))


def mid1_kernel(count, me_ref, z_ref, msg_ref, fw_ref, conv_ref, x_ref, gains_ref, *refs):
    wo, up = refs[:count], refs[count : 2 * count]
    (ctx_ref, hidt_ref, xhat_ref, rstd_ref, act_ref, slope_ref, comb_ref, mixn_ref, st_ref,
     wo_ref, up_ref, sems) = refs[2 * count :]
    me = me_ref[0]

    @pl.when(pl.program_id(0) == 0)
    def _():
        placed(wo, wo_ref, sems.at[0], me, True)
        placed(up, up_ref, sems.at[1], me, True)
        merged(msg_ref, mixn_ref, st_ref)
        for i in range(HEADS // 2):
            mixed = mixn_ref[i]
            comb_ref[i] = jnp.concatenate(
                [nn3(z_ref[2 * i], mixed[:, :HDIM]), nn3(z_ref[2 * i + 1], mixed[:, HDIM:])], 1
            ).astype(BF16)
        placed(wo, wo_ref, sems.at[0], me, False)
        placed(up, up_ref, sems.at[1], me, False)

    for h in range(HEADS):
        half = slice((h % 2) * HDIM, (h % 2) * HDIM + HDIM)
        att = tn(comb_ref[h // 2][:, half], fw_ref[hs(h), :])
        ctx_ref[hs(h), :] = (att + conv_ref[hs(h), :]).astype(BF16)
    branch = nn(ctx_ref[...].T, wo_ref[...])
    xhat, rstd = norm_stats(x_ref[...].astype(F32) + branch)
    xhat_ref[...] = xhat
    rstd_ref[...] = jnp.broadcast_to(rstd, rstd_ref.shape)
    hidden = (xhat * gains_ref[0:1, :] + gains_ref[1:2, :]).astype(BF16)
    xor_rows(hidt_ref, hidden.T, me, count)
    part = up_ref.shape[1] // count
    for c in range(count):
        at = slice(c * part, (c + 1) * part)
        act, slope = gelu_pair(nn(hidden, up_ref[:, at]))
        act_ref[:, at] = act.astype(BF16)
        slope_ref[:, at] = slope.astype(BF16)


def mid1(me, z, msgs, fw, convt, x, gains, wo, up, after=()):
    tokens, width = x.shape
    ff = up[0].shape[1]
    pairs = HEADS // 2
    return call(
        functools.partial(mid1_kernel, len(wo)),
        (me, z, msgs, fw, convt, x, gains, *wo, *up),
        [sspec(), whole(z), whole(msgs), tall(width), tall(width), row(width), whole(gains)]
        + [aspec()] * (len(wo) + len(up)),
        [
            shape((width, tokens), BF16),
            shape((width, tokens), BF16),
            shape((tokens, width), F32),
            shape((tokens, 128), F32),
            shape((tokens, ff), BF16),
            shape((tokens, ff), BF16),
            shape((pairs, LANDMARKS, 128), BF16),
            shape((pairs, LANDMARKS, 128), F32),
            shape((LANDMARKS, 128), F32),
        ],
        [tall(width), tall(width), row(width), row(128), row(ff), row(ff)]
        + [fixed(pairs, LANDMARKS, 128)] * 2
        + [fixed(LANDMARKS, 128)],
        "mid_one",
        cost(2e9, 3e6),
        grid=(tokens // STEP,),
        scratch=[
            pltpu.VMEM((width, width), BF16),
            pltpu.VMEM((width, ff), BF16),
            pltpu.SemaphoreType.DMA((2, len(wo))),
        ],
        after=after,
    )


def mid2_kernel(count, me_ref, act_ref, slope_ref, xhat_ref, ct_ref, gains_ref, *refs):
    down = refs[:count]
    out_ref, second_ref, redt_ref, ge_ref, sums_ref, down_ref, sems = refs[count:]
    me = me_ref[0]

    @pl.when(pl.program_id(0) == 0)
    def _():
        placed(down, down_ref, sems, me, True)
        sums_ref[...] = jnp.zeros_like(sums_ref)
        placed(down, down_ref, sems, me, False)

    reduced = nn(act_ref[...], down_ref[...])
    hidden = xhat_ref[...] * gains_ref[0:1, :] + gains_ref[1:2, :]
    xhat, rstd = norm_stats(hidden + reduced)
    out_ref[...] = (xhat * gains_ref[2:3, :] + gains_ref[3:4, :]).astype(BF16)
    ct = ct_ref[...].astype(F32)
    sums_ref[0:1, :] = sums_ref[0:1, :] + jnp.sum(ct * xhat, axis=0, keepdims=True)
    sums_ref[1:2, :] = sums_ref[1:2, :] + jnp.sum(ct, axis=0, keepdims=True)
    second = norm_back(ct * gains_ref[2:3, :], xhat, rstd)
    second_ref[...] = second
    red = second.astype(BF16)
    redt_ref[...] = red.T
    part = down_ref.shape[0] // count
    for k in range(count):
        cols = slice(k * part, (k + 1) * part)
        ge = nt(red, down_ref[cols, :]) * slope_ref[:, cols].astype(F32)
        ge_ref[:, cols] = ge.astype(BF16)


def mid2(me, act, slope, xhat, ct, gains, down, after=()):
    tokens, width = ct.shape
    ff = act.shape[1]
    return call(
        functools.partial(mid2_kernel, len(down)),
        (me, act, slope, xhat, ct, gains, *down),
        [sspec(), row(ff), row(ff), row(width), row(width), whole(gains)] + [aspec()] * len(down),
        [
            shape((tokens, width), BF16),
            shape((tokens, width), F32),
            shape((width, tokens), BF16),
            shape((tokens, ff), BF16),
            shape((8, width), F32),
        ],
        [row(width), row(width), tall(width), row(ff), fixed(8, width)],
        "mid_two",
        cost(2e9, 3e6),
        grid=(tokens // STEP,),
        scratch=[pltpu.VMEM((ff, width), BF16), pltpu.SemaphoreType.DMA((len(down),))],
        after=after,
    )


def mid3_kernel(count, me_ref, second_ref, ge_ref, xhat_ref, rstd_ref, fw_ref, gains_ref, *refs):
    wo, up = refs[:count], refs[count : 2 * count]
    (first_ref, branch_ref, gct_ref, top_ref, end_ref, sums_ref, parts_ref,
     wo_ref, up_ref, gc_ref, sems) = refs[2 * count :]
    me = me_ref[0]
    at = pl.program_id(0)

    @pl.when(at == 0)
    def _():
        placed(up, up_ref, sems.at[0], me, True)
        placed(wo, wo_ref, sems.at[1], me, True)
        sums_ref[...] = jnp.zeros_like(sums_ref)
        gc_ref[...] = jnp.zeros_like(gc_ref)
        placed(up, up_ref, sems.at[0], me, False)
        placed(wo, wo_ref, sems.at[1], me, False)

    g = second_ref[...] + nt(ge_ref[...], up_ref[...])
    xhat = xhat_ref[...]
    sums_ref[0:1, :] = sums_ref[0:1, :] + jnp.sum(g * xhat, axis=0, keepdims=True)
    sums_ref[1:2, :] = sums_ref[1:2, :] + jnp.sum(g, axis=0, keepdims=True)
    first = norm_back(g * gains_ref[0:1, :], xhat, rstd_ref[:, 0:1])
    first_ref[...] = first
    branch = first.astype(BF16)
    branch_ref[...] = branch
    gctx = nt(branch, wo_ref[...]).astype(BF16)

    @pl.when(at == 0)
    def _():
        top_ref[...] = gctx[:REACH]

    @pl.when(at == pl.num_programs(0) - 1)
    def _():
        end_ref[...] = gctx[gctx.shape[0] - REACH :]

    gct_ref[...] = gctx.T
    for i in range(HEADS // 2):
        gc_ref[i] = gc_ref[i] + jnp.concatenate(
            [nt(fw_ref[hs(h), :], gct_ref[hs(h), :]) for h in (2 * i, 2 * i + 1)], 1
        )

    @pl.when(at == pl.num_programs(0) - 1)
    def _():
        for d in range(parts_ref.shape[0]):
            parts_ref[d] = gc_ref[...].astype(BF16)


def mid3(me, second, ge, xhat, rstd, fw, gains, wo, up, size, after=()):
    tokens, width = second.shape
    ff = ge.shape[1]
    pairs = HEADS // 2
    return call(
        functools.partial(mid3_kernel, len(wo)),
        (me, second, ge, xhat, rstd, fw, gains, *wo, *up),
        [sspec(), row(width), row(ff), row(width), row(128), tall(width), whole(gains)]
        + [aspec()] * (2 * len(wo)),
        [
            shape((tokens, width), F32),
            shape((tokens, width), BF16),
            shape((width, tokens), BF16),
            shape((REACH, width), BF16),
            shape((REACH, width), BF16),
            shape((8, width), F32),
            shape((size, pairs, LANDMARKS, 128), BF16),
        ],
        [row(width), row(width), tall(width), fixed(REACH, width), fixed(REACH, width),
         fixed(8, width), fixed(size, pairs, LANDMARKS, 128)],
        "mid_three",
        cost(2e9, 3e6),
        grid=(tokens // STEP,),
        scratch=[
            pltpu.VMEM((width, width), BF16),
            pltpu.VMEM((width, ff), BF16),
            pltpu.VMEM((pairs, LANDMARKS, 128), F32),
            pltpu.SemaphoreType.DMA((2, len(wo))),
        ],
        after=after,
    )


def grad_down_kernel(count, me_ref, red_ref, act_ref, *outs):
    part = act_ref.shape[1] // count
    for k in range(count):
        at = pl.ds(pl.multiple_of((me_ref[0] ^ k) * part, 128), part)
        outs[k][...] = nn(red_ref[...], act_ref[:, at]).astype(BF16)


def grad_down(count, me, redt, act, after=()):
    width = redt.shape[0]
    return call(
        functools.partial(grad_down_kernel, count),
        (me, redt, act),
        [sspec(), vspec(), vspec()],
        [shape((width, act.shape[1] // count), BF16)] * count,
        [vspec()] * count,
        "grad_down",
        cost(5e8, 1e6),
        after=after,
    )


def grad_up_kernel(count, hid_ref, ge_ref, *outs):
    y = nn(hid_ref[...], ge_ref[...]).astype(BF16)
    rows = y.shape[0] // count
    for k in range(count):
        outs[k][...] = y[k * rows : (k + 1) * rows]


def grad_up(count, hidt, ge, after=()):
    width, tokens = hidt.shape
    ff = ge.shape[1]
    step = 768
    return call(
        functools.partial(grad_up_kernel, count),
        (hidt, ge),
        [whole(hidt), pl.BlockSpec((tokens, step), lambda i: (0, i))],
        [shape((width // count, ff), BF16)] * count,
        [pl.BlockSpec((width // count, step), lambda i: (0, i))] * count,
        "grad_up",
        cost(5e8, 1e6),
        grid=(ff // step,),
        after=after,
    )


def grad_o_kernel(count, me_ref, ctx_ref, branch_ref, sums1_ref, sums2_ref, taps_ref, *refs):
    outs, y_ref = refs[:count], refs[count]
    width = ctx_ref.shape[0]
    rows = width // count
    taps = jnp.concatenate([taps_ref[:HEADS], jnp.zeros((HEADS, width - 128), F32)], 1)
    little = jnp.concatenate(
        [sums1_ref[0:2, :], sums2_ref[0:2, :], taps, jnp.zeros((128 - 4 - HEADS, width), F32)], 0
    )
    y_ref[:, width:] = little.T.astype(BF16)
    y_ref[:, :width] = nn(ctx_ref[...], branch_ref[...]).astype(BF16)
    for k in range(count):
        outs[k][...] = y_ref[pl.ds(pl.multiple_of((me_ref[0] ^ k) * rows, 16), rows), :]


def grad_o(count, me, ctxt, branch, sums1, sums2, taps, after=()):
    width = ctxt.shape[0]
    return call(
        functools.partial(grad_o_kernel, count),
        (me, ctxt, branch, sums1, sums2, taps),
        [sspec()] + [vspec()] * 5,
        [shape((width // count, width + 128), BF16)] * count,
        [vspec()] * count,
        "grad_o",
        cost(2e8, 1e6),
        scratch=[pltpu.VMEM((width, width + 128), BF16)],
        after=after,
    )


def grad_qkv_kernel(count, xt_ref, xmt_ref, gq_ref, gk_ref, gv_ref, gqm_ref, gkm_ref, *outs):
    width = xt_ref.shape[0]
    rows = width // count
    for i, (g_ref, m_ref) in enumerate(((gq_ref, gqm_ref), (gk_ref, gkm_ref), (gv_ref, None))):
        y = nt(xt_ref[...], g_ref[...])
        if m_ref is not None:
            y = y + nn(xmt_ref[...], m_ref[...].astype(BF16))
        y = y.astype(BF16)
        for k in range(count):
            outs[k][:, i * width : (i + 1) * width] = y[k * rows : (k + 1) * rows]


def grad_qkv(count, xt, xmt, gq, gk, gv, gqm, gkm, after=()):
    width = xt.shape[0]
    return call(
        functools.partial(grad_qkv_kernel, count),
        (xt, xmt, gq, gk, gv, gqm, gkm),
        [vspec()] * 7,
        [shape((width // count, 3 * width), BF16)] * count,
        [vspec()] * count,
        "grad_qkv",
        cost(2e8, 1e6),
        after=after,
    )


def lead_back_kernel(gct_ref, fw_ref, qt_ref, comb_ref, km_ref, gq_ref, gkm_ref):
    km = km_ref[...]
    pair = []
    for h in range(HEADS):
        half = slice((h % 2) * HDIM, (h % 2) * HDIM + HDIM)
        pf = fw_ref[hs(h), :].astype(F32)
        g = nn(comb_ref[h // 2][:, half], gct_ref[hs(h), :])
        gs = (pf * (g - jnp.sum(pf * g, axis=0, keepdims=True))).astype(BF16)
        gq_ref[hs(h), :] = tn(km[:, hs(h)], gs).astype(BF16)
        pair.append(nt(gs, qt_ref[hs(h), :]))
        if h % 2:
            gkm_ref[:, (h - 1) * HDIM : (h + 1) * HDIM] = jnp.concatenate(pair, 1)
            pair = []


def lead_back(gct, fw, qt, comb, km):
    return pl.pallas_call(
        lead_back_kernel,
        out_shape=[shape(gct.shape, BF16), shape(km.shape, F32)],
        in_specs=[vspec()] * 5,
        out_specs=[vspec()] * 2,
        compiler_params=params(),
        cost_estimate=cost(3e+08, 600000),
        name="lead_back",
    )(gct, fw, qt, comb, km)


def rear_back_kernel(z_ref, parts_ref, mixn_ref, st_ref, own_ref, eb_ref, vt_ref, kt_ref, qm_ref, gvc_ref,
                     gk_ref, gv_ref, gqm_ref, gc_ref):
    qm = qm_ref[...]
    gc_ref[...] = sum(parts_ref[d].astype(F32) for d in range(parts_ref.shape[0]))
    scale = jnp.exp(own_ref[...] - st_ref[...])
    pair = []
    for h in range(HEADS):
        half = slice((h % 2) * HDIM, (h % 2) * HDIM + HDIM)
        gmix = tn3(z_ref[h], gc_ref[h // 2][:, half]).astype(BF16)
        dot = jnp.sum(gmix.astype(F32) * mixn_ref[h // 2][:, half], axis=1, keepdims=True)
        factor = scale[:, h : h + 1] / st_ref[:, 16 + h : 17 + h]
        pb = eb_ref[hs(h), :].astype(F32) * factor
        gs = (pb * (nn(gmix, vt_ref[hs(h), :]) - dot)).astype(BF16)
        gk_ref[hs(h), :] = tn(qm[:, hs(h)], gs).astype(BF16)
        gv_ref[hs(h), :] = (tn(gmix, pb.astype(BF16)) + gvc_ref[hs(h), :]).astype(BF16)
        pair.append(nt(gs, kt_ref[hs(h), :]))
        if h % 2:
            gqm_ref[:, (h - 1) * HDIM : (h + 1) * HDIM] = jnp.concatenate(pair, 1)
            pair = []


def rear_back(z, parts, mixn, stats, own, eb, vt, kt, qm, gvc, after=()):
    return call(
        rear_back_kernel,
        (z, parts, mixn, stats, own, eb, vt, kt, qm, gvc),
        [vspec()] * 10,
        [shape(vt.shape, BF16), shape(vt.shape, BF16), shape(qm.shape, F32), shape(mixn.shape, F32)],
        [vspec()] * 4,
        "rear_back",
        cost(3e8, 1e6),
        after=after,
    )


def last_kernel(count, segment, me_ref, gq_ref, gk_ref, gv_ref, first_ref, own_ref, *refs):
    pieces = refs[:count]
    out_ref, w_ref, sems = refs[count:]
    me = me_ref[0]
    width = gq_ref.shape[0]

    @pl.when(pl.program_id(0) == 0)
    def _():
        placed(pieces, w_ref, sems, me, True)
        placed(pieces, w_ref, sems, me, False)

    wq, wk, wv = (w_ref[:, i * width : (i + 1) * width] for i in range(3))
    g = SCALE * (nn(wq, gq_ref[...]) + nn(wk, gk_ref[...])) + nn(wv, gv_ref[...])
    own = own_ref[...]
    marks = (SCALE / segment) * (
        nt(own[:, :width].astype(BF16), wq) + nt(own[:, width:].astype(BF16), wk)
    )
    step = out_ref.shape[0]
    token = pl.program_id(0) * step + lax.broadcasted_iota(jnp.int32, (step, own.shape[0]), 0)
    mark = lax.broadcasted_iota(jnp.int32, (step, own.shape[0]), 1) * segment
    pick = ((token >= mark) & (token < mark + segment)).astype(BF16)
    high, low = split(marks)
    spread = nn(pick, high) + nn(pick, low)
    out_ref[...] = (first_ref[...] + g.T + spread).astype(BF16)


def last(me, gq, gk, gv, first, own, pieces, segment):
    width, tokens = gq.shape
    step = 256
    tall = pl.BlockSpec((width, step), lambda i: (0, i))
    row = pl.BlockSpec((step, width), lambda i: (i, 0))
    return pl.pallas_call(
        functools.partial(last_kernel, len(pieces), segment),
        grid=(tokens // step,),
        out_shape=shape((tokens, width), BF16),
        in_specs=[sspec(), tall, tall, tall, row, pl.BlockSpec(own.shape, lambda i: (0, 0))]
        + [aspec()] * len(pieces),
        out_specs=row,
        scratch_shapes=[
            pltpu.VMEM((width, 3 * width), BF16),
            pltpu.SemaphoreType.DMA((len(pieces),)),
        ],
        compiler_params=params(),
        cost_estimate=cost(4e+08, 1.2e+06),
        name="last",
    )(me, gq, gk, gv, first, own, *pieces)


def bits(axis):
    size = lax.axis_size(axis)
    assert size & (size - 1) == 0
    return [1 << i for i in range(size.bit_length() - 1)]


def swap(array, axis, bit):
    return lax.ppermute(array, axis, [(i, i ^ bit) for i in range(lax.axis_size(axis))])


def shift(array, axis, by):
    size = lax.axis_size(axis)
    return lax.ppermute(array, axis, [(i, i + by) for i in range(size) if 0 <= i + by < size])


def spread(pieces, axis, steps):
    for bit in steps:
        pieces = {**pieces, **{k | bit: swap(piece, axis, bit) for k, piece in pieces.items()}}
    return pieces


def far(array, axis):
    return spread({0: array}, axis, bits(axis)[1:])


def near(pieces, axis):
    pieces = spread(pieces, axis, bits(axis)[:1])
    return [pieces[k] for k in range(lax.axis_size(axis))]


def gathered(array, axis):
    return near(far(array, axis), axis)


def tie(*values):
    return lax.optimization_barrier(values)


def rows_out(array, groups=None):
    size = len(groups[0]) if groups else lax.axis_size("seq")
    blocks = array.reshape(size, -1, array.shape[1])
    return lax.all_to_all(blocks, "seq", 0, 0, axis_index_groups=groups)


def rows_in(blocks):
    return jnp.sum(blocks.astype(F32), axis=0)


def copies(array, axis, groups=None):
    size = len(groups[0]) if groups else lax.axis_size(axis)
    blocks = jnp.broadcast_to(array[None], (size, *array.shape))
    return lax.all_to_all(blocks, axis, 0, 0, axis_index_groups=groups)


class Total:
    def __init__(self, pieces, order):
        self.pieces = dict(enumerate(pieces))
        self.order = list(order)
        self.back = [step for step in reversed(order) if step[0] != "swap"]
        self.got = None

    def send(self):
        if self.order:
            kind, what = self.order[0]
            if kind == "swap":
                self.got = {k: swap(p, "fsdp", what) for k, p in self.pieces.items() if k & what}
                self.pieces = {k: p for k, p in self.pieces.items() if not k & what}
                return
            (piece,) = self.pieces.values()
            if kind == "rows":
                self.got = {0: rows_out(piece, what)}
                return
            upper = ((lax.axis_index("seq") & what) != 0).astype(jnp.int32)
            half = piece.shape[0] // 2
            self.pieces = {0: lax.dynamic_slice_in_dim(piece, upper * half, half, 0)}
            sent = lax.dynamic_slice_in_dim(piece, (1 - upper) * half, half, 0)
            self.got = {0: swap(sent, "seq", what)}
        else:
            kind, what = self.back[0]
            if kind == "rows":
                self.got = {0: copies(self.pieces[0], "seq", what)}
            else:
                self.got = {0: swap(self.pieces[0], "seq", what)}

    def take(self):
        if self.order:
            kind, what = self.order.pop(0)
            if kind == "rows":
                self.pieces = {0: rows_in(self.got[0]).astype(BF16)}
            else:
                extra = what if kind == "swap" else 0
                self.pieces = {
                    k: (p.astype(F32) + self.got[k | extra].astype(F32)).astype(BF16)
                    for k, p in self.pieces.items()
                }
        else:
            kind, what = self.back.pop(0)
            mine, other = self.pieces[0], self.got[0]
            if kind == "rows":
                self.pieces = {0: other.reshape(-1, other.shape[2])}
            else:
                upper = (lax.axis_index("seq") & what) != 0
                self.pieces = {
                    0: jnp.where(
                        upper, jnp.concatenate([other, mine], 0), jnp.concatenate([mine, other], 0)
                    )
                }
        self.got = None

    def step(self, *values):
        self.got, values = tie(self.got, values)
        self.take()
        if self.order or self.back:
            self.send()
        return values

    def ready(self, *values):
        self.pieces, values = tie(self.pieces, values)
        return values

    def finish(self):
        while self.got is not None:
            self.step()
        return self.pieces[0]


def orders():
    size = lax.axis_size("seq")
    over = [("swap", bit) for bit in bits("fsdp")]
    parts = size // 4
    groups = [[low + parts * high for high in range(4)] for low in range(parts)]
    near = [("half", bit) for bit in bits("seq") if bit < parts]
    tree = over + [("half", bit) for bit in bits("seq")]
    return over, over + near + [("rows", groups)], over + [("rows", None)], tree


def shards(
    inputs,
    cotangent,
    query_weight,
    key_weight,
    value_weight,
    output_weight,
    up_weight,
    down_weight,
    norm_gain,
    norm_shift,
    final_gain,
    final_shift,
    conv_kernel,
):
    x = inputs[0]
    ct = cotangent[0]
    tokens, width = x.shape
    marks = LANDMARKS // lax.axis_size("seq")
    segment = tokens // marks
    count = lax.axis_size("fsdp")
    rows = width // count
    here = lax.axis_index("fsdp")
    place = lax.axis_index("seq")
    size = lax.axis_size("seq")
    me = jnp.stack([here, place]).astype(jnp.int32)
    over, nested, flat, tree = orders()

    packed, xm = pack(x, (query_weight, key_weight, value_weight), size, marks)
    first_weights = far(packed, "fsdp")
    space = 256 + 2 * EDGE
    taps = jnp.pad(conv_kernel.T, ((0, 4), (EDGE - REACH, space - KERNEL - EDGE + REACH)))
    spat = jnp.pad(conv_kernel[::-1].T, ((0, 4), (EDGE - REACH, space - KERNEL - EDGE + REACH)))
    xm, taps, spat, me = tie(xm, taps, spat, me)
    xm = lax.all_to_all(xm, "seq", 0, 0).reshape(LANDMARKS, width)
    gains = jnp.stack([norm_gain, norm_shift, final_gain, final_shift] * 2)
    gains = gathered(gains, "fsdp")
    first_weights, gains, xm, output_weight = tie(first_weights, gains, xm, output_weight)
    wqkv = near(first_weights, "fsdp")
    wo = far(output_weight, "fsdp")
    wqkv, up_weight = tie(wqkv, up_weight)
    up = far(up_weight, "fsdp")
    source = lax.broadcasted_iota(jnp.int32, (8, width), 1) // rows ^ here
    gains = sum(
        jnp.where(source == k, jnp.concatenate([piece.astype(F32)] * count, 1), 0.0)
        for k, piece in enumerate(gains)
    )

    (xt, xmt, qt, kt, vt, fw, eb, own, msg, qm, km, v_top, v_end) = front(me, x, xm, wqkv, size)
    msg, down_weight = tie(msg, down_weight)
    msgs = lax.all_to_all(msg, "seq", 0, 0)
    down = far(down_weight, "fsdp")
    v_before = shift(v_end, "seq", 1)
    v_after = shift(v_top, "seq", -1)
    a, z, *saved = inverse(qm, km)
    v_before, v_after, z, up, wo = tie(v_before, v_after, z, up, wo)
    up = near(up, "fsdp")
    wo = near(wo, "fsdp")
    convt = conv(vt, v_before, v_after, taps)

    ctxt, hidt, xhat, rstd, act, slope, comb, mixn, stats = mid1(
        me, z, msgs, fw, convt, x, gains, wo, up
    )
    down, act = tie(down, act)
    down = near(down, "fsdp")
    out, second, redt, ge, sums2 = mid2(me, act, slope, xhat, ct, gains, down)
    d_up = grad_up(count, hidt, ge)
    t_up = Total(d_up, tree)
    t_up.send()
    d_down = grad_down(count, me, redt, act, after=d_up)
    second, d_down = t_up.step(second, d_down)
    t_down = Total(d_down, tree)
    t_down.send()
    (second,) = t_up.ready(second)
    first, branch, gct, g_top, g_end, sums1, gc = mid3(
        me, second, ge, xhat, rstd, fw, gains, wo, up, size, after=d_down
    )
    g_before = shift(g_end, "seq", 1)
    g_after = shift(g_top, "seq", -1)
    gc, g_before, g_after = tie(gc, g_before, g_after)
    parts = lax.all_to_all(gc, "seq", 0, 0)
    (gct,) = t_down.step(gct)
    gq, gkm = lead_back(gct, fw, qt, comb, km)
    gct, gq = t_up.step(gct, gq)
    gct, gq = t_up.ready(gct, gq)
    gvc, g_taps = conv_back(vt, v_before, v_after, gct, g_before, g_after, spat)
    d_o = grad_o(count, me, ctxt, branch, sums1, sums2, g_taps)
    t_o = Total(d_o, tree)
    t_o.send()
    gk, gv, gqm, gc = rear_back(z, parts, mixn, stats, own, eb, vt, kt, qm, gvc, after=d_o)
    for t in (t_up, t_o, t_down):
        (gqm,) = t.step(gqm)
        (gqm,) = t.ready(gqm)
    gqm, gkm = inverse_back(me, qm, km, a, mixn, gc, saved, gqm, gkm, size)
    for t in (t_up, t_down):
        (gqm,) = t.step(gqm)
        (gqm,) = t.ready(gqm)
    d_qkv = grad_qkv(count, xt, xmt, gq, gk, gv, gqm, gkm)
    t_qkv = Total(d_qkv, flat)
    t_qkv.send()
    for _ in over[:-1]:
        gqm, gkm = t_qkv.step(gqm, gkm)
    (gqm,) = t_qkv.ready(gqm)
    for t in (t_up, t_down, t_o):
        (gqm,) = t.step(gqm)
        (gqm,) = t.ready(gqm)
    landed = rows_out(jnp.concatenate([gqm, gkm], 1).astype(BF16))
    for t in (t_up, t_down, t_o):
        (landed,) = t.step(landed)
        (landed,) = t.ready(landed)
    landed = rows_in(landed)
    grad_x = last(me, gq, gk, gv, first, landed, wqkv, segment)
    (grad_x,) = t_qkv.step(grad_x)
    for t in (t_up, t_down, t_o) * 2:
        if t.got is not None:
            (grad_x,) = t.step(grad_x)
    g_up = t_up.finish().astype(F32)
    g_down = t_down.finish().T.astype(F32)
    (grad_x, g_up, g_down) = t_qkv.step(grad_x, g_up, g_down)
    g_o = t_o.finish().astype(F32)
    qkv = t_qkv.finish().astype(F32)

    tap = g_o[:KERNEL, width + 4 : width + 4 + HEADS]
    tap = jnp.where(here == 0, tap, 0.0)
    for _, bit in over:
        tap = tap + swap(tap, "fsdp", bit)
    return (
        out[None],
        grad_x[None],
        SCALE * qkv[:, :width],
        SCALE * qkv[:, width : 2 * width],
        qkv[:, 2 * width :],
        g_o[:, :width],
        g_up,
        g_down,
        g_o[:, width],
        g_o[:, width + 1],
        g_o[:, width + 2],
        g_o[:, width + 3],
        tap,
    )


def solution(mesh):
    tokens = P("fsdp", "seq", None)
    matrix = P("fsdp", None)
    row = P("fsdp")
    in_specs = (tokens,) * 2 + (matrix,) * 6 + (row,) * 4 + (P(),)
    out_specs = (tokens,) * 2 + (matrix,) * 6 + (row,) * 4 + (P(),)
    return jax.shard_map(shards, mesh=mesh, in_specs=in_specs, out_specs=out_specs, check_vma=False)
```

time: 542 us -> 443 us (0.82)
  waiting for transfers between devices: 219 us -> 118 us
  matrix products: 42.1 us -> 0 us
  Pallas kernels: 158 us -> 183 us
  starting transfers between devices: 68 us -> 88.7 us
  other arithmetic: 18.4 us -> 26.8 us
  blocking collectives: 5.46 us -> 0 us
    ppermute x65 -> x47, waiting for transfers between devices: 219 us -> 107 us  [swap(): lax.ppermute(array, axis, [(i, i ^ bit) for i in range(lax.axis_size(axis...]
    dot_general x24 -> x0, matrix products: 42.1 us -> none  [the longest x12 32.2 us: nn(): return jnp.dot(a, b, preferred_element_type=F32)]
    all_to_all x0 -> x6, starting transfers between devices: none -> 34.5 us  [the longest x2 8.27 us: rows_out(): return lax.all_to_all(blocks, 'seq', 0, 0, axis_index_groups=groups)]
    pallas_call x10 -> x12, Pallas kernels: 118 us -> 142 us  [call(): pl.pallas_call(body, grid=grid, out_shape=out_shape, in_specs=list(in_spe...]
    ppermute x65 -> x47, starting transfers between devices: 56.6 us -> 42.8 us  [swap(): lax.ppermute(array, axis, [(i, i ^ bit) for i in range(lax.axis_size(axis...]
    convert_element_type x27 -> x24, other arithmetic: 11.9 us -> 18.9 us  [the longest x20 14.6 us: take(): (p.astype(F32) + self.got[k | extra].astype(F32)).astype(BF16)]
    all_to_all x0 -> x6, waiting for transfers between devices: none -> 5.85 us  [the longest x2 5.83 us: rows_out(): return lax.all_to_all(blocks, 'seq', 0, 0, axis_index_groups=groups)]
    all_gather x1 -> x0, blocking collectives: 5.46 us -> none  [shards(): gains = lax.all_gather(gains, 'fsdp', axis=1, tiled=True).astype(F32)]
  transfers between devices with their start and end apart: 69 -> 57, of which waited for: 35 -> 21; matrix products, arithmetic and copies ran while one was open for 12% -> 8% of each run, Pallas kernels for 22% -> 32%
where the time goes in v2:
time: 443 us; the launch traced here: 434 us
  Pallas kernels  183 us (41%)
  waiting for transfers between devices  118 us (27%)
  starting transfers between devices  88.7 us (20%)
  other arithmetic  26.8 us (6%)
  local copies, waits for them, and re-layouts  16.1 us (4%)
    pallas_call x12, Pallas kernels, call(): pl.pallas_call(body, grid=grid, out_shape=out_shape, in_specs=list(in_spe...  142 us
    ppermute x47, waiting for transfers between devices, swap(): lax.ppermute(array, axis, [(i, i ^ bit) for i in range(lax.axis_size(axis...  107 us
    ppermute x47, starting transfers between devices, swap(): lax.ppermute(array, axis, [(i, i ^ bit) for i in range(lax.axis_size(axis...  42.8 us
    pallas_call x1, Pallas kernels, front(): pl.pallas_call(functools.partial(front_kernel, len(pieces)), out_shape=[f...  16.5 us
    convert_element_type x20, other arithmetic, take(): (p.astype(F32) + self.got[k | extra].astype(F32)).astype(BF16)  14.6 us
    pallas_call x1, Pallas kernels, last(): pl.pallas_call(functools.partial(last_kernel, len(pieces), segment), grid...  13.7 us
    ppermute x4, starting transfers between devices, shift(): lax.ppermute(array, axis, [(i, i + by) for i in range(size) if 0 <= i + b...  11.4 us
  transfers between devices with their start and end apart: 57, of which 21 were waited for; matrix products, arithmetic and copies ran while one was open for 8% of the time, Pallas kernels for 32%

profile of v2, /device:TPU:0, one launch (start us, length us, event | category | flops | bytes accessed | tf_op | source)
XLA Modules:
  0.0 434.2 jit_solution(9541636509496076509)
XLA Ops:
  8.8 5.8 %all-to-all-start = ((f32[8,8,768]{2,1,0:T(8,128)}), f32[8,8,768]{2,1,0:T(8,128)S(1)}, u32[]{:S(2)}, u32[]{:S(2)}) async-start(f32[8,8,768]{2,1,0:T(8,128)} %get-tuple-element.203), calls=%async_computation | async-start | bytes 393216 | tf_op jit(solution)/shard_map/all_to_all | solution.py:1111
  15.3 11.4 %collective-permute-done.2 = bf16[8,192]{1,0:T(8,128)(2,1)S(1)} collective-permute-done((bf16[8,192]{1,0:T(8,128)(2,1)S(1)}, bf16[8,192]{1,0:T(8,128)(2,1)S(1)}, u32[]{:S(2)}, u32[]{:S(2)}) %collective-permute-start.2) | collective-permute-done | bytes 3104 | tf_op jit(solution)/shard_map/ppermute | solution.py:948
  33.4 16.5 %front.1 = (bf16[768,1024]{1,0:T(8,128)(2,1)}, bf16[768,64]{1,0:T(8,128)(2,1)}, bf16[768,1024]{1,0:T(8,128)(2,1)}, bf16[768,1024]{1,0:T(8,128)(2,1)}, bf16[768,1...) custom-call(s32[2]{0:T(128)} %pad_add_fusion.me_ref.refs_0_, ...), custom_call_target="tpu_custom_call" | custom-call | flops 450000000 | bytes 1600000 | tf_op jit(solution)/shard_map/front/pallas_call | solution.py:232
  50.0 6.0 %all-to-all-start.1 = ((bf16[8,7,64,128]{3,2,1,0:T(8,128)(2,1)}), bf16[8,7,64,128]{3,2,1,0:T(8,128)(2,1)}, u32[]{:S(2)}, u32[]{:S(2)}) async-start(bf16[8,7,64,128]{3,2,1,0:T(8,128)(2,1)} %get-tuple-element.221), calls=%async_computation.1 | async-start | bytes 1835008 | tf_op jit(solution)/shard_map/all_to_all | solution.py:1127
  62.5 11.8 %inverse.1 = (f32[12,64,64]{2,1,0:T(8,128)}, f32[12,64,64]{2,1,0:T(8,128)}, f32[6,12,64,64]{3,2,1,0:T(8,128)}, f32[6,12,64,64]{3,2,1,0:T(8,128)}, f32[6,12,64,64]{3,2,1,0:T(8,128)}, /*index=5*/f32[6,12,64,64]{3,2,1,0:T(8,128)}) custom-call(bf16[64,768]{1,0:T(8,128)(2,1)} %get-tuple-element.215.refs_0_.refs_8_.refs_1_, ...), custom_call_target="tpu_custom_call" | custom-call | flops 100000000 | bytes 1000000 | tf_op jit(solution)/shard_map/inverse/pallas_call | solution.py:96
  77.3 4.2 conv.1.refs_4_
  83.4 22.3 %mid_one.1 = (bf16[768,1024]{1,0:T(8,128)(2,1)}, bf16[768,1024]{1,0:T(8,128)(2,1)}, f32[1024,768]{1,0:T(8,128)}, f32[1024,128]{1,0:T(8,128)}, bf16[1024,3072]{1,...) custom-call(s32[2]{0:T(128)} %pad_add_fusion.me_ref.refs_0_, ...), custom_call_target="tpu_custom_call" | custom-call | flops 2000000000 | bytes 3000000 | tf_op jit(solution)/shard_map/mid_one/pallas_call | solution.py:96
  111.6 23.2 %mid_two.1 = (bf16[1024,768]{1,0:T(8,128)(2,1)}, f32[1024,768]{1,0:T(8,128)}, bf16[768,1024]{1,0:T(8,128)(2,1)}, bf16[1024,3072]{1,0:T(8,128)(2,1)}, f32[8,768]{1,0:T(8,128)}) custom-call(s32[2]{0:T(128)} %pad_add_fusion.me_ref.refs_0_, bf16[1024,3072]{1,0:T(8,128)(2,1)} %get-tuple-element.236.refs_1_.refs_2_, ...), custom_call_target="tpu_custom_call" | custom-call | flops 2000000000 | bytes 3000000 | tf_op jit(solution)/shard_map/mid_two/pallas_call | solution.py:96
  134.8 8.9 %grad_up.1 = (bf16[192,3072]{1,0:T(8,128)(2,1)}, bf16[192,3072]{1,0:T(8,128)(2,1)}, bf16[192,3072]{1,0:T(8,128)(2,1)}, bf16[192,3072]{1,0:T(8,128)(2,1)}) custom-call(bf16[768,1024]{1,0:T(8,128)(2,1)} %get-tuple-element.244.refs_0_, bf16[1024,3072]{1,0:T(8,128)(2,1)} %get-tuple-element.245.refs_1_.refs_2_), custom_call_target="tpu_custom_call" | custom-call | flops 500000000 | bytes 1000000 | tf_op jit(solution)/shard_map/grad_up/pallas_call | solution.py:96
  144.3 9.5 %grad_down.1 = (bf16[768,768]{1,0:T(8,128)(2,1)}, bf16[768,768]{1,0:T(8,128)(2,1)}, bf16[768,768]{1,0:T(8,128)(2,1)}, bf16[768,768]{1,0:T(8,128)(2,1)}) custom-call(s32[2]{0:T(128)} %pad_add_fusion.me_ref.refs_0_, bf16[768,1024]{1,0:T(8,128)(2,1)} %get-tuple-element.250.refs_1_, bf16[1024,3072]{1,0:T(8,128)(2,1)} %get-tuple-element.236.refs_1_.refs_2_, ...), custom_call_target="tpu_custom_call" | custom-call | flops 500000000 | bytes 1000000 | tf_op jit(solution)/shard_map/grad_down/pallas_call | solution.py:96
  157.2 19.5 %mid_three.1 = (f32[1024,768]{1,0:T(8,128)}, bf16[1024,768]{1,0:T(8,128)(2,1)}, bf16[768,1024]{1,0:T(8,128)(2,1)}, bf16[32,768]{1,0:T(8,128)(2,1)}, bf16[32,768]...) custom-call(s32[2]{0:T(128)} %pad_add_fusion.me_ref.refs_0_, ...), custom_call_target="tpu_custom_call" | custom-call | flops 2000000000 | bytes 3000000 | tf_op jit(solution)/shard_map/mid_three/pallas_call | solution.py:96
  176.7 4.5 %collective-permute-start.22 = (bf16[32,768]{1,0:T(8,128)(2,1)}, bf16[32,768]{1,0:T(8,128)(2,1)S(1)}, u32[]{:S(2)}, u32[]{:S(2)}) collective-permute-start(bf16[32,768]{1,0:T(8,128)(2,1)} %get-tuple-element.276), channel_id=1, source_target_pairs={{0,4},{4,8},{8,12},{12,16},{16,20},{20,24},{24,28},{1,5},{5,9},{9,... | collective-permute-start | bytes 147464 | tf_op jit(solution)/shard_map/ppermute | solution.py:953
  183.3 4.5 %collective-permute-done.23.refs_5_ = bf16[32,768]{1,0:T(8,128)(2,1)S(1)} collective-permute-done((bf16[32,768]{1,0:T(8,128)(2,1)}, bf16[32,768]{1,0:T(8,128)(2,1)S(1)}, u32[]{:S(2)}, u32[]{:S(2)}) %collective-permute-start.23) | collective-permute-done | bytes 49184 | tf_op jit(solution)/shard_map/ppermute | solution.py:953
  187.8 7.8 %all-to-all-start.2 = ((bf16[8,6,64,128]{3,2,1,0:T(8,128)(2,1)}), bf16[8,6,64,128]{3,2,1,0:T(8,128)(2,1)S(1)}, u32[]{:S(2)}, u32[]{:S(2)}) async-start(bf16[8,6,64,128]{3,2,1,0:T(8,128)(2,1)} %get-tuple-element.278), calls=%async_computation.2 | async-start | bytes 1572864 | tf_op jit(solution)/shard_map/all_to_all | solution.py:1157
  195.7 6.5 %lead_back.1 = (bf16[768,1024]{1,0:T(8,128)(2,1)}, f32[64,768]{1,0:T(8,128)}) custom-call(bf16[768,1024]{1,0:T(8,128)(2,1)} %get-tuple-element.284.gct_ref.refs_3_, bf16[768,1024]{1,0:T(8,128)(2,1)} %get-tuple-element.222.refs_3_.refs_5_.fw_ref, bf16[768,1024]{1,0:T(8,128)(2,1)} %get-tuple-element.268.qt_ref, ...), custom_call_target="tpu_custom_call" | custom-call | flops 300000000 | bytes 600000 | tf_op jit(solution)/shard_map/lead_back/pallas_call | solution.py:848
  206.8 7.5 %conv_back.1 = (f32[768,1024]{1,0:T(8,128)}, f32[16,128]{1,0:T(8,128)}) custom-call(bf16[768,1024]{1,0:T(8,128)(2,1)} %get-tuple-element.223.vt_ref.refs_0_.refs_6_, bf16[32,768]{1,0:T(8,128)(2,1)} %copy-done.27, bf16[32,768]{1,0:T(8,128)(2,1)} %copy-done.28, bf16[768,1024]{1,0:T(8,128)(2,1)} %get-tuple-element.284.gct_ref.refs_3_, ...), custom_call_target="tpu_custom_call" | custom-call | flops 400000000 | bytes 1000000 | tf_op jit(solution)/shard_map/conv_back/pallas_call | solution.py:96
  214.3 4.5 %grad_o.1 = (bf16[192,896]{1,0:T(8,128)(2,1)}, bf16[192,896]{1,0:T(8,128)(2,1)}, bf16[192,896]{1,0:T(8,128)(2,1)}, bf16[192,896]{1,0:T(8,128)(2,1)}) custom-call(s32[2]{0:T(128)} %pad_add_fusion.me_ref.refs_0_, bf16[768,1024]{1,0:T(8,128)(2,1)} %get-tuple-element.289.refs_1_, bf16[1024,768]{1,0:T(8,128)(2,1)} %get-tuple-element.290.refs_2_, ...), custom_call_target="tpu_custom_call" | custom-call | flops 200000000 | bytes 1000000 | tf_op jit(solution)/shard_map/grad_o/pallas_call | solution.py:96
  222.9 10.2 %rear_back.1 = (bf16[768,1024]{1,0:T(8,128)(2,1)}, bf16[768,1024]{1,0:T(8,128)(2,1)}, f32[64,768]{1,0:T(8,128)}, f32[6,64,128]{2,1,0:T(8,128)}) custom-call(f32[12,64,64]{2,1,0:T(8,128)} %get-tuple-element.220.refs_1_.refs_0_, bf16[8,6,64,128]{3,2,1,0:T(8,128)(2,1)} %copy-done.10, f32[6,64,128]{2,1,0:T(8,128)} %get-tuple-element.279.refs_2_.refs_4_, ...), custom_call_target="tpu_custom_call" | custom-call | flops 300000000 | bytes 1000000 | tf_op jit(solution)/shard_map/rear_back/pallas_call | solution.py:96
  237.0 11.8 %collective-permute-done.24 = bf16[768,768]{1,0:T(8,128)(2,1)S(1)} collective-permute-done((bf16[768,768]{1,0:T(8,128)(2,1)}, bf16[768,768]{1,0:T(8,128)(2,1)S(1)}, u32[]{:S(2)}, u32[]{:S(2)}) %collective-permute-start.24) | collective-permute-done | bytes 1179680 | tf_op jit(solution)/shard_map/ppermute | solution.py:948
  250.7 12.2 %inverse_back.1 = (f32[64,768]{1,0:T(8,128)}, f32[64,768]{1,0:T(8,128)}) custom-call(s32[2]{0:T(128)} %pad_add_fusion.me_ref.refs_0_, bf16[64,768]{1,0:T(8,128)(2,1)} %get-tuple-element.215.refs_0_.refs_8_.refs_1_, bf16[64,768]{1,0:T(8,128)(2,1)} %get-tuple-element.216.refs_1_.km_ref.refs_2_, f32[12,64,64]{2,1,0:T(8,128)} %get-tuple-element.314.refs_3_, ...), custom_call_target="tpu_custom_call" | custom-call | flops 200000000 | bytes 2000000 | tf_op jit(solution)/shard_map/inverse_back/pallas_call | solution.py:96
  263.7 13.6 %collective-permute-done.28 = bf16[384,768]{1,0:T(8,128)(2,1)S(1)} collective-permute-done((bf16[384,768]{1,0:T(8,128)(2,1)S(1)}, bf16[384,768]{1,0:T(8,128)(2,1)S(1)}, u32[]{:S(2)}, u32[]{:S(2)}) %collective-permute-start.28) | collective-permute-done | bytes 589856 | tf_op jit(solution)/shard_map/ppermute | solution.py:948
  278.2 9.1 %grad_qkv.1 = (bf16[192,2304]{1,0:T(8,128)(2,1)}, bf16[192,2304]{1,0:T(8,128)(2,1)}, bf16[192,2304]{1,0:T(8,128)(2,1)}, bf16[192,2304]{1,0:T(8,128)(2,1)}) custom-call(bf16[768,1024]{1,0:T(8,128)(2,1)} %get-tuple-element.242.refs_0_, bf16[768,64]{1,0:T(8,128)(2,1)} %get-tuple-element.243.refs_1_, bf16[768,1024]{1,0:T(8,128)(2,1)} %get-tuple-element.274.refs_2_.gq_ref, ...), custom_call_target="tpu_custom_call" | custom-call | flops 200000000 | bytes 1000000 | tf_op jit(solution)/shard_map/grad_qkv/pallas_call | solution.py:96
  294.5 4.7 %collective-permute-done.35 = bf16[24,3072]{1,0:T(8,128)(2,1)S(1)} collective-permute-done((bf16[24,3072]{1,0:T(8,128)(2,1)}, bf16[24,3072]{1,0:T(8,128)(2,1)S(1)}, u32[]{:S(2)}, u32[]{:S(2)}) %collective-permute-start.35) | collective-permute-done | bytes 147488 | tf_op jit(solution)/shard_map/ppermute | solution.py:948
  305.0 4.0 all-to-all-start.3
  314.3 5.8 %all-to-all-done.3 = bf16[8,8,1536]{2,1,0:T(8,128)(2,1)} async-done(((bf16[8,8,1536]{2,1,0:T(8,128)(2,1)}), bf16[8,8,1536]{2,1,0:T(8,128)(2,1)}, u32[]{:S(2)}, u32[]{:S(2)}) %all-to-all-start.3) | async-done | bytes 196640 | tf_op jit(solution)/shard_map/all_to_all | solution.py:982
  328.2 13.7 %last.1 = bf16[1024,768]{1,0:T(8,128)(2,1)} custom-call(s32[2]{0:T(128)} %pad_add_fusion.me_ref.refs_0_, bf16[768,1024]{1,0:T(8,128)(2,1)} %get-tuple-element.274.refs_2_.gq_ref, bf16[768,1024]{1,0:T(8,128)(2,1)} %get-tuple-element.298.refs_3_.gk_ref, bf16[768,1024]{1,0:T(8,128)(2,1)} %get-tuple-element.299.refs_4_.gv_ref, ...), custom_call_target="tpu_custom_call" | custom-call | flops 400000000 | bytes 1200000 | tf_op jit(solution)/shard_map/last/pallas_call | solution.py:924
  344.5 4.3 all-to-all-start.4
  352.2 18.6 %collective-permute-done.39 = bf16[48,896]{1,0:T(8,128)(2,1)S(1)} collective-permute-done((bf16[48,896]{1,0:T(8,128)(2,1)S(1)}, bf16[48,896]{1,0:T(8,128)(2,1)S(1)}, u32[]{:S(2)}, u32[]{:S(2)}) %collective-permute-start.39) | collective-permute-done | bytes 86048 | tf_op jit(solution)/shard_map/ppermute | solution.py:948
  384.2 6.6 %all-to-all-start.5 = ((bf16[8,24,2304]{2,1,0:T(8,128)(2,1)}), bf16[8,24,2304]{2,1,0:T(8,128)(2,1)S(1)}, u32[]{:S(2)}, u32[]{:S(2)}) async-start(bf16[8,24,2304]{2,1,0:T(8,128)(2,1)} %broadcast_in_dim.26), calls=%async_computation.5 | async-start | bytes 1769472 | tf_op jit(solution)/shard_map/all_to_all | solution.py:992
  393.8 19.3 %collective-permute-done.46 = bf16[24,896]{1,0:T(8,128)(2,1)S(1)} collective-permute-done((bf16[24,896]{1,0:T(8,128)(2,1)S(1)}, bf16[24,896]{1,0:T(8,128)(2,1)S(1)}, u32[]{:S(2)}, u32[]{:S(2)}) %collective-permute-start.46) | collective-permute-done | bytes 43040 | tf_op jit(solution)/shard_map/ppermute | solution.py:948
  413.2 4.5 %collective-permute-done.47 = bf16[48,896]{1,0:T(8,128)(2,1)S(1)} collective-permute-done((bf16[48,896]{1,0:T(8,128)(2,1)S(1)}, bf16[48,896]{1,0:T(8,128)(2,1)S(1)}, u32[]{:S(2)}, u32[]{:S(2)}) %collective-permute-start.47) | collective-permute-done | bytes 86048 | tf_op jit(solution)/shard_map/ppermute | solution.py:948
  419.0 4.3 collective-permute-done.48
  (241 shorter events, 115.0 us)
Async XLA Ops:
  3.7 24.2 %collective-permute-start = (bf16[192,2304]{1,0:T(8,128)(2,1)}, bf16[192,2304]{1,0:T(8,128)(2,1)S(1)}, u32[]{:S(2)}, u32[]{:S(2)}) collective-permute-start(bf16[192,2304]{1,0:T(8,128)(2,1)} %get-tuple-element.207.refs_0_), channel_id=1, source_target_pairs={{0,2},{1,3},{2,0},{3,1},{4,6},{5,7},{6,4},{7,5},{8,10},{9,11},{10,... | collective-permute-start | bytes 2654216 | tf_op jit(solution)/shard_map/ppermute | solution.py:948
  8.8 19.1 %all-to-all-start = ((f32[8,8,768]{2,1,0:T(8,128)}), f32[8,8,768]{2,1,0:T(8,128)S(1)}, u32[]{:S(2)}, u32[]{:S(2)}) async-start(f32[8,8,768]{2,1,0:T(8,128)} %get-tuple-element.203), calls=%async_computation | async-start | bytes 393216 | tf_op jit(solution)/shard_map/all_to_all | solution.py:1111
  31.7 42.7 %collective-permute-start.9 = (bf16[192,3072]{1,0:T(8,128)(2,1)S(1)}, bf16[192,3072]{1,0:T(8,128)(2,1)S(1)}, u32[]{:S(2)}, u32[]{:S(2)}) collective-permute-start(bf16[192,3072]{1,0:T(8,128)(2,1)S(1)} %copy-done), channel_id=1, source_target_pairs={{0,2},{1,3},{2,0},{3,1},{4,6},{5,7},{6,4},{7,5},{8,10},{9,11},{10,... | collective-permute-start | bytes 3538952 | tf_op jit(solution)/shard_map/ppermute | solution.py:948
  50.0 32.3 %all-to-all-start.1 = ((bf16[8,7,64,128]{3,2,1,0:T(8,128)(2,1)}), bf16[8,7,64,128]{3,2,1,0:T(8,128)(2,1)}, u32[]{:S(2)}, u32[]{:S(2)}) async-start(bf16[8,7,64,128]{3,2,1,0:T(8,128)(2,1)} %get-tuple-element.221), calls=%async_computation.1 | async-start | bytes 1835008 | tf_op jit(solution)/shard_map/all_to_all | solution.py:1127
  55.9 18.4 %collective-permute-start.10 = (bf16[192,768]{1,0:T(8,128)(2,1)S(1)}, bf16[192,768]{1,0:T(8,128)(2,1)S(1)}, u32[]{:S(2)}, u32[]{:S(2)}) collective-permute-start(bf16[192,768]{1,0:T(8,128)(2,1)S(1)} %copy-done.16), channel_id=1, source_target_pairs={{0,2},{1,3},{2,0},{3,1},{4,6},{5,7},{6,4},{7,5},{8,10},{9,11},{10,... | collective-permute-start | bytes 884744 | tf_op jit(solution)/shard_map/ppermute | solution.py:948
  56.9 17.4 %collective-permute-start.7 = (bf16[32,768]{1,0:T(8,128)(2,1)S(1)}, bf16[32,768]{1,0:T(8,128)(2,1)S(1)}, u32[]{:S(2)}, u32[]{:S(2)}) collective-permute-start(bf16[32,768]{1,0:T(8,128)(2,1)S(1)} %copy-done.34), channel_id=1, source_target_pairs={{0,4},{4,8},{8,12},{12,16},{16,20},{20,24},{24,28},{1,5},{5,9},{9,... | collective-permute-start | bytes 147464 | tf_op jit(solution)/shard_map/ppermute | solution.py:953
  60.8 13.6 %collective-permute-start.8 = (bf16[32,768]{1,0:T(8,128)(2,1)S(1)}, bf16[32,768]{1,0:T(8,128)(2,1)S(1)}, u32[]{:S(2)}, u32[]{:S(2)}) collective-permute-start(bf16[32,768]{1,0:T(8,128)(2,1)S(1)} %copy-done.33), channel_id=1, source_target_pairs={{4,0},{8,4},{12,8},{16,12},{20,16},{24,20},{28,24},{5,1},{9,5},{13... | collective-permute-start | bytes 147464 | tf_op jit(solution)/shard_map/ppermute | solution.py:953
  75.0 30.7 %collective-permute-start.6 = (bf16[768,768]{1,0:T(8,128)(2,1)}, bf16[768,768]{1,0:T(8,128)(2,1)}, u32[]{:S(2)}, u32[]{:S(2)}) collective-permute-start(bf16[768,768]{1,0:T(8,128)(2,1)} %refs_6_), channel_id=1, source_target_pairs={{0,2},{1,3},{2,0},{3,1},{4,6},{5,7},{6,4},{7,5},{8,10},{9,11},{10,... | collective-permute-start | bytes 3538952 | tf_op jit(solution)/shard_map/ppermute | solution.py:948
  153.8 41.8 %collective-permute-start.20 = (bf16[768,768]{1,0:T(8,128)(2,1)}, bf16[768,768]{1,0:T(8,128)(2,1)}, u32[]{:S(2)}, u32[]{:S(2)}) collective-permute-start(bf16[768,768]{1,0:T(8,128)(2,1)} %get-tuple-element.260.refs_16_), channel_id=1, source_target_pairs={{0,1},{1,0},{2,3},{3,2},{4,5},{5,4},{6,7},{7,6},{8,9},{9,8},{10,11... | collective-permute-start | bytes 3538952 | tf_op jit(solution)/shard_map/ppermute | solution.py:948
  154.0 41.6 %collective-permute-start.21 = (bf16[768,768]{1,0:T(8,128)(2,1)}, bf16[768,768]{1,0:T(8,128)(2,1)S(1)}, u32[]{:S(2)}, u32[]{:S(2)}) collective-permute-start(bf16[768,768]{1,0:T(8,128)(2,1)} %get-tuple-element.261.refs_18_), channel_id=1, source_target_pairs={{0,1},{1,0},{2,3},{3,2},{4,5},{5,4},{6,7},{7,6},{8,9},{9,8},{10,11... | collective-permute-start | bytes 3538952 | tf_op jit(solution)/shard_map/ppermute | solution.py:948
  155.8 46.4 %collective-permute-start.19 = (bf16[192,3072]{1,0:T(8,128)(2,1)}, bf16[192,3072]{1,0:T(8,128)(2,1)}, u32[]{:S(2)}, u32[]{:S(2)}) collective-permute-start(bf16[192,3072]{1,0:T(8,128)(2,1)} %add_convert_fusion.4), channel_id=1, source_target_pairs={{0,2},{1,3},{2,0},{3,1},{4,6},{5,7},{6,4},{7,5},{8,10},{9,11},{10,... | collective-permute-start | bytes 3538952 | tf_op jit(solution)/shard_map/ppermute | solution.py:948
  187.8 34.2 %all-to-all-start.2 = ((bf16[8,6,64,128]{3,2,1,0:T(8,128)(2,1)}), bf16[8,6,64,128]{3,2,1,0:T(8,128)(2,1)S(1)}, u32[]{:S(2)}, u32[]{:S(2)}) async-start(bf16[8,6,64,128]{3,2,1,0:T(8,128)(2,1)} %get-tuple-element.278), calls=%async_computation.2 | async-start | bytes 1572864 | tf_op jit(solution)/shard_map/all_to_all | solution.py:1157
  204.8 28.2 %collective-permute-start.27 = (bf16[96,3072]{1,0:T(8,128)(2,1)}, bf16[96,3072]{1,0:T(8,128)(2,1)S(1)}, u32[]{:S(2)}, u32[]{:S(2)}) collective-permute-start(bf16[96,3072]{1,0:T(8,128)(2,1)} %get-tuple-element.422), channel_id=1, source_target_pairs={{0,4},{4,0},{8,12},{12,8},{16,20},{20,16},{24,28},{28,24},{1,5},{5... | collective-permute-start | bytes 1769480 | tf_op jit(solution)/shard_map/ppermute | solution.py:948
  218.8 14.5 %collective-permute-start.25 = (bf16[192,896]{1,0:T(8,128)(2,1)}, bf16[192,896]{1,0:T(8,128)(2,1)}, u32[]{:S(2)}, u32[]{:S(2)}) collective-permute-start(bf16[192,896]{1,0:T(8,128)(2,1)} %get-tuple-element.295.refs_11_), channel_id=1, source_target_pairs={{0,1},{1,0},{2,3},{3,2},{4,5},{5,4},{6,7},{7,6},{8,9},{9,8},{10,11... | collective-permute-start | bytes 1032200 | tf_op jit(solution)/shard_map/ppermute | solution.py:948
  218.8 14.5 %collective-permute-start.26 = (bf16[192,896]{1,0:T(8,128)(2,1)}, bf16[192,896]{1,0:T(8,128)(2,1)S(1)}, u32[]{:S(2)}, u32[]{:S(2)}) collective-permute-start(bf16[192,896]{1,0:T(8,128)(2,1)} %get-tuple-element.297.refs_13_), channel_id=1, source_target_pairs={{0,1},{1,0},{2,3},{3,2},{4,5},{5,4},{6,7},{7,6},{8,9},{9,8},{10,11... | collective-permute-start | bytes 1032200 | tf_op jit(solution)/shard_map/ppermute | solution.py:948
  220.7 28.1 %collective-permute-start.24 = (bf16[768,768]{1,0:T(8,128)(2,1)}, bf16[768,768]{1,0:T(8,128)(2,1)S(1)}, u32[]{:S(2)}, u32[]{:S(2)}) collective-permute-start(bf16[768,768]{1,0:T(8,128)(2,1)} %add_convert_fusion.1), channel_id=1, source_target_pairs={{0,2},{1,3},{2,0},{3,1},{4,6},{5,7},{6,4},{7,5},{8,10},{9,11},{10,... | collective-permute-start | bytes 3538952 | tf_op jit(solution)/shard_map/ppermute | solution.py:948
  235.2 27.6 %collective-permute-start.29 = (bf16[48,3072]{1,0:T(8,128)(2,1)S(1)}, bf16[48,3072]{1,0:T(8,128)(2,1)S(1)}, u32[]{:S(2)}, u32[]{:S(2)}) collective-permute-start(bf16[48,3072]{1,0:T(8,128)(2,1)S(1)} %get-tuple-element.426), channel_id=1, source_target_pairs={{0,8},{4,12},{8,0},{12,4},{16,24},{20,28},{24,16},{28,20},{1,9},{5... | collective-permute-start | bytes 884744 | tf_op jit(solution)/shard_map/ppermute | solution.py:948
  262.8 14.4 %collective-permute-start.28 = (bf16[384,768]{1,0:T(8,128)(2,1)S(1)}, bf16[384,768]{1,0:T(8,128)(2,1)S(1)}, u32[]{:S(2)}, u32[]{:S(2)}) collective-permute-start(bf16[384,768]{1,0:T(8,128)(2,1)S(1)} %get-tuple-element.421), channel_id=1, source_target_pairs={{0,4},{4,0},{8,12},{12,8},{16,20},{20,16},{24,28},{28,24},{1,5},{5... | collective-permute-start | bytes 1769480 | tf_op jit(solution)/shard_map/ppermute | solution.py:948
  287.9 15.5 %collective-permute-start.33 = (bf16[192,896]{1,0:T(8,128)(2,1)S(1)}, bf16[192,896]{1,0:T(8,128)(2,1)S(1)}, u32[]{:S(2)}, u32[]{:S(2)}) collective-permute-start(bf16[192,896]{1,0:T(8,128)(2,1)S(1)} %add_convert_fusion.12), channel_id=1, source_target_pairs={{0,2},{1,3},{2,0},{3,1},{4,6},{5,7},{6,4},{7,5},{8,10},{9,11},{10,... | collective-permute-start | bytes 1032200 | tf_op jit(solution)/shard_map/ppermute | solution.py:948
  299.9 14.5 %collective-permute-start.38 = (bf16[24,3072]{1,0:T(8,128)(2,1)}, bf16[24,3072]{1,0:T(8,128)(2,1)}, u32[]{:S(2)}, u32[]{:S(2)}) collective-permute-start(bf16[24,3072]{1,0:T(8,128)(2,1)} %add_convert_fusion.18), channel_id=1, source_target_pairs={{0,16},{4,20},{8,24},{12,28},{16,0},{20,4},{24,8},{28,12},{1,17},{... | collective-permute-start | bytes 442376 | tf_op jit(solution)/shard_map/ppermute | solution.py:948
  305.0 15.1 %all-to-all-start.3 = ((bf16[8,8,1536]{2,1,0:T(8,128)(2,1)}), bf16[8,8,1536]{2,1,0:T(8,128)(2,1)}, u32[]{:S(2)}, u32[]{:S(2)}) async-start(bf16[8,8,1536]{2,1,0:T(8,128)(2,1)} %pad_maximum_fusion), calls=%async_computation.3 | async-start | bytes 393216 | tf_op jit(solution)/shard_map/all_to_all | solution.py:982
  309.0 13.0 %collective-permute-start.37 = (bf16[96,768]{1,0:T(8,128)(2,1)}, bf16[96,768]{1,0:T(8,128)(2,1)}, u32[]{:S(2)}, u32[]{:S(2)}) collective-permute-start(bf16[96,768]{1,0:T(8,128)(2,1)} %get-tuple-element.430), channel_id=1, source_target_pairs={{0,16},{4,20},{8,24},{12,28},{16,0},{20,4},{24,8},{28,12},{1,17},{... | collective-permute-start | bytes 442376 | tf_op jit(solution)/shard_map/ppermute | solution.py:948
  311.9 13.0 %collective-permute-start.36 = (bf16[96,896]{1,0:T(8,128)(2,1)}, bf16[96,896]{1,0:T(8,128)(2,1)}, u32[]{:S(2)}, u32[]{:S(2)}) collective-permute-start(bf16[96,896]{1,0:T(8,128)(2,1)} %get-tuple-element.429), channel_id=1, source_target_pairs={{0,4},{4,0},{8,12},{12,8},{16,20},{20,16},{24,28},{28,24},{1,5},{5... | collective-permute-start | bytes 516104 | tf_op jit(solution)/shard_map/ppermute | solution.py:948
  313.5 28.4 %collective-permute-start.32 = (bf16[192,2304]{1,0:T(8,128)(2,1)S(1)}, bf16[192,2304]{1,0:T(8,128)(2,1)S(1)}, u32[]{:S(2)}, u32[]{:S(2)}) collective-permute-start(bf16[192,2304]{1,0:T(8,128)(2,1)S(1)} %add_convert_fusion.7), channel_id=1, source_target_pairs={{0,2},{1,3},{2,0},{3,1},{4,6},{5,7},{6,4},{7,5},{8,10},{9,11},{10,... | collective-permute-start | bytes 2654216 | tf_op jit(solution)/shard_map/ppermute | solution.py:948
  321.4 20.6 %collective-permute-start.41 = (bf16[48,3072]{1,0:T(8,128)(2,1)S(1)}, bf16[48,3072]{1,0:T(8,128)(2,1)S(1)}, u32[]{:S(2)}, u32[]{:S(2)}) collective-permute-start(bf16[48,3072]{1,0:T(8,128)(2,1)S(1)} %maximum_select_fusion.5), channel_id=1, source_target_pairs={{0,8},{4,12},{8,0},{12,4},{16,24},{20,28},{24,16},{28,20},{1,9},{5... | collective-permute-start | bytes 884744 | tf_op jit(solution)/shard_map/ppermute | solution.py:948
  323.8 25.0 %collective-permute-start.40 = (bf16[96,768]{1,0:T(8,128)(2,1)}, bf16[96,768]{1,0:T(8,128)(2,1)}, u32[]{:S(2)}, u32[]{:S(2)}) collective-permute-start(bf16[96,768]{1,0:T(8,128)(2,1)} %add_convert_fusion.17), channel_id=1, source_target_pairs={{0,16},{4,20},{8,24},{12,28},{16,0},{20,4},{24,8},{28,12},{1,17},{... | collective-permute-start | bytes 442376 | tf_op jit(solution)/shard_map/ppermute | solution.py:948
  342.1 28.7 %collective-permute-start.44 = (bf16[96,3072]{1,0:T(8,128)(2,1)S(1)}, bf16[96,3072]{1,0:T(8,128)(2,1)}, u32[]{:S(2)}, u32[]{:S(2)}) collective-permute-start(bf16[96,3072]{1,0:T(8,128)(2,1)S(1)} %maximum_select_fusion.2), channel_id=1, source_target_pairs={{0,4},{4,0},{8,12},{12,8},{16,20},{20,16},{24,28},{28,24},{1,5},{5... | collective-permute-start | bytes 1769480 | tf_op jit(solution)/shard_map/ppermute | solution.py:948
  344.5 38.6 %all-to-all-start.4 = ((bf16[8,24,2304]{2,1,0:T(8,128)(2,1)}), bf16[8,24,2304]{2,1,0:T(8,128)(2,1)S(1)}, u32[]{:S(2)}, u32[]{:S(2)}) async-start(bf16[8,24,2304]{2,1,0:T(8,128)(2,1)} %bitcast.10), calls=%async_computation.4 | async-start | bytes 1769472 | tf_op jit(solution)/shard_map/all_to_all | solution.py:982
  350.0 20.8 %collective-permute-start.43 = (bf16[192,768]{1,0:T(8,128)(2,1)S(1)}, bf16[192,768]{1,0:T(8,128)(2,1)S(1)}, u32[]{:S(2)}, u32[]{:S(2)}) collective-permute-start(bf16[192,768]{1,0:T(8,128)(2,1)S(1)} %maximum_select_fusion.6), channel_id=1, source_target_pairs={{0,8},{4,12},{8,0},{12,4},{16,24},{20,28},{24,16},{28,20},{1,9},{5... | collective-permute-start | bytes 884744 | tf_op jit(solution)/shard_map/ppermute | solution.py:948
  352.1 18.7 %collective-permute-start.39 = (bf16[48,896]{1,0:T(8,128)(2,1)S(1)}, bf16[48,896]{1,0:T(8,128)(2,1)S(1)}, u32[]{:S(2)}, u32[]{:S(2)}) collective-permute-start(bf16[48,896]{1,0:T(8,128)(2,1)S(1)} %copy-done.29), channel_id=1, source_target_pairs={{0,8},{4,12},{8,0},{12,4},{16,24},{20,28},{24,16},{28,20},{1,9},{5... | collective-permute-start | bytes 258056 | tf_op jit(solution)/shard_map/ppermute | solution.py:948
  384.2 48.2 %all-to-all-start.5 = ((bf16[8,24,2304]{2,1,0:T(8,128)(2,1)}), bf16[8,24,2304]{2,1,0:T(8,128)(2,1)S(1)}, u32[]{:S(2)}, u32[]{:S(2)}) async-start(bf16[8,24,2304]{2,1,0:T(8,128)(2,1)} %broadcast_in_dim.26), calls=%async_computation.5 | async-start | bytes 1769472 | tf_op jit(solution)/shard_map/all_to_all | solution.py:992
  390.8 22.3 %collective-permute-start.46 = (bf16[24,896]{1,0:T(8,128)(2,1)S(1)}, bf16[24,896]{1,0:T(8,128)(2,1)S(1)}, u32[]{:S(2)}, u32[]{:S(2)}) collective-permute-start(bf16[24,896]{1,0:T(8,128)(2,1)S(1)} %add_convert_fusion.20), channel_id=1, source_target_pairs={{0,16},{4,20},{8,24},{12,28},{16,0},{20,4},{24,8},{28,12},{1,17},{... | collective-permute-start | bytes 129032 | tf_op jit(solution)/shard_map/ppermute | solution.py:948
  (64 other events, 498.4 us)
